TPU v7x, 32 devices: a whole 2x2x4 slice. The times are simulated.
32 devices in a mesh: rep: 8 (over y, x, core), fsdp: 4 (over z).
Axes of the slice: x: 2, y: 2, z: 4, core: 2. Of those that a mesh axis runs over, the one named last changes fastest.
Arguments:
- tokens: bfloat16 [128, 256, 384], P(('rep', 'fsdp')), may hold values from -6 to 6
- cotangent: bfloat16 [128, 256, 384], P(('rep', 'fsdp')), may hold values from -6 to 6
- cond_table: bfloat16 [1000, 384], replicated, may hold values from -6 to 6
- labels: int32 [128], P(('rep', 'fsdp')), may hold values from 0 to 999
- counts: int32 [32], P(('rep', 'fsdp')), may hold values from 1 to 4, as said below
- mod_weight: float32 [384, 2304], P('fsdp'), may hold values from -0.3125 to 0.3125
- qkv_weight: float32 [384, 1152], P('fsdp'), may hold values from -0.3125 to 0.3125
- out_weight: float32 [384, 384], P('fsdp'), may hold values from -3.5 to 3.5
- up_weight: float32 [384, 1536], P('fsdp'), may hold values from -0.3125 to 0.3125
- down_weight: float32 [1536, 384], P('fsdp'), may hold values from -0.625 to 0.625
- biases: float32 [5376], P('fsdp'), may hold values from -1.8 to 1.8
- mod_mean: float32 [384, 2304], P('fsdp'), may hold values from -32 to 32
- qkv_mean: float32 [384, 1152], P('fsdp'), may hold values from -32 to 32
- out_mean: float32 [384, 384], P('fsdp'), may hold values from -32 to 32
- up_mean: float32 [384, 1536], P('fsdp'), may hold values from -32 to 32
- down_mean: float32 [1536, 384], P('fsdp'), may hold values from -32 to 32
- bias_mean: float32 [5376], P('fsdp'), may hold values from -32 to 32
- mod_square: float32 [384, 2304], P('fsdp'), may hold values from 0 to 410
- qkv_square: float32 [384, 1152], P('fsdp'), may hold values from 0 to 410
- out_square: float32 [384, 384], P('fsdp'), may hold values from 0 to 410
- up_square: float32 [384, 1536], P('fsdp'), may hold values from 0 to 410
- down_square: float32 [1536, 384], P('fsdp'), may hold values from 0 to 410
- bias_square: float32 [5376], P('fsdp'), may hold values from 0 to 410
Outputs:
- block_out: bfloat16 [128, 256, 384], P(('rep', 'fsdp'))
- token_grad: bfloat16 [128, 256, 384], P(('rep', 'fsdp'))
- table_grad: float32 [1000, 384], P('fsdp')
- mod_grad: float32 [384, 2304], P('fsdp')
- qkv_grad: float32 [384, 1152], P('fsdp')
- out_grad: float32 [384, 384], P('fsdp')
- up_grad: float32 [384, 1536], P('fsdp')
- down_grad: float32 [1536, 384], P('fsdp')
- bias_grad: float32 [5376], P('fsdp')
- mod_next: float32 [384, 2304], P('fsdp')
- qkv_next: float32 [384, 1152], P('fsdp')
- out_next: float32 [384, 384], P('fsdp')
- up_next: float32 [384, 1536], P('fsdp')
- down_next: float32 [1536, 384], P('fsdp')
- bias_next: float32 [5376], P('fsdp')
- mean_mod: float32 [384, 2304], P('fsdp')
- mean_qkv: float32 [384, 1152], P('fsdp')
- mean_out: float32 [384, 384], P('fsdp')
- mean_up: float32 [384, 1536], P('fsdp')
- mean_down: float32 [1536, 384], P('fsdp')
- mean_bias: float32 [5376], P('fsdp')
- square_mod: float32 [384, 2304], P('fsdp')
- square_qkv: float32 [384, 1152], P('fsdp')
- square_out: float32 [384, 384], P('fsdp')
- square_up: float32 [384, 1536], P('fsdp')
- square_down: float32 [1536, 384], P('fsdp')
- square_bias: float32 [5376], P('fsdp')
Inputs may be any that keep to these rules, and one draw needn't show every extreme that they name: `counts`: live latents of each device; some device holds exactly 4.
All inputs are finite; a program needn't handle non-finite values.
Results may differ from a plain program's by a relative error of at most 0.03.
Values may be sent and summed in bfloat16 or wider, within the bound.
No kernel may reach another device: no remote copies, remote signals or barrier semaphores. Data moves between devices by JAX's collectives and lax.ppermute only.
A program may use at most 192 MiB of HBM per device.

v0:
```python
import jax
import jax.numpy as jnp
from jax import lax
from jax.sharding import PartitionSpec as P

HEADS = 6
HD = 64
STEP = 5


norm_eps = 1e-06
beta_one = 0.9
beta_two = 0.999
adam_eps = 1e-08
learn_rate = 0.01
weight_decay = 0.1
gelu_coef = 0.7978845608
cubic_coef = 0.044715


def batched(pattern, left_op, right_op):
    return jnp.einsum(pattern, left_op, right_op, preferred_element_type=jnp.float32)


def layer_norm(values):
    centre = values - jnp.mean(values, axis=-1, keepdims=True)
    inverse = lax.rsqrt(jnp.mean(centre * centre, axis=-1, keepdims=True) + norm_eps)
    return (centre * inverse, inverse)


def norm_back(normed, inverse, upstream):
    return inverse * (
        upstream
        - jnp.mean(upstream, axis=-1, keepdims=True)
        - normed * jnp.mean(upstream * normed, axis=-1, keepdims=True)
    )


def gelu_value(preact):
    return (
        0.5
        * preact
        * (1.0 + jnp.tanh(gelu_coef * (preact + cubic_coef * preact * preact * preact)))
    )


def gelu_slope(preact):
    tanh_value = jnp.tanh(gelu_coef * (preact + cubic_coef * preact * preact * preact))
    return 0.5 * (1.0 + tanh_value) + 0.5 * preact * (1.0 - tanh_value * tanh_value) * gelu_coef * (
        1.0 + 3.0 * cubic_coef * preact * preact
    )


def split_bias(bias_all, features):
    return (
        bias_all[: 6 * features],
        bias_all[6 * features : 8 * features],
        bias_all[8 * features : 9 * features],
        bias_all[9 * features : 13 * features],
        bias_all[13 * features :],
    )


def forward_one(tokens, cond_row, weights):
    mod_w, qkv_w, out_w, up_w, down_w, bias_all = weights
    length, features = tokens.shape
    mod_bias, qv_bias, out_bias, up_bias, down_bias = split_bias(
        bias_all.astype(jnp.float32), features
    )
    activation = jax.nn.silu(cond_row.astype(jnp.float32)).astype(jnp.bfloat16)
    modulation = (
        jnp.dot(activation[None, :], mod_w, preferred_element_type=jnp.float32)[0] + mod_bias
    )
    shift_one, scale_one, gate_one, shift_two, scale_two, gate_two = jnp.split(modulation, 6)
    inputs = tokens.astype(jnp.float32)
    normed_one, inv_one = layer_norm(inputs)
    h_one = (normed_one * (1.0 + scale_one) + shift_one).astype(jnp.bfloat16)
    qkv_bias = jnp.concatenate(
        [qv_bias[:features], jnp.zeros((features,), jnp.float32), qv_bias[features:]]
    )
    qkv_rows = (jnp.dot(h_one, qkv_w, preferred_element_type=jnp.float32) + qkv_bias).astype(
        jnp.bfloat16
    )
    queries = qkv_rows[:, :features].reshape(length, HEADS, HD)
    keys_h = qkv_rows[:, features : 2 * features].reshape(length, HEADS, HD)
    values_h = qkv_rows[:, 2 * features :].reshape(length, HEADS, HD)
    scores = batched("qhd,khd->hqk", queries, keys_h) * HD ** (-0.5)
    exponent = jnp.exp(scores)
    row_total = jnp.sum(exponent, axis=-1, keepdims=True)
    log_total = jnp.log(row_total[:, :, 0])
    probabilities = (exponent / row_total).astype(jnp.bfloat16)
    attn_out = (
        batched("hqk,khd->qhd", probabilities, values_h)
        .reshape(length, features)
        .astype(jnp.bfloat16)
    )
    attn_proj = jnp.dot(attn_out, out_w, preferred_element_type=jnp.float32) + out_bias
    residual = inputs + gate_one * attn_proj
    normed_two, inv_two = layer_norm(residual)
    h_two = (normed_two * (1.0 + scale_two) + shift_two).astype(jnp.bfloat16)
    preact = jnp.dot(h_two, up_w, preferred_element_type=jnp.float32) + up_bias
    hidden = gelu_value(preact).astype(jnp.bfloat16)
    mlp_out = jnp.dot(hidden, down_w, preferred_element_type=jnp.float32) + down_bias
    block_value = (residual + gate_two * mlp_out).astype(jnp.bfloat16)
    kept = (
        activation,
        modulation,
        normed_one,
        inv_one,
        h_one,
        qkv_rows,
        log_total,
        attn_out,
        attn_proj,
        normed_two,
        inv_two,
        h_two,
        preact,
        hidden,
        mlp_out,
    )
    return (block_value, kept)


def backward_one(cotangent, cond_row, weights, kept):
    mod_w, qkv_w, out_w, up_w, down_w, bias_all = weights
    (
        activation,
        modulation,
        normed_one,
        inv_one,
        h_one,
        qkv_rows,
        log_total,
        attn_out,
        attn_proj,
        normed_two,
        inv_two,
        h_two,
        preact,
        hidden,
        mlp_out,
    ) = kept
    length, features = cotangent.shape
    shift_one, scale_one, gate_one, shift_two, scale_two, gate_two = jnp.split(modulation, 6)
    upstream = cotangent.astype(jnp.float32)
    d_gate_two = jnp.sum(upstream * mlp_out, axis=0)
    e_mlp = upstream * gate_two
    d_mlp = e_mlp.astype(jnp.bfloat16)
    grad_down = jnp.dot(hidden.T, d_mlp, preferred_element_type=jnp.float32)
    d_hidden = jnp.dot(d_mlp, down_w.T, preferred_element_type=jnp.float32)
    e_pre = d_hidden * gelu_slope(preact)
    d_pre = e_pre.astype(jnp.bfloat16)
    grad_up = jnp.dot(h_two.T, d_pre, preferred_element_type=jnp.float32)
    d_h_two = jnp.dot(d_pre, up_w.T, preferred_element_type=jnp.float32)
    d_scale_two = jnp.sum(d_h_two * normed_two, axis=0)
    d_shift_two = jnp.sum(d_h_two, axis=0)
    d_mid = upstream + norm_back(normed_two, inv_two, d_h_two * (1.0 + scale_two))
    d_gate_one = jnp.sum(d_mid * attn_proj, axis=0)
    e_proj = d_mid * gate_one
    d_proj = e_proj.astype(jnp.bfloat16)
    grad_out = jnp.dot(attn_out.T, d_proj, preferred_element_type=jnp.float32)
    d_attn = jnp.dot(d_proj, out_w.T, preferred_element_type=jnp.float32).astype(jnp.bfloat16)
    queries = qkv_rows[:, :features].reshape(length, HEADS, HD)
    keys_h = qkv_rows[:, features : 2 * features].reshape(length, HEADS, HD)
    values_h = qkv_rows[:, 2 * features :].reshape(length, HEADS, HD)
    d_heads = d_attn.reshape(length, HEADS, HD)
    scores = batched("qhd,khd->hqk", queries, keys_h) * HD ** (-0.5)
    prob_again = jnp.exp(scores - log_total[:, :, None])
    d_values = batched("hqk,qhd->khd", prob_again.astype(jnp.bfloat16), d_heads).reshape(
        length, features
    )
    d_prob = batched("qhd,khd->hqk", d_heads, values_h)
    row_delta = jnp.sum(
        (d_attn.astype(jnp.float32) * attn_out.astype(jnp.float32)).reshape(length, HEADS, HD),
        axis=-1,
    ).T
    d_scores = (prob_again * (d_prob - row_delta[:, :, None]) * HD ** (-0.5)).astype(jnp.bfloat16)
    d_queries = batched("hqk,khd->qhd", d_scores, keys_h).reshape(length, features)
    d_keys = batched("hqk,qhd->khd", d_scores, queries).reshape(length, features)
    d_qkv = jnp.concatenate([d_queries, d_keys, d_values], axis=1).astype(jnp.bfloat16)
    grad_qkv = jnp.dot(h_one.T, d_qkv, preferred_element_type=jnp.float32)
    d_h_one = jnp.dot(d_qkv, qkv_w.T, preferred_element_type=jnp.float32)
    d_scale_one = jnp.sum(d_h_one * normed_one, axis=0)
    d_shift_one = jnp.sum(d_h_one, axis=0)
    token_grad = (d_mid + norm_back(normed_one, inv_one, d_h_one * (1.0 + scale_one))).astype(
        jnp.bfloat16
    )
    e_mod = jnp.concatenate(
        [d_shift_one, d_scale_one, d_gate_one, d_shift_two, d_scale_two, d_gate_two]
    )
    d_mod = e_mod.astype(jnp.bfloat16)
    grad_mod = activation.astype(jnp.float32)[:, None] * d_mod.astype(jnp.float32)[None, :]
    grad_bias = jnp.concatenate(
        [
            e_mod,
            jnp.sum(d_queries, axis=0),
            jnp.sum(d_values, axis=0),
            jnp.sum(e_proj, axis=0),
            jnp.sum(e_pre, axis=0),
            jnp.sum(e_mlp, axis=0),
        ]
    )
    d_act = jnp.dot(d_mod[None, :], mod_w.T, preferred_element_type=jnp.float32)[0]
    cond_full = cond_row.astype(jnp.float32)
    sigmoid_c = jax.nn.sigmoid(cond_full)
    d_cond = d_act * sigmoid_c * (1.0 + cond_full * (1.0 - sigmoid_c))
    return (
        token_grad,
        (grad_mod, grad_qkv, grad_out, grad_up, grad_down, grad_bias),
        d_cond,
        d_mod,
    )


def empty_stored(capacity, length, features):
    layout = [
        ((features,), jnp.bfloat16),
        ((6 * features,), jnp.float32),
        ((length, features), jnp.float32),
        ((length, 1), jnp.float32),
        ((length, features), jnp.bfloat16),
        ((length, 3 * features), jnp.bfloat16),
        ((HEADS, length), jnp.float32),
        ((length, features), jnp.bfloat16),
        ((length, features), jnp.float32),
        ((length, features), jnp.float32),
        ((length, 1), jnp.float32),
        ((length, features), jnp.bfloat16),
        ((length, 4 * features), jnp.float32),
        ((length, 4 * features), jnp.bfloat16),
        ((length, features), jnp.float32),
    ]
    return tuple((jnp.zeros((capacity,) + extent, dtype_of) for extent, dtype_of in layout))


def adamw_update(weight, gradient, mean, square):
    mean_new = beta_one * mean + (1.0 - beta_one) * gradient
    square_new = beta_two * square + (1.0 - beta_two) * gradient * gradient
    mean_hat = mean_new / (1.0 - beta_one**STEP)
    square_hat = square_new / (1.0 - beta_two**STEP)
    weight_new = weight - learn_rate * (
        mean_hat / (jnp.sqrt(square_hat) + adam_eps) + weight_decay * weight
    )
    return (weight_new, mean_new, square_new)


def body(
    tokens,
    cotangent,
    cond_table,
    labels,
    counts,
    mod_weight,
    qkv_weight,
    out_weight,
    up_weight,
    down_weight,
    biases,
    mod_mean,
    qkv_mean,
    out_mean,
    up_mean,
    down_mean,
    bias_mean,
    mod_square,
    qkv_square,
    out_square,
    up_square,
    down_square,
    bias_square,
):
    capacity, length, features = tokens.shape
    classes_all = cond_table.shape[0]
    live_count = counts[0]
    mod_half = mod_weight.astype(jnp.bfloat16)
    qkv_half = qkv_weight.astype(jnp.bfloat16)
    out_half = out_weight.astype(jnp.bfloat16)
    up_half = up_weight.astype(jnp.bfloat16)
    down_half = down_weight.astype(jnp.bfloat16)
    bias_half = biases.astype(jnp.bfloat16)
    gathered = (
        lax.all_gather(mod_half, "fsdp", axis=0, tiled=True),
        lax.all_gather(qkv_half, "fsdp", axis=0, tiled=True),
        lax.all_gather(out_half, "fsdp", axis=0, tiled=True),
        lax.all_gather(up_half, "fsdp", axis=0, tiled=True),
        lax.all_gather(down_half, "fsdp", axis=0, tiled=True),
        lax.all_gather(bias_half, "fsdp", axis=0, tiled=True),
    )

    def forward_step(position, running):
        outputs, stored = running
        label_id = labels[position]
        cond_row = lax.dynamic_index_in_dim(cond_table, label_id, 0, keepdims=False)
        block_value, kept = forward_one(tokens[position], cond_row, gathered)
        outputs = outputs.at[position].set(block_value)
        stored = tuple((buffer.at[position].set(portion) for buffer, portion in zip(stored, kept)))
        return (outputs, stored)

    block_out, stored = lax.fori_loop(
        0,
        live_count,
        forward_step,
        (jnp.zeros_like(tokens), empty_stored(capacity, length, features)),
    )
    back_weights = (
        lax.all_gather(mod_half, "fsdp", axis=0, tiled=True),
        lax.all_gather(qkv_half, "fsdp", axis=0, tiled=True),
        lax.all_gather(out_half, "fsdp", axis=0, tiled=True),
        lax.all_gather(up_half, "fsdp", axis=0, tiled=True),
        lax.all_gather(down_half, "fsdp", axis=0, tiled=True),
        lax.all_gather(bias_half, "fsdp", axis=0, tiled=True),
    )
    class_ids = lax.iota(jnp.int32, classes_all)
    core_zero = tuple((jnp.zeros(full.shape, jnp.float32) for full in back_weights[1:]))
    side_zero = (
        jnp.zeros(back_weights[0].shape, jnp.float32),
        jnp.zeros((classes_all, features), jnp.float32),
    )
    mod_rows_zero = jnp.zeros((capacity, 6 * features), jnp.bfloat16)
    cond_rows_zero = jnp.zeros((capacity, features), jnp.float32)

    def backward_step(position, running):
        token_grads, core_in, side_in, mod_rows_buf, cond_rows_buf = running
        label_id = labels[position]
        cond_row = lax.dynamic_index_in_dim(cond_table, label_id, 0, keepdims=False)
        kept = tuple((buffer[position] for buffer in stored))
        d_tokens, gradients, d_cond, d_mod = backward_one(
            cotangent[position], cond_row, back_weights, kept
        )
        token_grads = token_grads.at[position].set(d_tokens)
        core_out = tuple((total + term for total, term in zip(core_in, gradients[1:])))
        table_term = jnp.where((class_ids == label_id)[:, None], d_cond[None, :], 0.0)
        side_out = (side_in[0] + gradients[0], side_in[1] + table_term)
        mod_rows_buf = mod_rows_buf.at[position].set(d_mod)
        cond_rows_buf = cond_rows_buf.at[position].set(d_cond)
        return (token_grads, core_out, side_out, mod_rows_buf, cond_rows_buf)

    token_grad, core_sums, side_sums, mod_rows, cond_rows = lax.fori_loop(
        0,
        live_count,
        backward_step,
        (jnp.zeros_like(tokens), core_zero, side_zero, mod_rows_zero, cond_rows_zero),
    )
    sum_qkv, sum_out, sum_up, sum_down, sum_bias = core_sums
    mod_share, table_share = (
        lax.psum_scatter(side_sums[0], "fsdp", scatter_dimension=0, tiled=True),
        lax.psum_scatter(side_sums[1], "fsdp", scatter_dimension=0, tiled=True),
    )
    shares = (
        lax.psum_scatter(sum_qkv, "fsdp", scatter_dimension=0, tiled=True),
        lax.psum_scatter(sum_out, "fsdp", scatter_dimension=0, tiled=True),
        lax.psum_scatter(sum_up, "fsdp", scatter_dimension=0, tiled=True),
        lax.psum_scatter(sum_down, "fsdp", scatter_dimension=0, tiled=True),
        lax.psum_scatter(sum_bias, "fsdp", scatter_dimension=0, tiled=True),
    )
    summed_all = lax.psum(
        (mod_share, shares[0], shares[1], shares[2], shares[3], shares[4], table_share), "rep"
    )
    mod_grad, qkv_grad, out_grad, up_grad, down_grad, bias_grad, table_grad = summed_all
    mod_next, mean_mod, square_mod = adamw_update(mod_weight, mod_grad, mod_mean, mod_square)
    qkv_next, mean_qkv, square_qkv = adamw_update(qkv_weight, qkv_grad, qkv_mean, qkv_square)
    out_next, mean_out, square_out = adamw_update(out_weight, out_grad, out_mean, out_square)
    up_next, mean_up, square_up = adamw_update(up_weight, up_grad, up_mean, up_square)
    down_next, mean_down, square_down = adamw_update(down_weight, down_grad, down_mean, down_square)
    bias_next, mean_bias, square_bias = adamw_update(biases, bias_grad, bias_mean, bias_square)
    return (
        block_out,
        token_grad,
        table_grad,
        mod_grad,
        qkv_grad,
        out_grad,
        up_grad,
        down_grad,
        bias_grad,
        mod_next,
        qkv_next,
        out_next,
        up_next,
        down_next,
        bias_next,
        mean_mod,
        mean_qkv,
        mean_out,
        mean_up,
        mean_down,
        mean_bias,
        square_mod,
        square_qkv,
        square_out,
        square_up,
        square_down,
        square_bias,
    )


def solution(mesh):
    placed = (
        P(("rep", "fsdp"), None, None),
        P(("rep", "fsdp"), None, None),
        P(),
        P(("rep", "fsdp")),
        P(("rep", "fsdp")),
        P("fsdp", None),
        P("fsdp", None),
        P("fsdp", None),
        P("fsdp", None),
        P("fsdp", None),
        P("fsdp"),
        P("fsdp", None),
        P("fsdp", None),
        P("fsdp", None),
        P("fsdp", None),
        P("fsdp", None),
        P("fsdp"),
        P("fsdp", None),
        P("fsdp", None),
        P("fsdp", None),
        P("fsdp", None),
        P("fsdp", None),
        P("fsdp"),
    )
    return jax.shard_map(
        body,
        mesh=mesh,
        in_specs=placed,
        out_specs=(
            P(("rep", "fsdp"), None, None),
            P(("rep", "fsdp"), None, None),
            P("fsdp", None),
            P("fsdp", None),
            P("fsdp", None),
            P("fsdp", None),
            P("fsdp", None),
            P("fsdp", None),
            P("fsdp"),
            P("fsdp", None),
            P("fsdp", None),
            P("fsdp", None),
            P("fsdp", None),
            P("fsdp", None),
            P("fsdp"),
            P("fsdp", None),
            P("fsdp", None),
            P("fsdp", None),
            P("fsdp", None),
            P("fsdp", None),
            P("fsdp"),
            P("fsdp", None),
            P("fsdp", None),
            P("fsdp", None),
            P("fsdp", None),
            P("fsdp", None),
            P("fsdp"),
        ),
        check_vma=False,
    )
```

profile of v0, /device:TPU:0, one launch (start us, length us, event | category | flops | bytes accessed | tf_op | source)
XLA Modules:
  0.0 890.7 jit_solution(18401510512041878953)
XLA Ops:
  12.7 21.0 %all-reduce = bf16[5376]{0:T(1024)(128)(2,1)S(1)} all-reduce(bf16[5376]{0:T(1024)(128)(2,1)S(1)} %dynamic-update-slice.54), channel_id=1, replica_groups=mesh['rep'=8,'fsdp'=4] {'fsdp'}, use_global_device_ids=true, to_apply=%add | all-reduce | flops 5376 | bytes 21504
  33.7 16.6 %all_gather.26 = bf16[384,384]{1,0:T(8,128)(2,1)} all-gather(bf16[96,384]{1,0:T(8,128)(2,1)S(1)} %convert_element_type.166), channel_id=1, replica_groups=mesh['rep'=8,'fsdp'=4] {'fsdp'}, dimensions={0}, use_global_device_ids=true | all-gather | bytes 368640 | tf_op jit(solution)/shard_map/all_gather | solution.py:285
  50.3 23.4 %all_gather.25 = bf16[384,1152]{1,0:T(8,128)(2,1)} all-gather(bf16[96,1152]{1,0:T(8,128)(2,1)S(1)} %convert_element_type.165), channel_id=1, replica_groups=mesh['rep'=8,'fsdp'=4] {'fsdp'}, dimensions={0}, use_global_device_ids=true | all-gather | bytes 1105920 | tf_op jit(solution)/shard_map/all_gather | solution.py:284
  73.7 10.0 %all-gather.8.cloned.1.call-done = bf16[1536,384]{1,0:T(8,128)(2,1)} async-done(((bf16[384,384]{1,0:T(8,128)(2,1)}), bf16[1536,384]{1,0:T(8,128)(2,1)}) %all-gather.8.cloned.1.call-update) | async-done | bytes 1179664 | tf_op jit(solution)/shard_map/all_gather | solution.py:287
  83.7 42.5 %all-gather.4.cloned.1.call-done = bf16[384,2304]{1,0:T(8,128)(2,1)} async-done(((bf16[96,2304]{1,0:T(8,128)(2,1)}), bf16[384,2304]{1,0:T(8,128)(2,1)}) %all-gather.4.cloned.1.call-update) | async-done | bytes 1769488 | tf_op jit(solution)/shard_map/all_gather | solution.py:283
  138.5 3.4 broadcast_in_dim.99
  145.4 47.9 %while.87 = (s32[]{:T(128)}, bf16[4,256,384]{2,1,0:T(8,128)(2,1)}, bf16[4,384]{1,0:T(4,128)(2,1)}, f32[4,2304]{1,0:T(4,128)}, f32[4,256,384]{2,1,0:T(8,128)}, /*...) while((s32[]{:T(128)}, bf16[4,256,384]{2,1,0:T(8,128)(2,1)}, ...), condition=%wide.region_8.9_spmd, body=%wide.region_0.8_spmd.sunk | while | flops 1024445056 | bytes 49656664 | solution.py:300
  153.3 3.1 fusion.240
  160.5 4.3 fusion.244
  164.8 3.8 fusion.245
  176.0 3.0 fusion.246
  181.7 2.9 fusion.247
  186.5 2.8 fusion.249
  189.3 3.3 fusion.250
  203.7 56.1 %while.88 = (s32[]{:T(128)}, bf16[4,256,384]{2,1,0:T(8,128)(2,1)}, f32[384,1152]{1,0:T(8,128)}, f32[384,384]{1,0:T(8,128)}, f32[384,1536]{1,0:T(8,128)}, /*index...) while((s32[]{:T(128)}, bf16[4,256,384]{2,1,0:T(8,128)(2,1)}, ...), condition=%wide.region_27.28_spmd.clone, body=%wide.region_9.27_spmd.clone.sunk | while | flops 2089441792 | bytes 111662480 | solution.py:339
  205.9 3.7 fusion.274
  209.7 2.9 fusion.275
  213.8 2.1 fusion.276
  232.5 2.4 fusion.281
  238.5 3.7 convolution_add_fusion.14
  242.3 4.0 convolution_add_fusion.15
  248.0 4.2 multiply_add_fusion.16
  263.1 122.6 %fusion.2 = f32[256,384]{1,0:T(8,128)S(1)} fusion(f32[1000,384]{1,0:T(8,128)S(1)} %copy-done.9), kind=kCustom, calls=%all-reduce-scatter | all-reduce-scatter fusion | flops 393217 | bytes 1929728
  389.9 197.1 %reduce-scatter.12.cloned.1.call-done = f32[96,384]{1,0:T(8,128)} async-done(((f32[384,384]{1,0:T(8,128)}), f32[96,384]{1,0:T(8,128)}) %reduce-scatter.12.cloned.1.call-update) | async-done | bytes 147472 | tf_op jit(solution)/shard_map/reduce_scatter | solution.py:352
  587.0 41.6 %reduce-scatter.10.cloned.1.call-done = f32[96,1152]{1,0:T(8,128)} async-done(((f32[384,1152]{1,0:T(8,128)}), f32[96,1152]{1,0:T(8,128)}) %reduce-scatter.10.cloned.1.call-update) | async-done | bytes 442384 | tf_op jit(solution)/shard_map/reduce_scatter | solution.py:351
  628.6 48.9 %reduce-scatter.14.cloned.1.call-done = f32[96,1536]{1,0:T(8,128)} async-done(((f32[384,1536]{1,0:T(8,128)}), f32[96,1536]{1,0:T(8,128)}) %reduce-scatter.14.cloned.1.call-update) | async-done | bytes 589840 | tf_op jit(solution)/shard_map/reduce_scatter | solution.py:353
  677.5 49.4 %reduce-scatter.16.cloned.1.call-done = f32[384,384]{1,0:T(8,128)} async-done(((f32[1536,384]{1,0:T(8,128)}), f32[384,384]{1,0:T(8,128)}) %reduce-scatter.16.cloned.1.call-update) | async-done | bytes 589840 | tf_op jit(solution)/shard_map/reduce_scatter | solution.py:354
  726.9 68.2 %reduce-scatter.8.cloned.1.call-done = f32[96,2304]{1,0:T(8,128)} async-done(((f32[384,2304]{1,0:T(8,128)}), f32[96,2304]{1,0:T(8,128)}) %reduce-scatter.8.cloned.1.call-update) | async-done | bytes 884752 | tf_op jit(solution)/shard_map/reduce_scatter | solution.py:347
  796.0 17.9 %all-reduce.2 = f32[5376]{0:T(1024)S(1)} all-reduce(f32[5376]{0:T(1024)S(1)} %copy-done.35), channel_id=8, replica_groups=mesh['rep'=8,'fsdp'=4] {'fsdp'}, use_global_device_ids=true, to_apply=%region_40.41.clone | all-reduce | flops 5376 | bytes 43008
  813.9 12.5 %psum.55 = f32[1344]{0:T(1024)S(1)} all-reduce(f32[1344]{0:T(1024)S(1)} %dynamic-slice.184), channel_id=1, replica_groups=mesh['rep'=8,'fsdp'=4] {'rep'}, use_global_device_ids=true, to_apply=%region_41.42 | all-reduce | flops 1344 | bytes 10752 | tf_op jit(solution)/shard_map/psum | solution.py:357
  827.2 42.8 %all-reduce.7.cloned.1.call-done = (f32[250,384]{1,0:T(8,128)}, f32[96,2304]{1,0:T(8,128)}, f32[96,1152]{1,0:T(8,128)}, f32[96,384]{1,0:T(8,128)}, f32[96,1536]{1,0:T(8,128)}, /*index=5*/f32[384,384]{1,0:T(8,128)}) async-done(((f32[250,384]{1,0:T(8,128)}, f32[96,2304]{1,0:T(8,128)}, f32[96,1152]{1,0:T(8,128)}, f32[96,384]{1,0:T(8,128)}, f32[96,1536]{1,0:T(8,128)}, /*index=5*/f32[384,384]{1,0:T(8,128)}), ...) | async-done | bytes 3038224 | tf_op jit(solution)/shard_map/psum | solution.py:357
  870.0 3.2 multiply_subtract_fusion
  (323 shorter events, 99.6 us)
Async XLA Ops:
  7.2 66.5 %all-gather.6.cloned.1.call-start = ((), (), s32[]{:S(2)}) async-start(), calls=%async_computation.6 | async-start | bytes 1474560 | tf_op jit(solution)/shard_map/all_gather | solution.py:286
  9.2 74.5 %all-gather.8.cloned.1.call-start = ((), (), s32[]{:S(2)}) async-start(), calls=%async_computation.7 | async-start | bytes 1474560 | tf_op jit(solution)/shard_map/all_gather | solution.py:287
  10.0 116.2 %all-gather.4.cloned.1.call-start = ((), (), s32[]{:S(2)}) async-start(), calls=%async_computation.5 | async-start | bytes 2211840 | tf_op jit(solution)/shard_map/all_gather | solution.py:283
  10.9 576.1 %reduce-scatter.12.cloned.1.call-start = ((), (), s32[]{:S(2)}) async-start(), calls=%async_computation.10 | async-start | bytes 737280 | tf_op jit(solution)/shard_map/reduce_scatter | solution.py:352
  146.0 10.4 %copy-start.28 = (bf16[5376]{0:T(1024)(128)(2,1)}, bf16[5376]{0:T(1024)(128)(2,1)S(1)}, u32[]{:S(2)}) copy-start(bf16[5376]{0:T(1024)(128)(2,1)S(1)} %get-tuple-element.1707) | copy-start | bytes 32260 | tf_op jit(solution)/shard_map/while
  159.5 5.2 copy-start.53
  159.7 5.0 copy-start.55
  164.8 4.5 copy-start.73
  176.0 8.6 copy-start.41
  176.0 10.6 %copy-start.54 = (f32[256]{0:T(256)S(1)}, f32[256]{0:T(256)}, u32[]{:S(2)}) copy-start(f32[256]{0:T(256)} %copy-done.53) | copy-start | bytes 3076 | tf_op jit(solution)/shard_map/while
  181.7 7.6 copy-start.2
  209.7 6.3 copy-start.17
  230.5 4.5 copy-start.5
  236.6 5.6 copy-start.6
  242.3 4.4 copy-start.33
  242.3 5.7 copy-start.58
  246.7 5.5 copy-start.34
  252.2 5.3 copy-start.7
  259.8 368.8 %reduce-scatter.10.cloned.1.call-start = ((), (), s32[]{:S(2)}) async-start(), calls=%async_computation.9 | async-start | bytes 2211840 | tf_op jit(solution)/shard_map/reduce_scatter | solution.py:351
  260.4 417.1 %reduce-scatter.14.cloned.1.call-start = ((), (), s32[]{:S(2)}) async-start(), calls=%async_computation.11 | async-start | bytes 2949120 | tf_op jit(solution)/shard_map/reduce_scatter | solution.py:353
  260.9 466.0 %reduce-scatter.16.cloned.1.call-start = ((), (), s32[]{:S(2)}) async-start(), calls=%async_computation.12 | async-start | bytes 2949120 | tf_op jit(solution)/shard_map/reduce_scatter | solution.py:354
  261.7 533.5 %reduce-scatter.8.cloned.1.call-start = ((), (), s32[]{:S(2)}) async-start(), calls=%async_computation.8 | async-start | bytes 4423680 | tf_op jit(solution)/shard_map/reduce_scatter | solution.py:347
  262.4 607.5 %all-reduce.7.cloned.1.call-start = ((), (), s32[]{:S(2)}) async-start(), calls=%async_computation.13 | async-start | bytes 6094848 | tf_op jit(solution)/shard_map/psum | solution.py:357
  385.8 2.9 collective-permute-start
  389.9 406.1 %copy-start.35 = (f32[5376]{0:T(1024)S(1)}, f32[5376]{0:T(1024)}, u32[]{:S(2)}) copy-start(f32[5376]{0:T(1024)} %get-tuple-element.694) | copy-start | bytes 64516
  795.1 31.3 %copy-start.80 = (f32[1344]{0:T(1024)S(1)}, f32[1344]{0:T(1024)}, u32[]{:S(2)}) copy-start(f32[1344]{0:T(1024)} %param.75) | copy-start | bytes 16132
  795.1 31.4 %copy-start.83 = (f32[1344]{0:T(1024)S(1)}, f32[1344]{0:T(1024)}, u32[]{:S(2)}) copy-start(f32[1344]{0:T(1024)} %param.81) | copy-start | bytes 16132
  795.1 31.4 %copy-start.84 = (f32[1344]{0:T(1024)S(1)}, f32[1344]{0:T(1024)}, u32[]{:S(2)}) copy-start(f32[1344]{0:T(1024)} %param.87) | copy-start | bytes 16132
  795.1 74.8 %copy-start.22 = (f32[96,2304]{1,0:T(8,128)S(1)}, f32[96,2304]{1,0:T(8,128)}, u32[]{:S(2)}) copy-start(f32[96,2304]{1,0:T(8,128)} %param.70) | copy-start | bytes 2654212
  795.2 74.8 %copy-start.36 = (f32[96,2304]{1,0:T(8,128)S(1)}, f32[96,2304]{1,0:T(8,128)}, u32[]{:S(2)}) copy-start(f32[96,2304]{1,0:T(8,128)} %param.76) | copy-start | bytes 2654212
  795.2 74.8 %copy-start.37 = (f32[96,2304]{1,0:T(8,128)S(1)}, f32[96,2304]{1,0:T(8,128)}, u32[]{:S(2)}) copy-start(f32[96,2304]{1,0:T(8,128)} %param.82) | copy-start | bytes 2654212
  826.5 46.7 %copy-start.81 = (f32[1344]{0:T(1024)}, f32[1344]{0:T(1024)S(1)}, u32[]{:S(2)}) copy-start(f32[1344]{0:T(1024)S(1)} %psum.55) | copy-start | bytes 16132
  (64 other events, 159.1 us)
Sparse Core Ops, SparseCore 0:
  10.2 37.8 all-gather.5
  50.2 33.4 all-gather.7
  85.9 40.3 all-gather.3
  259.9 327.0 reduce-scatter.11
  589.2 39.3 reduce-scatter.9
  630.8 46.6 reduce-scatter.13
  679.8 47.0 reduce-scatter.15
  729.2 65.8 reduce-scatter.7
  799.8 70.0 all-reduce.6
where the time goes:
time: 897 us; the launch traced here: 891 us
  waiting for transfers between devices  504 us (56%)
  blocking collectives  214 us (24%)
  local copies, waits for them, and re-layouts  57.9 us (6%)
  other arithmetic  49.2 us (5%)
  matrix products  40.2 us (4%)
  between operations  16.3 us (2%)
    reduce_scatter x1, waiting for transfers between devices, body(): lax.psum_scatter(sum_out, 'fsdp', scatter_dimension=0, tiled=True)  197 us
    unnamed x3, blocking collectives  161 us
    reduce_scatter x1, waiting for transfers between devices, body(): lax.psum_scatter(side_sums[0], 'fsdp', scatter_dimension=0, tiled=True)  68.2 us
    reduce_scatter x1, waiting for transfers between devices, body(): lax.psum_scatter(sum_down, 'fsdp', scatter_dimension=0, tiled=True)  49.4 us
    reduce_scatter x1, waiting for transfers between devices, body(): lax.psum_scatter(sum_up, 'fsdp', scatter_dimension=0, tiled=True)  48.9 us
    psum x1, waiting for transfers between devices, body(): lax.psum((mod_share, shares[0], shares[1], shares[2], shares[3], shares[4...  42.8 us
    all_gather x1, waiting for transfers between devices, body(): lax.all_gather(mod_half, 'fsdp', axis=0, tiled=True)  42.5 us
    reduce_scatter x1, waiting for transfers between devices, body(): lax.psum_scatter(sum_qkv, 'fsdp', scatter_dimension=0, tiled=True)  41.6 us
  transfers between devices with their start and end apart: 10, of which 9 were waited for; matrix products, arithmetic and copies ran while one was open for 14% of the time, Pallas kernels for 0%

commit v1 on v0

v1 whole, which is shorter than its diff:
```python
import functools

import jax
import jax.numpy as jnp
from jax import lax
from jax.experimental import pallas as pl
from jax.experimental.pallas import tpu as pltpu
from jax.sharding import Mesh
from jax.sharding import PartitionSpec as P

HEADS = 6
HD = 64
STEP = 5


norm_eps = 1e-06
beta_one = 0.9
beta_two = 0.999
adam_eps = 1e-08
learn_rate = 0.01
weight_decay = 0.1
gelu_coef = 0.7978845608
cubic_coef = 0.044715
half = jnp.bfloat16
full = jnp.float32


def dot_nn(left, right):
    return lax.dot_general(left, right, (((1,), (0,)), ((), ())), preferred_element_type=full)


def dot_nt(left, right):
    return lax.dot_general(left, right, (((1,), (1,)), ((), ())), preferred_element_type=full)


def dot_tn(left, right):
    return lax.dot_general(left, right, (((0,), (0,)), ((), ())), preferred_element_type=full)


def layer_norm(values):
    centre = values - jnp.mean(values, axis=-1, keepdims=True)
    inverse = lax.rsqrt(jnp.mean(centre * centre, axis=-1, keepdims=True) + norm_eps)
    return (centre * inverse, inverse)


def norm_back(normed, inverse, upstream):
    return inverse * (
        upstream
        - jnp.mean(upstream, axis=-1, keepdims=True)
        - normed * jnp.mean(upstream * normed, axis=-1, keepdims=True)
    )


def head_masks():
    lane = lax.broadcasted_iota(jnp.int32, (1, 2 * HD), 1)
    low = jnp.where(lane < HD, 1.0, 0.0).astype(full)
    return (low, 1.0 - low)


def load_first(info_ref, weight_ref, parts):
    if len(parts) == 1:
        weight_ref[...] = parts[0][...]
        return
    groups = len(parts) // 2
    rows = parts[0].shape[0]
    for flip in range(2):
        for step in range(groups):
            core = info_ref[1] ^ flip
            group = info_ref[3] ^ step
            top = pl.multiple_of((group * 2 + core) * rows, rows)
            weight_ref[pl.ds(top, rows), :] = parts[flip * groups + step][...]


def load_second(info_ref, up_ref, down_ref, parts):
    width = up_ref.shape[2]
    if parts[0].ndim == 2:
        for chunk in range(up_ref.shape[0]):
            up_ref[chunk] = parts[0][:, chunk * width : (chunk + 1) * width]
        down_ref[...] = parts[1][...]
        return
    chips = len(parts) // 2
    groups, _, rows, _ = parts[0].shape
    for flip in range(2):
        for hop in range(chips):
            for step in range(groups):
                core = info_ref[1] ^ flip
                chip = info_ref[2] ^ hop
                group = info_ref[3] ^ step
                source = parts[flip * chips + hop]
                top = pl.multiple_of((group * 2 + core) * rows, rows)
                up_ref[chip, pl.ds(top, rows), :] = source[step, 0]
                top = pl.multiple_of(((group * chips + chip) * 2 + core) * rows, rows)
                down_ref[pl.ds(top, rows), :] = source[step, 1]


def attn_forward(info_ref, tok_ref, mod_ref, bias_ref, *rest):
    *parts, qkv_ref, prob_ref, attn_ref, proj_ref, weight_ref = rest
    features = tok_ref.shape[2]

    @pl.when(pl.program_id(0) == 0)
    def _():
        load_first(info_ref, weight_ref, parts)

    @pl.when(pl.program_id(0) < info_ref[0])
    def _():
        mods = mod_ref[0]
        shift_one = mods[:, :features]
        scale_one = mods[:, features : 2 * features]
        inputs = tok_ref[0].astype(full)
        normed_one, _ = layer_norm(inputs)
        h_one = (normed_one * (1.0 + scale_one) + shift_one).astype(half)
        masks = head_masks()
        qkv_ref[0] = (
            dot_nn(h_one, weight_ref[:, : 3 * features]) + bias_ref[:, : 3 * features]
        ).astype(half)
        width = 2 * HD
        for pair in range(HEADS // 2):
            low = pair * width
            queries = qkv_ref[0, :, low : low + width]
            keys_h = qkv_ref[0, :, features + low : features + low + width]
            values_h = qkv_ref[0, :, 2 * features + low : 2 * features + low + width]
            total = None
            for side in range(2):
                scaled = queries * (masks[side] * HD ** (-0.5)).astype(half)
                exponent = jnp.exp(dot_nt(scaled, keys_h))
                row_total = jnp.sum(exponent, axis=-1, keepdims=True)
                probs = (exponent * (1.0 / row_total)).astype(half)
                prob_ref[0, 2 * pair + side] = probs
                term = dot_nn(probs, values_h * masks[side].astype(half))
                total = term if total is None else total + term
            attn_ref[0, :, low : low + width] = total.astype(half)
        proj_ref[0] = (
            dot_nn(attn_ref[0], weight_ref[:, 3 * features :]) + bias_ref[:, 3 * features :]
        )


def mlp_both(count_parts, info_ref, tok_ref, cot_ref, mod_ref, proj_ref, bias_ref, *rest):
    features = tok_ref.shape[2]
    parts = rest[:count_parts]
    out_ref, dmid_ref, keep_ref, send_ref, note_ref, *rest = rest[count_parts:]
    vec_ref, hidden_ref, slope_ref, acc_up, acc_down, down_t, up_ref, down_ref = rest
    wide = hidden_ref.shape[1]
    slot = pl.program_id(0)
    chunks = wide // features

    @pl.when(slot == 0)
    def _():
        load_second(info_ref, up_ref, down_ref, parts)
        acc_up[...] = jnp.zeros_like(acc_up)
        acc_down[...] = jnp.zeros_like(acc_down)
        vec_ref[...] = jnp.zeros_like(vec_ref)

    @pl.when(slot >= info_ref[0])
    def _():
        out_ref[...] = jnp.zeros_like(out_ref)

    @pl.when(slot < info_ref[0])
    def _():
        mods = mod_ref[0]
        gate_one = mods[:, 2 * features : 3 * features]
        shift_two = mods[:, 3 * features : 4 * features]
        scale_two = mods[:, 4 * features : 5 * features]
        gate_two = mods[:, 5 * features :]
        residual = tok_ref[0].astype(full) + gate_one * proj_ref[0]
        normed_two, inv_two = layer_norm(residual)
        h_two = (normed_two * (1.0 + scale_two) + shift_two).astype(half)
        mlp = None
        for j in range(chunks):
            cols = slice(j * features, (j + 1) * features)
            pre = dot_nn(h_two, up_ref[j]) + bias_ref[:, cols]
            square = pre * pre
            tanh_value = jnp.tanh(pre * (gelu_coef + gelu_coef * cubic_coef * square))
            gate = 0.5 + 0.5 * tanh_value
            hidden = pre * gate
            slope_ref[:, cols] = gate + hidden * (1.0 - gate) * (
                2.0 * gelu_coef + 6.0 * gelu_coef * cubic_coef * square
            )
            hidden_ref[:, cols] = hidden.astype(half)
            term = dot_nn(hidden_ref[:, cols], down_ref[cols, :])
            mlp = term if mlp is None else mlp + term
        mlp = mlp + bias_ref[:, wide:]
        out_ref[0] = (residual + gate_two * mlp).astype(half)
        upstream = cot_ref[0].astype(full)
        d_gate_two = jnp.sum(upstream * mlp, axis=0, keepdims=True)
        e_mlp = upstream * gate_two
        sum_mlp = jnp.sum(e_mlp, axis=0, keepdims=True)
        d_mlp = e_mlp.astype(half)
        d_h_two = None
        for j in range(chunks):
            cols = slice(j * features, (j + 1) * features)
            acc_down[:, cols] += dot_tn(d_mlp, hidden_ref[:, cols])
            e_pre = dot_nt(d_mlp, down_ref[cols, :]) * slope_ref[:, cols]
            vec_ref[4:5, cols] += jnp.sum(e_pre, axis=0, keepdims=True)
            d_pre = e_pre.astype(half)
            acc_up[j] += dot_tn(h_two, d_pre)
            term = dot_nt(d_pre, up_ref[j])
            d_h_two = term if d_h_two is None else d_h_two + term
        d_scale_two = jnp.sum(d_h_two * normed_two, axis=0, keepdims=True)
        d_shift_two = jnp.sum(d_h_two, axis=0, keepdims=True)
        d_mid = upstream + norm_back(normed_two, inv_two, d_h_two * (1.0 + scale_two))
        d_gate_one = jnp.sum(d_mid * proj_ref[0], axis=0, keepdims=True)
        sum_proj = jnp.sum(d_mid, axis=0, keepdims=True) * gate_one
        dmid_ref[0] = d_mid
        vec_ref[5:6, :features] += sum_proj
        vec_ref[5:6, features : 2 * features] += sum_mlp
        vec_ref[pl.ds(slot, 1), :] = jnp.concatenate(
            [d_gate_one, d_shift_two, d_scale_two, d_gate_two], axis=1
        )

    @pl.when(slot == pl.num_programs(0) - 1)
    def _():
        lane = lax.broadcasted_iota(jnp.int32, (1, wide), 1)
        codes = jnp.zeros((1, wide), full)
        for row in range(8):
            label = info_ref[4 + row]
            high = (label >> 5).astype(full)
            low = (label & 31).astype(full)
            codes = jnp.where(lane == row, high, codes)
            codes = jnp.where(lane == 8 + row, low, codes)
        vec_ref[6:7, :] = codes
        note_ref[...] = vec_ref[...].astype(half)
        if keep_ref.ndim == 2:
            for j in range(chunks):
                keep_ref[:, j * features : (j + 1) * features] = acc_up[j].astype(half)
            send_ref[...] = acc_down[...].T.astype(half)
            return
        down_t[...] = acc_down[...].T
        chips, groups, _, rows, _ = keep_ref.shape
        for flip, target in enumerate((keep_ref, send_ref)):
            core = info_ref[1] ^ flip
            for hop in range(chips):
                for step in range(groups):
                    chip = info_ref[2] ^ hop
                    group = info_ref[3] ^ step
                    top = pl.multiple_of((group * 2 + core) * rows, rows)
                    target[hop, step, 0] = acc_up[chip, pl.ds(top, rows), :].astype(half)
                    top = pl.multiple_of(((group * chips + chip) * 2 + core) * rows, rows)
                    target[hop, step, 1] = down_t[pl.ds(top, rows), :].astype(half)


def attn_backward(info_ref, tok_ref, mod_ref, qkv_ref, prob_ref, attn_ref, dmid_ref, *rest):
    *parts, grad_ref, keep_ref, send_ref, note_ref, vec_ref, d_qkv_ref, acc_ref, weight_ref = rest
    features = tok_ref.shape[2]
    slot = pl.program_id(0)

    @pl.when(slot == 0)
    def _():
        load_first(info_ref, weight_ref, parts)
        acc_ref[...] = jnp.zeros_like(acc_ref)
        vec_ref[...] = jnp.zeros_like(vec_ref)

    @pl.when(slot >= info_ref[0])
    def _():
        grad_ref[...] = jnp.zeros_like(grad_ref)

    @pl.when(slot < info_ref[0])
    def _():
        mods = mod_ref[0]
        shift_one = mods[:, :features]
        scale_one = mods[:, features : 2 * features]
        gate_one = mods[:, 2 * features : 3 * features]
        normed_one, inv_one = layer_norm(tok_ref[0].astype(full))
        h_one = (normed_one * (1.0 + scale_one) + shift_one).astype(half)
        d_mid = dmid_ref[0]
        d_proj = (d_mid * gate_one).astype(half)
        acc_ref[:, 3 * features :] += dot_tn(attn_ref[0], d_proj)
        d_attn = dot_nt(d_proj, weight_ref[:, 3 * features :]).astype(half)
        masks = head_masks()
        width = 2 * HD
        for pair in range(HEADS // 2):
            low = pair * width
            queries = qkv_ref[0, :, low : low + width]
            keys_h = qkv_ref[0, :, features + low : features + low + width]
            values_h = qkv_ref[0, :, 2 * features + low : 2 * features + low + width]
            d_heads = d_attn[:, low : low + width]
            product = d_heads.astype(full) * attn_ref[0, :, low : low + width].astype(full)
            sums = [None, None, None]
            for side in range(2):
                mask = masks[side]
                probs = prob_ref[0, 2 * pair + side]
                d_side = d_heads * mask.astype(half)
                delta = jnp.sum(product * mask, axis=-1, keepdims=True)
                d_prob = dot_nt(d_side, values_h)
                d_scores = (probs.astype(full) * (d_prob - delta)).astype(half)
                scaled = (mask * HD ** (-0.5)).astype(half)
                terms = (
                    dot_nn(d_scores, keys_h * scaled),
                    dot_tn(d_scores, queries * scaled),
                    dot_tn(probs, d_side),
                )
                sums = [
                    term if total is None else total + term for total, term in zip(sums, terms)
                ]
            for part in range(3):
                d_qkv_ref[:, part * features + low : part * features + low + width] = sums[
                    part
                ].astype(half)
            vec_ref[4:5, low : low + width] += jnp.sum(sums[0], axis=0, keepdims=True)
            vec_ref[4:5, features + low : features + low + width] += jnp.sum(
                sums[2], axis=0, keepdims=True
            )
        acc_ref[:, : 3 * features] += dot_tn(h_one, d_qkv_ref[...])
        d_h_one = dot_nt(d_qkv_ref[...], weight_ref[:, : 3 * features])
        d_scale_one = jnp.sum(d_h_one * normed_one, axis=0, keepdims=True)
        d_shift_one = jnp.sum(d_h_one, axis=0, keepdims=True)
        grad_ref[0] = (d_mid + norm_back(normed_one, inv_one, d_h_one * (1.0 + scale_one))).astype(
            half
        )
        vec_ref[pl.ds(slot, 1), :] = jnp.concatenate([d_shift_one, d_scale_one], axis=1)

    @pl.when(slot == pl.num_programs(0) - 1)
    def _():
        note_ref[...] = vec_ref[...].astype(half)
        if keep_ref.ndim == 2:
            keep_ref[...] = acc_ref[...].astype(half)
            send_ref[...] = jnp.zeros_like(send_ref)
            return
        pieces, rows, cols = keep_ref.shape
        chips = acc_ref.shape[1] // cols
        groups = pieces // chips
        for flip, target in enumerate((keep_ref, send_ref)):
            core = info_ref[1] ^ flip
            for chip in range(chips):
                for group in range(groups):
                    top = pl.multiple_of((group * 2 + core) * rows, rows)
                    target[chip * groups + group] = acc_ref[
                        pl.ds(top, rows), chip * cols : (chip + 1) * cols
                    ].astype(half)


def per_slot(*extent):
    return pl.BlockSpec((1,) + extent, lambda slot, info: (slot,) + (0,) * len(extent))


def whole(*extent):
    return pl.BlockSpec(extent, lambda slot, info: (0,) * len(extent))


def run_kernel(kernel, steps, work, ins, outs, scratch, info, operands):
    return pl.pallas_call(
        kernel,
        grid_spec=pltpu.PrefetchScalarGridSpec(
            num_scalar_prefetch=1,
            grid=(steps,),
            in_specs=ins,
            out_specs=[spec for spec, _ in outs],
            scratch_shapes=scratch,
        ),
        out_shape=[shape for _, shape in outs],
        cost_estimate=pl.CostEstimate(
            flops=int(work), bytes_accessed=int(work) // 300, transcendentals=int(work) // 1000
        ),
    )(info, *operands)


def adamw_update(weight, gradient, mean, square):
    mean_new = beta_one * mean + (1.0 - beta_one) * gradient
    square_new = beta_two * square + (1.0 - beta_two) * gradient * gradient
    mean_hat = mean_new / (1.0 - beta_one**STEP)
    square_hat = square_new / (1.0 - beta_two**STEP)
    weight_new = weight - learn_rate * (
        mean_hat / (jnp.sqrt(square_hat) + adam_eps) + weight_decay * weight
    )
    return (weight_new, mean_new, square_new)


def swap(values, axis, step):
    count = lax.axis_size(axis)
    return lax.ppermute(values, axis, [(i, i ^ step) for i in range(count)])


def exchange(pieces, axes):
    return lax.all_to_all(pieces, axes, 0, 0, tiled=True)


def spread(values, count, axes):
    return exchange(jnp.broadcast_to(values[None], (count,) + values.shape), axes)


def neighbours(values, axis):
    return [values] + [swap(values, axis, k) for k in range(1, lax.axis_size(axis))]


def order(pieces, index):
    buffer = jnp.zeros((len(pieces),) + pieces[0].shape, pieces[0].dtype)
    for step, piece in enumerate(pieces):
        buffer = lax.dynamic_update_index_in_dim(buffer, piece, index ^ step, 0)
    return buffer


def choose(values, index):
    return lax.dynamic_index_in_dim(values, index, 0, keepdims=False)


def add_up(pieces):
    return jnp.sum(pieces.astype(full), axis=0)


def body(
    reps,
    groups,
    tokens,
    cotangent,
    cond_table,
    labels,
    counts,
    mod_weight,
    qkv_weight,
    out_weight,
    up_weight,
    down_weight,
    biases,
    mod_mean,
    qkv_mean,
    out_mean,
    up_mean,
    down_mean,
    bias_mean,
    mod_square,
    qkv_square,
    out_square,
    up_square,
    down_square,
    bias_square,
):
    cores = 2
    chips = reps // cores
    devices = reps * groups
    core = lax.axis_index("core")
    chip = lax.axis_index("chip")
    group = lax.axis_index("fsdp")
    capacity, length, features = tokens.shape
    classes_all = cond_table.shape[0]
    wide = up_weight.shape[1]
    shard = features // groups
    rows = shard // cores
    cols = wide // chips
    down_rows = wide // (devices)
    aligned = rows % 16 == 0 and cols % 128 == 0 and (rows, cols) == (down_rows, features)

    live = lax.iota(jnp.int32, capacity) < counts[0]
    own_labels = jnp.where(live, labels, -1)
    head = jnp.concatenate([own_labels.astype(full), lax.reduce_precision(biases, 8, 7)])
    heads = spread(head[None], groups, "fsdp")[:, 0]
    group_labels = heads[:, :capacity].astype(jnp.int32)
    bias_full = heads[:, capacity:].reshape(-1)

    first_own = jnp.concatenate(
        [
            lax.dynamic_slice_in_dim(qkv_weight, core * rows, rows, 0),
            lax.dynamic_slice_in_dim(out_weight, core * rows, rows, 0),
        ],
        axis=1,
    ).astype(half)
    first_own = neighbours(first_own, "fsdp")
    first_other = [swap(part, "core", 1) for part in first_own]

    second_up = lax.dynamic_slice(up_weight, (core * rows, chip * cols), (rows, cols))
    second_down = lax.dynamic_slice_in_dim(
        down_weight, (chip * cores + core) * down_rows, down_rows, 0
    )
    if aligned:
        second_own = jnp.stack([second_up, second_down])
    else:
        second_own = jnp.concatenate([second_up.reshape(-1), second_down.reshape(-1)])
    second_own = jnp.stack(neighbours(second_own.astype(half), "fsdp"))
    second_own = neighbours(second_own, "chip")

    mod_half = mod_weight.astype(half)
    column = group * shard
    group_cond = cond_table[jnp.maximum(group_labels.reshape(-1), 0)]
    group_cond = lax.dynamic_slice_in_dim(group_cond, column, shard, 1).astype(full)
    partial = jnp.dot(
        jax.nn.silu(group_cond).astype(half), mod_half, preferred_element_type=full
    ).reshape(groups, capacity, 6 * features)
    modulation = add_up(exchange(partial, "fsdp")) + bias_full[: 6 * features]
    modulation = modulation[:, None, :]

    if aligned:
        first_parts = first_own + first_other
    else:
        first_all = order([order(first_own, group), order(first_other, group)], core)
        first_parts = [first_all.transpose(1, 0, 2, 3).reshape(features, wide)]

    info = jnp.concatenate(
        [
            jnp.stack([counts[0], core, chip, group]).astype(jnp.int32),
            own_labels,
            jnp.full((8 - capacity,), -1, jnp.int32),
        ]
    )
    nothing = jnp.zeros((features,), full)
    b0 = 6 * features
    first_bias = jnp.concatenate(
        [
            bias_full[b0 : b0 + features],
            nothing,
            bias_full[b0 + features : b0 + 3 * features],
        ]
    )[None]
    second_bias = bias_full[b0 + 3 * features :][None]
    slot_tok = per_slot(length, features)
    slot_mod = per_slot(1, 6 * features)
    first_specs = [whole(*part.shape) for part in first_parts]
    work = 2 * capacity * length * features * wide * 4

    def shaped(dtype, *extent):
        return jax.ShapeDtypeStruct(extent, dtype)

    qkv_rows, probs, attn_out, proj = run_kernel(
        attn_forward,
        capacity,
        2 * work,
        [slot_tok, slot_mod, whole(1, wide), *first_specs],
        [
            (per_slot(length, 3 * features), shaped(half, capacity, length, 3 * features)),
            (per_slot(HEADS, length, length), shaped(half, capacity, HEADS, length, length)),
            (slot_tok, shaped(half, capacity, length, features)),
            (slot_tok, shaped(full, capacity, length, features)),
        ],
        [pltpu.VMEM((features, wide), half)],
        info,
        (tokens, modulation, first_bias, *first_parts),
    )

    second_own, proj = lax.optimization_barrier((second_own, proj))
    second_other = [swap(part, "core", 1) for part in second_own]
    if aligned:
        second_parts = second_own + second_other
    else:
        second_all = order(
            [
                order([order(list(part), group) for part in side], chip)
                for side in (second_own, second_other)
            ],
            core,
        )
        border = rows * cols
        second_parts = [
            second_all[..., :border]
            .reshape(cores, chips, groups, rows, cols)
            .transpose(2, 0, 3, 1, 4)
            .reshape(features, wide),
            second_all[..., border:]
            .reshape(cores, chips, groups, down_rows, features)
            .transpose(2, 1, 0, 3, 4)
            .reshape(wide, features),
        ]
    second_specs = [whole(*part.shape) for part in second_parts]

    if aligned:
        first_packs = [(chips * groups, rows, cols)] * 2
        second_packs = [(chips, groups, 2, rows, cols)] * 2
    else:
        first_packs = [(features, wide), (8, 128)]
        second_packs = [(features, wide), (wide, features)]
    block_out, d_mid, second_keep, second_send, note_two = run_kernel(
        functools.partial(mlp_both, len(second_parts)),
        capacity,
        4 * work,
        [
            slot_tok,
            slot_tok,
            slot_mod,
            slot_tok,
            whole(1, wide + features),
            *second_specs,
        ],
        [
            (slot_tok, shaped(half, capacity, length, features)),
            (slot_tok, shaped(full, capacity, length, features)),
            *[(whole(*pack), shaped(half, *pack)) for pack in second_packs],
            (whole(8, wide), shaped(half, 8, wide)),
        ],
        [
            pltpu.VMEM((8, wide), full),
            pltpu.VMEM((length, wide), half),
            pltpu.VMEM((length, wide), full),
            pltpu.VMEM((wide // features, features, features), full),
            pltpu.VMEM((features, wide), full),
            pltpu.VMEM((wide, features), full),
            pltpu.VMEM((wide // features, features, features), half),
            pltpu.VMEM((wide, features), half),
        ],
        info,
        (tokens, cotangent, modulation, proj, second_bias, *second_parts),
    )
    if not aligned:
        up_part = (
            second_keep.reshape(groups, cores, rows, chips, cols)
            .transpose(1, 3, 0, 2, 4)
            .reshape(cores, chips, groups, -1)
        )
        down_part = (
            second_send.reshape(groups, chips, cores, down_rows, features)
            .transpose(2, 1, 0, 3, 4)
            .reshape(cores, chips, groups, -1)
        )
        packed = jnp.concatenate([up_part, down_part], axis=-1)
        packed = packed[:, lax.iota(jnp.int32, chips) ^ chip]
        packed = packed[:, :, lax.iota(jnp.int32, groups) ^ group]
        second_keep, second_send = choose(packed, core), choose(packed, 1 - core)
    second_back = swap(second_send, "core", 1)
    by_chip = [
        (second_keep[k].astype(full) + second_back[k].astype(full)).astype(half)
        for k in range(chips)
    ]
    by_chip = [by_chip[0]] + [swap(by_chip[k], "chip", k) for k in range(1, chips)]
    all_two = spread(note_two, devices, ("chip", "core", "fsdp"))

    token_grad, first_keep, first_send, note_three = run_kernel(
        attn_backward,
        capacity,
        3 * work,
        [
            slot_tok,
            slot_mod,
            per_slot(length, 3 * features),
            per_slot(HEADS, length, length),
            slot_tok,
            slot_tok,
            *first_specs,
        ],
        [
            (slot_tok, shaped(half, capacity, length, features)),
            *[(whole(*pack), shaped(half, *pack)) for pack in first_packs],
            (whole(8, 2 * features), shaped(half, 8, 2 * features)),
        ],
        [
            pltpu.VMEM((8, 2 * features), full),
            pltpu.VMEM((length, 3 * features), half),
            pltpu.VMEM((features, wide), full),
            pltpu.VMEM((features, wide), half),
        ],
        info,
        (tokens, modulation, qkv_rows, probs, attn_out, d_mid, *first_parts),
    )
    if not aligned:
        packed = (
            first_keep.reshape(groups, cores, rows, chips, cols)
            .transpose(1, 3, 0, 2, 4)
            .reshape(cores, chips * groups, rows, cols)
        )
        first_keep, first_send = choose(packed, core), choose(packed, 1 - core)
    first_back = swap(first_send, "core", 1)
    first_sum = (first_keep.astype(full) + first_back.astype(full)).astype(half)
    pieces = exchange(first_sum, ("chip", "fsdp"))
    by_chip, all_two, first_sum = lax.optimization_barrier((by_chip, all_two, first_sum))

    by_group = []
    for k in range(groups):
        total = by_chip[0][k].astype(full)
        for part in by_chip[1:]:
            total = total + part[k].astype(full)
        by_group.append(total.astype(half))
    second_sum = by_group[0].astype(full)
    for k in range(1, groups):
        second_sum = second_sum + swap(by_group[k], "fsdp", k).astype(full)
    second_sum = second_sum.astype(half)

    note_three = jnp.stack(neighbours(note_three, "fsdp"))
    note_three = jnp.stack(neighbours(note_three, "chip"))
    note_three = jnp.stack(neighbours(note_three, "core"))
    count = devices * 8
    spot = lax.iota(jnp.int32, count)
    line, where = spot % 8, spot // 8
    where_group = (where % groups) ^ group
    where_core = (where // groups % cores) ^ core
    where_chip = (where // (groups * cores)) ^ chip
    where = ((where_core * chips + where_chip) * groups + where_group) * 8 + line
    moved = (where[:, None] == spot[None, :]).astype(half)
    d_three = jnp.dot(
        moved, note_three.reshape(count, 2 * features), preferred_element_type=full
    ).astype(half)
    d_two = all_two.reshape(count, wide)

    first_sum = add_up(pieces).astype(half)
    if aligned:
        third = jnp.concatenate([second_sum, first_sum[None]])
    else:
        third = jnp.concatenate([second_sum, first_sum.reshape(-1)])
    third = spread(third, reps, ("chip", "core")).reshape(chips, cores, *third.shape)
    if aligned:
        up_all, down_all, first_all = third[:, :, 0], third[:, :, 1], third[:, :, 2]
    else:
        border = rows * cols
        up_all = third[..., :border].reshape(chips, cores, rows, cols)
        down_all = third[..., border : border + down_rows * features]
        first_all = third[..., border + down_rows * features :]
        first_all = first_all.reshape(chips, cores, rows, cols)
    up_grad = up_all.transpose(1, 2, 0, 3).reshape(shard, wide).astype(full)
    down_grad = down_all.reshape(down_weight.shape).astype(full)
    first_grad = first_all.transpose(1, 2, 0, 3).reshape(shard, wide).astype(full)
    qkv_grad = first_grad[:, : 3 * features]
    out_grad = first_grad[:, 3 * features :]

    label_notes = all_two[:, 6, :16].astype(jnp.int32)
    all_labels = (32 * label_notes[:, :8] + label_notes[:, 8:]).reshape(-1)
    all_cond = cond_table[jnp.maximum(all_labels, 0)]
    all_cond = lax.dynamic_slice_in_dim(all_cond, column, shard, 1).astype(full)
    all_live = (all_labels >= 0)[:, None]
    sigmoid_c = jax.nn.sigmoid(all_cond)
    all_active = jnp.where(all_live, all_cond * sigmoid_c, 0.0).astype(half)
    slope_c = jnp.where(all_live, sigmoid_c * (1.0 + all_cond * (1.0 - sigmoid_c)), 0.0)
    mod_grad = jnp.concatenate([dot_tn(all_active, d_three), dot_tn(all_active, d_two)], axis=1)
    d_act = dot_nt(d_three, mod_half[:, : 2 * features]) + dot_nt(
        d_two, mod_half[:, 2 * features :]
    )
    picks = jnp.stack([line < capacity, line == 4, line == 5]).astype(half)
    sum_two = dot_nn(picks, d_two)
    sum_three = dot_nn(picks, d_three)
    d_cond = order(neighbours((d_act * slope_c).astype(half), "fsdp"), group)
    class_share = classes_all // groups
    class_ids = lax.iota(jnp.int32, class_share) + group * class_share
    chosen = (class_ids[:, None] == all_labels[None, :]).astype(half)
    table_grad = jnp.concatenate(
        [
            jnp.dot(chosen, d_cond[k], preferred_element_type=full)
            for k in range(groups)
        ],
        axis=1,
    )
    bias_all = jnp.concatenate(
        [
            sum_three[0],
            sum_two[0],
            sum_three[1],
            sum_two[2, :features],
            sum_two[1],
            sum_two[2, features : 2 * features],
        ]
    )
    bias_share = biases.shape[0]
    bias_grad = lax.dynamic_slice_in_dim(bias_all, group * bias_share, bias_share, 0)

    mod_next, mean_mod, square_mod = adamw_update(mod_weight, mod_grad, mod_mean, mod_square)
    qkv_next, mean_qkv, square_qkv = adamw_update(qkv_weight, qkv_grad, qkv_mean, qkv_square)
    out_next, mean_out, square_out = adamw_update(out_weight, out_grad, out_mean, out_square)
    up_next, mean_up, square_up = adamw_update(up_weight, up_grad, up_mean, up_square)
    down_next, mean_down, square_down = adamw_update(down_weight, down_grad, down_mean, down_square)
    bias_next, mean_bias, square_bias = adamw_update(biases, bias_grad, bias_mean, bias_square)
    return (
        block_out,
        token_grad,
        table_grad,
        mod_grad,
        qkv_grad,
        out_grad,
        up_grad,
        down_grad,
        bias_grad,
        mod_next,
        qkv_next,
        out_next,
        up_next,
        down_next,
        bias_next,
        mean_mod,
        mean_qkv,
        mean_out,
        mean_up,
        mean_down,
        mean_bias,
        square_mod,
        square_qkv,
        square_out,
        square_up,
        square_down,
        square_bias,
    )


def solution(mesh):
    placed = (
        P(("chip", "core", "fsdp"), None, None),
        P(("chip", "core", "fsdp"), None, None),
        P(),
        P(("chip", "core", "fsdp")),
        P(("chip", "core", "fsdp")),
        P("fsdp", None),
        P("fsdp", None),
        P("fsdp", None),
        P("fsdp", None),
        P("fsdp", None),
        P("fsdp"),
        P("fsdp", None),
        P("fsdp", None),
        P("fsdp", None),
        P("fsdp", None),
        P("fsdp", None),
        P("fsdp"),
        P("fsdp", None),
        P("fsdp", None),
        P("fsdp", None),
        P("fsdp", None),
        P("fsdp", None),
        P("fsdp"),
    )
    reps, groups = mesh.shape["rep"], mesh.shape["fsdp"]
    fine = Mesh(mesh.devices.reshape(reps // 2, 2, groups), ("chip", "core", "fsdp"))
    return jax.shard_map(
        functools.partial(body, reps, groups),
        mesh=fine,
        in_specs=placed,
        out_specs=(
            P(("chip", "core", "fsdp"), None, None),
            P(("chip", "core", "fsdp"), None, None),
            P("fsdp", None),
            P("fsdp", None),
            P("fsdp", None),
            P("fsdp", None),
            P("fsdp", None),
            P("fsdp", None),
            P("fsdp"),
            P("fsdp", None),
            P("fsdp", None),
            P("fsdp", None),
            P("fsdp", None),
            P("fsdp", None),
            P("fsdp"),
            P("fsdp", None),
            P("fsdp", None),
            P("fsdp", None),
            P("fsdp", None),
            P("fsdp", None),
            P("fsdp"),
            P("fsdp", None),
            P("fsdp", None),
            P("fsdp", None),
            P("fsdp", None),
            P("fsdp", None),
            P("fsdp"),
        ),
        check_vma=False,
    )
```

time: 897 us -> 196 us (0.22)
  waiting for transfers between devices: 504 us -> 46.4 us
  blocking collectives: 214 us -> 0 us
  starting transfers between devices: 1.65 us -> 73.4 us
  local copies, waits for them, and re-layouts: 57.9 us -> 20.2 us
  matrix products: 40.2 us -> 3.68 us
  Pallas kernels: 0 us -> 29.4 us
  other arithmetic: 49.2 us -> 19.9 us
  between operations: 16.3 us -> 2.01 us
    reduce_scatter x5 -> x0, waiting for transfers between devices: 405 us -> none  [the longest x1 197 us: body(): lax.psum_scatter(sum_out, 'fsdp', scatter_dimension=0, tiled=True)]
    unnamed x3 -> x0, blocking collectives: 161 us -> none
    ppermute x0 -> x35, starting transfers between devices: none -> 52.7 us  [swap(): return lax.ppermute(values, axis, [(i, i ^ step) for i in range(count)])]
    all_gather x3 -> x0, waiting for transfers between devices: 52.6 us -> none  [the longest x1 42.5 us: body(): lax.all_gather(mod_half, 'fsdp', axis=0, tiled=True)]
    psum x1 -> x0, waiting for transfers between devices: 42.8 us -> none  [body(): lax.psum((mod_share, shares[0], shares[1], shares[2], shares[3], shares[4...]
    all_gather x2 -> x0, blocking collectives: 40 us -> none  [the longest x1 23.4 us: body(): lax.all_gather(qkv_half, 'fsdp', axis=0, tiled=True)]
    dot_general x21 -> x12, matrix products: 40.2 us -> 3.68 us  [the longest x2 1.29 us: dot_nt(): lax.dot_general(left, right, (((1,), (1,)), ((), ())), preferred_element_...]
    pallas_call x0 -> x3, Pallas kernels: none -> 29.4 us  [run_kernel(): pl.pallas_call(kernel, grid_spec=pltpu.PrefetchScalarGridSpec(num_scalar_...]
  transfers between devices with their start and end apart: 10 -> 40, of which waited for: 9 -> 12; matrix products, arithmetic and copies ran while one was open for 14% -> 15% of each run, Pallas kernels for 0% -> 4%
where the time goes in v1:
time: 196 us; the launch traced here: 195 us
  starting transfers between devices  73.4 us (37%)
  waiting for transfers between devices  46.4 us (24%)
  Pallas kernels  29.4 us (15%)
  local copies, waits for them, and re-layouts  20.2 us (10%)
  other arithmetic  19.9 us (10%)
  matrix products  3.68 us (2%)
  between operations  2.01 us (1%)
    ppermute x35, starting transfers between devices, swap(): return lax.ppermute(values, axis, [(i, i ^ step) for i in range(count)])  52.7 us
    pallas_call x3, Pallas kernels, run_kernel(): pl.pallas_call(kernel, grid_spec=pltpu.PrefetchScalarGridSpec(num_scalar_...  29.4 us
    ppermute x35, waiting for transfers between devices, swap(): return lax.ppermute(values, axis, [(i, i ^ step) for i in range(count)])  24.7 us
    all_to_all x5, waiting for transfers between devices, exchange(): return lax.all_to_all(pieces, axes, 0, 0, tiled=True)  21.7 us
    all_to_all x5, starting transfers between devices, exchange(): return lax.all_to_all(pieces, axes, 0, 0, tiled=True)  20.6 us
    sub x6, other arithmetic, adamw_update(): weight - learn_rate * (mean_hat / (jnp.sqrt(square_hat) + adam_eps) + wei...  7.9 us
    unnamed x90, local copies, waits for them, and re-layouts  6.35 us
  transfers between devices with their start and end apart: 40, of which 12 were waited for; matrix products, arithmetic and copies ran while one was open for 15% of the time, Pallas kernels for 4%

profile of v1, /device:TPU:0, one launch (start us, length us, event | category | flops | bytes accessed | tf_op | source)
XLA Modules:
  0.0 195.0 jit_solution(13302588510951958910)
XLA Ops:
  2.7 3.1 %collective-permute-start.6 = (bf16[48,1536]{1,0:T(8,128)(2,1)S(1)}, bf16[48,1536]{1,0:T(8,128)(2,1)}, u32[]{:S(2)}, u32[]{:S(2)}) collective-permute-start(bf16[48,1536]{1,0:T(8,128)(2,1)S(1)} %pad_maximum_fusion.5.rest_0_), channel_id=1, source_target_pairs={{0,1},{1,0},{2,3},{3,2},{4,5},{5,4},{6,7},{7,6},{8,9},{9,8},{10,11... | collective-permute-start | bytes 442376 | tf_op jit(solution)/shard_map/ppermute | solution.py:369
  5.8 2.6 %collective-permute-start.7 = (bf16[48,1536]{1,0:T(8,128)(2,1)S(1)}, bf16[48,1536]{1,0:T(8,128)(2,1)}, u32[]{:S(2)}, u32[]{:S(2)}) collective-permute-start(bf16[48,1536]{1,0:T(8,128)(2,1)S(1)} %pad_maximum_fusion.5.rest_0_), channel_id=1, source_target_pairs={{0,2},{1,3},{2,0},{3,1},{4,6},{5,7},{6,4},{7,5},{8,10},{9,11},{10,... | collective-permute-start | bytes 442376 | tf_op jit(solution)/shard_map/ppermute | solution.py:369
  11.1 5.1 %all-to-all-start = ((f32[4,1,1348]{2,1,0:T(1,128)}), f32[4,1,1348]{2,1,0:T(1,128)S(1)}, u32[]{:S(2)}, u32[]{:S(2)}) async-start(f32[4,1,1348]{2,1,0:T(1,128)} %broadcast_in_dim.74), calls=%async_computation | async-start | bytes 45056 | tf_op jit(solution)/shard_map/all_to_all | solution.py:373
  18.0 3.9 %collective-permute-start.2 = (bf16[2,48,384]{2,1,0:T(8,128)(2,1)S(1)}, bf16[2,48,384]{2,1,0:T(8,128)(2,1)S(1)}, u32[]{:S(2)}, u32[]{:S(2)}) collective-permute-start(bf16[2,48,384]{2,1,0:T(8,128)(2,1)S(1)} %pad_maximum_fusion.7), channel_id=1, source_target_pairs={{0,3},{1,2},{2,1},{3,0},{4,7},{5,6},{6,5},{7,4},{8,11},{9,10},{10,... | collective-permute-start | bytes 221192 | tf_op jit(solution)/shard_map/ppermute | solution.py:369
  22.6 1.8 all-to-all-done
  26.3 3.3 %all-to-all-start.1 = ((f32[4,4,2304]{2,1,0:T(4,128)}), f32[4,4,2304]{2,1,0:T(4,128)S(1)}, u32[]{:S(2)}, u32[]{:S(2)}) async-start(f32[4,4,2304]{2,1,0:T(4,128)} %reshape.339), calls=%async_computation.1 | async-start | bytes 294912 | tf_op jit(solution)/shard_map/all_to_all | solution.py:373
  29.6 2.9 %collective-permute-start.1 = (bf16[2,48,384]{2,1,0:T(8,128)(2,1)S(1)}, bf16[2,48,384]{2,1,0:T(8,128)(2,1)S(1)}, u32[]{:S(2)}, u32[]{:S(2)}) collective-permute-start(bf16[2,48,384]{2,1,0:T(8,128)(2,1)S(1)} %pad_maximum_fusion.7), channel_id=1, source_target_pairs={{0,2},{1,3},{2,0},{3,1},{4,6},{5,7},{6,4},{7,5},{8,10},{9,11},{10,... | collective-permute-start | bytes 221192 | tf_op jit(solution)/shard_map/ppermute | solution.py:369
  33.1 4.3 %collective-permute-done.1 = bf16[2,48,384]{2,1,0:T(8,128)(2,1)S(1)} collective-permute-done((bf16[2,48,384]{2,1,0:T(8,128)(2,1)S(1)}, bf16[2,48,384]{2,1,0:T(8,128)(2,1)S(1)}, u32[]{:S(2)}, u32[]{:S(2)}) %collective-permute-start.1) | collective-permute-done | bytes 73760 | tf_op jit(solution)/shard_map/ppermute | solution.py:369
  42.5 7.7 %shard_map.430 = (bf16[4,256,1152]{2,1,0:T(8,128)(2,1)}, bf16[4,6,256,256]{3,2,1,0:T(8,128)(2,1)}, bf16[4,256,384]{2,1,0:T(8,128)(2,1)}, f32[4,256,384]{2,1,0:T(8,128)}) custom-call(s32[12]{0:T(128)} %concatenate.33.info_ref, bf16[4,256,384]{2,1,0:T(8,128)(2,1)} %tok_ref.5, f32[4,1,2304]{2,1,0:T(1,128)} %reshape_add_fusion.mod_ref, ...), custom_call_target="tpu_custom_call" | custom-call | flops 9663676416 | bytes 32212254 | tf_op jit(solution)/shard_map/pallas_call | solution.py:340
  50.2 5.8 %collective-permute-done.4.rest_2_ = bf16[4,2,48,384]{3,2,1,0:T(8,128)(2,1)S(1)} collective-permute-done((bf16[4,2,48,384]{3,2,1,0:T(8,128)(2,1)S(1)}, bf16[4,2,48,384]{3,2,1,0:T(8,128)(2,1)S(1)}, u32[]{:S(2)}, u32[]{:S(2)}) %collective-permute-start.4) | collective-permute-done | bytes 294944 | tf_op jit(solution)/shard_map/ppermute | solution.py:369
  59.5 12.2 %shard_map.431 = (bf16[4,256,384]{2,1,0:T(8,128)(2,1)}, f32[4,256,384]{2,1,0:T(8,128)}, bf16[4,4,2,48,384]{4,3,2,1,0:T(8,128)(2,1)}, bf16[4,4,2,48,384]{4,3,2,1,0:T(8,128)(2,1)}, bf16[8,1536]{1,0:T(8,128)(2,1)}) custom-call(s32[12]{0:T(128)} %concatenate.33.info_ref, bf16[4,256,384]{2,1,0:T(8,128)(2,1)} %tok_ref.5, bf16[4,256,384]{2,1,0:T(8,128)(2,1)} %cot_ref.1, ...), custom_call_target="tpu_custom_call" | custom-call | flops 19327352832 | bytes 64424508 | tf_op jit(solution)/shard_map/pallas_call | solution.py:340
  71.7 9.5 %shard_map.432 = (bf16[4,256,384]{2,1,0:T(8,128)(2,1)}, bf16[16,48,384]{2,1,0:T(8,128)(2,1)}, bf16[16,48,384]{2,1,0:T(8,128)(2,1)}, bf16[8,768]{1,0:T(8,128)(2,1)}) custom-call(s32[12]{0:T(128)} %concatenate.33.info_ref, bf16[4,256,384]{2,1,0:T(8,128)(2,1)} %tok_ref.5, f32[4,1,2304]{2,1,0:T(1,128)} %reshape_add_fusion.mod_ref, ...), custom_call_target="tpu_custom_call" | custom-call | flops 14495514624 | bytes 48318384 | tf_op jit(solution)/shard_map/pallas_call | solution.py:340
  81.6 8.4 %collective-permute-start.23 = (bf16[8,768]{1,0:T(8,128)(2,1)}, bf16[8,768]{1,0:T(8,128)(2,1)S(1)}, u32[]{:S(2)}, u32[]{:S(2)}) collective-permute-start(bf16[8,768]{1,0:T(8,128)(2,1)} %get-tuple-element.68), channel_id=1, source_target_pairs={{0,2},{1,3},{2,0},{3,1},{4,6},{5,7},{6,4},{7,5},{8,10},{9,11},{10,... | collective-permute-start | bytes 36872 | tf_op jit(solution)/shard_map/ppermute | solution.py:369
  90.1 1.9 collective-permute-done.23
  92.0 3.8 %collective-permute-done.24 = bf16[8,768]{1,0:T(8,128)(2,1)S(1)} collective-permute-done((bf16[8,768]{1,0:T(8,128)(2,1)}, bf16[8,768]{1,0:T(8,128)(2,1)S(1)}, u32[]{:S(2)}, u32[]{:S(2)}) %collective-permute-start.24) | collective-permute-done | bytes 12320 | tf_op jit(solution)/shard_map/ppermute | solution.py:369
  96.5 4.7 %collective-permute-start.25 = (bf16[4,8,768]{2,1,0:T(8,128)(2,1)S(1)}, bf16[4,8,768]{2,1,0:T(8,128)(2,1)S(1)}, u32[]{:S(2)}, u32[]{:S(2)}) collective-permute-start(bf16[4,8,768]{2,1,0:T(8,128)(2,1)S(1)} %get-tuple-element.231), channel_id=1, source_target_pairs={{0,8},{8,0},{16,24},{24,16},{1,9},{9,1},{17,25},{25,17},{2,10},{10... | collective-permute-start | bytes 147464 | tf_op jit(solution)/shard_map/ppermute | solution.py:369
  103.6 4.0 %collective-permute-start.17 = (bf16[4,4,2,48,384]{4,3,2,1,0:T(8,128)(2,1)}, bf16[4,4,2,48,384]{4,3,2,1,0:T(8,128)(2,1)}, u32[]{:S(2)}, u32[]{:S(2)}) collective-permute-start(bf16[4,4,2,48,384]{4,3,2,1,0:T(8,128)(2,1)} %get-tuple-element.63), channel_id=1, source_target_pairs={{0,4},{4,0},{1,5},{5,1},{2,6},{6,2},{3,7},{7,3},{8,12},{12,8},{9,1... | collective-permute-start | bytes 3538952 | tf_op jit(solution)/shard_map/ppermute | solution.py:369
  107.7 2.6 %collective-permute-start.28 = (bf16[4,4,8,768]{3,2,1,0:T(8,128)(2,1)S(1)}, bf16[4,4,8,768]{3,2,1,0:T(8,128)(2,1)S(1)}, u32[]{:S(2)}, u32[]{:S(2)}) collective-permute-start(bf16[4,4,8,768]{3,2,1,0:T(8,128)(2,1)S(1)} %get-tuple-element.229), channel_id=1, source_target_pairs={{0,4},{4,0},{1,5},{5,1},{2,6},{6,2},{3,7},{7,3},{8,12},{12,8},{9,1... | collective-permute-start | bytes 589832 | tf_op jit(solution)/shard_map/ppermute | solution.py:369
  111.8 2.8 %all-to-all-start.2 = ((bf16[32,8,1536]{2,1,0:T(8,128)(2,1)}), bf16[32,8,1536]{2,1,0:T(8,128)(2,1)S(1)}, u32[]{:S(2)}, u32[]{:S(2)}) async-start(bf16[32,8,1536]{2,1,0:T(8,128)(2,1)} %broadcast_in_dim.78), calls=%async_computation.2 | async-start | bytes 1572864 | tf_op jit(solution)/shard_map/all_to_all | solution.py:373
  116.7 2.5 %fusion.22 = (bf16[4,2,48,384]{3,2,1,0:T(8,128)(2,1)}, bf16[4,2,48,384]{3,2,1,0:T(8,128)(2,1)}, bf16[4,2,48,384]{3,2,1,0:T(8,128)(2,1)}, bf16[4,2,48,384]{3,2,1,0:T(8,128)(2,1)}) fusion(bf16[4,4,2,48,384]{4,3,2,1,0:T(8,128)(2,1)} %collective-permute-done.17, bf16[4,4,2,48,384]{4,3,2,1,0:T(8,128)(2,1)S(1)} %copy-done.3), kind=kLoop, calls=%fused_computation.48 | loop fusion | flops 2359296 | bytes 3538944 | tf_op jit(solution)/shard_map/convert_element_type | solution.py:605
  119.2 1.6 collective-permute-start.18
  124.0 2.0 %add_convert_fusion = bf16[16,48,384]{2,1,0:T(8,128)(2,1)} fusion(bf16[16,48,384]{2,1,0:T(8,128)(2,1)} %collective-permute-done.21, bf16[16,48,384]{2,1,0:T(8,128)(2,1)S(1)} %copy-done.12), kind=kLoop, calls=%fused_computation.4 | loop fusion | flops 1179648 | bytes 1769472 | tf_op jit(solution)/shard_map/convert_element_type | solution.py:646
  126.1 8.0 %all-to-all-done.2 = bf16[32,8,1536]{2,1,0:T(8,128)(2,1)S(1)} async-done(((bf16[32,8,1536]{2,1,0:T(8,128)(2,1)}), bf16[32,8,1536]{2,1,0:T(8,128)(2,1)S(1)}, u32[]{:S(2)}, u32[]{:S(2)}) %all-to-all-start.2) | async-done | bytes 786464 | tf_op jit(solution)/shard_map/all_to_all | solution.py:373
  134.1 5.7 %all-to-all-start.3 = ((bf16[16,48,384]{2,1,0:T(8,128)(2,1)}), bf16[16,48,384]{2,1,0:T(8,128)(2,1)}, u32[]{:S(2)}, u32[]{:S(2)}) async-start(bf16[16,48,384]{2,1,0:T(8,128)(2,1)} %add_convert_fusion), calls=%async_computation.3 | async-start | bytes 1179648 | tf_op jit(solution)/shard_map/all_to_all | solution.py:373
  144.6 1.9 collective-permute-start.29
  146.5 2.0 %collective-permute-start.30 = (bf16[256,96]{0,1:T(8,128)(2,1)S(1)}, bf16[256,96]{0,1:T(8,128)(2,1)S(1)}, u32[]{:S(2)}, u32[]{:S(2)}) collective-permute-start(bf16[256,96]{0,1:T(8,128)(2,1)S(1)} %get-tuple-element.233), channel_id=1, source_target_pairs={{0,2},{1,3},{2,0},{3,1},{4,6},{5,7},{6,4},{7,5},{8,10},{9,11},{10,... | collective-permute-start | bytes 147464 | tf_op jit(solution)/shard_map/ppermute | solution.py:369
  151.4 2.9 %collective-permute-start.33 = (bf16[2,48,384]{2,1,0:T(8,128)(2,1)S(1)}, bf16[2,48,384]{2,1,0:T(8,128)(2,1)S(1)}, u32[]{:S(2)}, u32[]{:S(2)}) collective-permute-start(bf16[2,48,384]{2,1,0:T(8,128)(2,1)S(1)} %get-tuple-element.220), channel_id=1, source_target_pairs={{0,2},{1,3},{2,0},{3,1},{4,6},{5,7},{6,4},{7,5},{8,10},{9,11},{10,... | collective-permute-start | bytes 221192 | tf_op jit(solution)/shard_map/ppermute | solution.py:369
  154.5 2.0 %multiply_subtract_fusion = (f32[96,2304]{1,0:T(8,128)}, f32[96,2304]{1,0:T(8,128)}, f32[96,2304]{1,0:T(8,128)}, f32[96,2304]{1,0:T(8,128)}) fusion(f32[96,2304]{1,0:T(8,128)S(1)} %copy-done.1, f32[96,2304]{1,0:T(8,128)S(1)} %copy-done.5, f32[96,2304]{1,0:T(8,128)S(1)} %copy-done.6, f32[96,1536]{1,0:T(8,128)S(1)} %fusion.5, f32[96,768]{1,0:T(8,128)S(1)} %fusion.78), kind=kLoop, calls=%fused_computation.10 | loop fusion | flops 3538944 | bytes 7077888 | tf_op jit(solution)/shard_map/sub | solution.py:361
  157.8 4.6 %collective-permute-done.30 = bf16[256,96]{0,1:T(8,128)(2,1)S(1)} collective-permute-done((bf16[256,96]{0,1:T(8,128)(2,1)S(1)}, bf16[256,96]{0,1:T(8,128)(2,1)S(1)}, u32[]{:S(2)}, u32[]{:S(2)}) %collective-permute-start.30) | collective-permute-done | bytes 49184 | tf_op jit(solution)/shard_map/ppermute | solution.py:369
  162.8 3.1 %collective-permute-done.33 = bf16[2,48,384]{2,1,0:T(8,128)(2,1)S(1)} collective-permute-done((bf16[2,48,384]{2,1,0:T(8,128)(2,1)S(1)}, bf16[2,48,384]{2,1,0:T(8,128)(2,1)S(1)}, u32[]{:S(2)}, u32[]{:S(2)}) %collective-permute-start.33) | collective-permute-done | bytes 73760 | tf_op jit(solution)/shard_map/ppermute | solution.py:369
  169.1 3.7 %all-to-all-start.4 = ((bf16[8,3,48,384]{3,2,1,0:T(8,128)(2,1)}), bf16[8,3,48,384]{3,2,1,0:T(8,128)(2,1)S(1)}, u32[]{:S(2)}, u32[]{:S(2)}) async-start(bf16[8,3,48,384]{3,2,1,0:T(8,128)(2,1)} %broadcast_in_dim.87), calls=%async_computation.4 | async-start | bytes 1769472 | tf_op jit(solution)/shard_map/all_to_all | solution.py:373
  174.6 11.9 %all-to-all-done.4 = bf16[8,3,48,384]{3,2,1,0:T(8,128)(2,1)S(1)} async-done(((bf16[8,3,48,384]{3,2,1,0:T(8,128)(2,1)}), bf16[8,3,48,384]{3,2,1,0:T(8,128)(2,1)S(1)}, u32[]{:S(2)}, u32[]{:S(2)}) %all-to-all-start.4) | async-done | bytes 884768 | tf_op jit(solution)/shard_map/all_to_all | solution.py:373
  (226 shorter events, 50.5 us)
Async XLA Ops:
  2.7 36.3 %collective-permute-start.6 = (bf16[48,1536]{1,0:T(8,128)(2,1)S(1)}, bf16[48,1536]{1,0:T(8,128)(2,1)}, u32[]{:S(2)}, u32[]{:S(2)}) collective-permute-start(bf16[48,1536]{1,0:T(8,128)(2,1)S(1)} %pad_maximum_fusion.5.rest_0_), channel_id=1, source_target_pairs={{0,1},{1,0},{2,3},{3,2},{4,5},{5,4},{6,7},{7,6},{8,9},{9,8},{10,11... | collective-permute-start | bytes 442376 | tf_op jit(solution)/shard_map/ppermute | solution.py:369
  5.8 33.2 %collective-permute-start.7 = (bf16[48,1536]{1,0:T(8,128)(2,1)S(1)}, bf16[48,1536]{1,0:T(8,128)(2,1)}, u32[]{:S(2)}, u32[]{:S(2)}) collective-permute-start(bf16[48,1536]{1,0:T(8,128)(2,1)S(1)} %pad_maximum_fusion.5.rest_0_), channel_id=1, source_target_pairs={{0,2},{1,3},{2,0},{3,1},{4,6},{5,7},{6,4},{7,5},{8,10},{9,11},{10,... | collective-permute-start | bytes 442376 | tf_op jit(solution)/shard_map/ppermute | solution.py:369
  8.4 31.1 %collective-permute-start.8 = (bf16[48,1536]{1,0:T(8,128)(2,1)S(1)}, bf16[48,1536]{1,0:T(8,128)(2,1)}, u32[]{:S(2)}, u32[]{:S(2)}) collective-permute-start(bf16[48,1536]{1,0:T(8,128)(2,1)S(1)} %pad_maximum_fusion.5.rest_0_), channel_id=1, source_target_pairs={{0,3},{1,2},{2,1},{3,0},{4,7},{5,6},{6,5},{7,4},{8,11},{9,10},{10,... | collective-permute-start | bytes 442376 | tf_op jit(solution)/shard_map/ppermute | solution.py:369
  11.1 13.3 %all-to-all-start = ((f32[4,1,1348]{2,1,0:T(1,128)}), f32[4,1,1348]{2,1,0:T(1,128)S(1)}, u32[]{:S(2)}, u32[]{:S(2)}) async-start(f32[4,1,1348]{2,1,0:T(1,128)} %broadcast_in_dim.74), calls=%async_computation | async-start | bytes 45056 | tf_op jit(solution)/shard_map/all_to_all | solution.py:373
  18.0 11.6 %collective-permute-start.2 = (bf16[2,48,384]{2,1,0:T(8,128)(2,1)S(1)}, bf16[2,48,384]{2,1,0:T(8,128)(2,1)S(1)}, u32[]{:S(2)}, u32[]{:S(2)}) collective-permute-start(bf16[2,48,384]{2,1,0:T(8,128)(2,1)S(1)} %pad_maximum_fusion.7), channel_id=1, source_target_pairs={{0,3},{1,2},{2,1},{3,0},{4,7},{5,6},{6,5},{7,4},{8,11},{9,10},{10,... | collective-permute-start | bytes 221192 | tf_op jit(solution)/shard_map/ppermute | solution.py:369
  21.9 11.2 %collective-permute-start = (bf16[2,48,384]{2,1,0:T(8,128)(2,1)S(1)}, bf16[2,48,384]{2,1,0:T(8,128)(2,1)S(1)}, u32[]{:S(2)}, u32[]{:S(2)}) collective-permute-start(bf16[2,48,384]{2,1,0:T(8,128)(2,1)S(1)} %pad_maximum_fusion.7), channel_id=1, source_target_pairs={{0,1},{1,0},{2,3},{3,2},{4,5},{5,4},{6,7},{7,6},{8,9},{9,8},{10,11... | collective-permute-start | bytes 221192 | tf_op jit(solution)/shard_map/ppermute | solution.py:369
  26.3 13.4 %all-to-all-start.1 = ((f32[4,4,2304]{2,1,0:T(4,128)}), f32[4,4,2304]{2,1,0:T(4,128)S(1)}, u32[]{:S(2)}, u32[]{:S(2)}) async-start(f32[4,4,2304]{2,1,0:T(4,128)} %reshape.339), calls=%async_computation.1 | async-start | bytes 294912 | tf_op jit(solution)/shard_map/all_to_all | solution.py:373
  29.6 7.8 %collective-permute-start.1 = (bf16[2,48,384]{2,1,0:T(8,128)(2,1)S(1)}, bf16[2,48,384]{2,1,0:T(8,128)(2,1)S(1)}, u32[]{:S(2)}, u32[]{:S(2)}) collective-permute-start(bf16[2,48,384]{2,1,0:T(8,128)(2,1)S(1)} %pad_maximum_fusion.7), channel_id=1, source_target_pairs={{0,2},{1,3},{2,0},{3,1},{4,6},{5,7},{6,4},{7,5},{8,10},{9,11},{10,... | collective-permute-start | bytes 221192 | tf_op jit(solution)/shard_map/ppermute | solution.py:369
  33.1 7.2 %collective-permute-start.9 = (bf16[48,1536]{1,0:T(8,128)(2,1)S(1)}, bf16[48,1536]{1,0:T(8,128)(2,1)}, u32[]{:S(2)}, u32[]{:S(2)}) collective-permute-start(bf16[48,1536]{1,0:T(8,128)(2,1)S(1)} %pad_maximum_fusion.5.rest_0_), channel_id=1, source_target_pairs={{0,4},{4,0},{1,5},{5,1},{2,6},{6,2},{3,7},{7,3},{8,12},{12,8},{9,1... | collective-permute-start | bytes 442376 | tf_op jit(solution)/shard_map/ppermute | solution.py:369
  37.5 12.7 %collective-permute-start.3 = (bf16[4,2,48,384]{3,2,1,0:T(8,128)(2,1)S(1)}, bf16[4,2,48,384]{3,2,1,0:T(8,128)(2,1)S(1)}, u32[]{:S(2)}, u32[]{:S(2)}) collective-permute-start(bf16[4,2,48,384]{3,2,1,0:T(8,128)(2,1)S(1)} %pad_maximum_fusion.3.rest_0_), channel_id=1, source_target_pairs={{0,8},{8,0},{16,24},{24,16},{1,9},{9,1},{17,25},{25,17},{2,10},{10... | collective-permute-start | bytes 884744 | tf_op jit(solution)/shard_map/ppermute | solution.py:369
  40.3 15.7 %collective-permute-start.4 = (bf16[4,2,48,384]{3,2,1,0:T(8,128)(2,1)S(1)}, bf16[4,2,48,384]{3,2,1,0:T(8,128)(2,1)S(1)}, u32[]{:S(2)}, u32[]{:S(2)}) collective-permute-start(bf16[4,2,48,384]{3,2,1,0:T(8,128)(2,1)S(1)} %pad_maximum_fusion.3.rest_0_), channel_id=1, source_target_pairs={{0,16},{8,24},{16,0},{24,8},{1,17},{9,25},{17,1},{25,9},{2,18},{10... | collective-permute-start | bytes 884744 | tf_op jit(solution)/shard_map/ppermute | solution.py:369
  41.8 14.2 %collective-permute-start.5 = (bf16[4,2,48,384]{3,2,1,0:T(8,128)(2,1)S(1)}, bf16[4,2,48,384]{3,2,1,0:T(8,128)(2,1)}, u32[]{:S(2)}, u32[]{:S(2)}) collective-permute-start(bf16[4,2,48,384]{3,2,1,0:T(8,128)(2,1)S(1)} %pad_maximum_fusion.3.rest_0_), channel_id=1, source_target_pairs={{0,24},{8,16},{16,8},{24,0},{1,25},{9,17},{17,9},{25,1},{2,26},{10... | collective-permute-start | bytes 884744 | tf_op jit(solution)/shard_map/ppermute | solution.py:369
  81.3 8.8 %collective-permute-start.22 = (bf16[8,768]{1,0:T(8,128)(2,1)}, bf16[8,768]{1,0:T(8,128)(2,1)S(1)}, u32[]{:S(2)}, u32[]{:S(2)}) collective-permute-start(bf16[8,768]{1,0:T(8,128)(2,1)} %get-tuple-element.68), channel_id=1, source_target_pairs={{0,1},{1,0},{2,3},{3,2},{4,5},{5,4},{6,7},{7,6},{8,9},{9,8},{10,11... | collective-permute-start | bytes 36872 | tf_op jit(solution)/shard_map/ppermute | solution.py:369
  81.6 10.4 %collective-permute-start.23 = (bf16[8,768]{1,0:T(8,128)(2,1)}, bf16[8,768]{1,0:T(8,128)(2,1)S(1)}, u32[]{:S(2)}, u32[]{:S(2)}) collective-permute-start(bf16[8,768]{1,0:T(8,128)(2,1)} %get-tuple-element.68), channel_id=1, source_target_pairs={{0,2},{1,3},{2,0},{3,1},{4,6},{5,7},{6,4},{7,5},{8,10},{9,11},{10,... | collective-permute-start | bytes 36872 | tf_op jit(solution)/shard_map/ppermute | solution.py:369
  90.0 5.7 %collective-permute-start.24 = (bf16[8,768]{1,0:T(8,128)(2,1)}, bf16[8,768]{1,0:T(8,128)(2,1)S(1)}, u32[]{:S(2)}, u32[]{:S(2)}) collective-permute-start(bf16[8,768]{1,0:T(8,128)(2,1)} %get-tuple-element.68), channel_id=1, source_target_pairs={{0,3},{1,2},{2,1},{3,0},{4,7},{5,6},{6,5},{7,4},{8,11},{9,10},{10,... | collective-permute-start | bytes 36872 | tf_op jit(solution)/shard_map/ppermute | solution.py:369
  96.5 11.1 %collective-permute-start.25 = (bf16[4,8,768]{2,1,0:T(8,128)(2,1)S(1)}, bf16[4,8,768]{2,1,0:T(8,128)(2,1)S(1)}, u32[]{:S(2)}, u32[]{:S(2)}) collective-permute-start(bf16[4,8,768]{2,1,0:T(8,128)(2,1)S(1)} %get-tuple-element.231), channel_id=1, source_target_pairs={{0,8},{8,0},{16,24},{24,16},{1,9},{9,1},{17,25},{25,17},{2,10},{10... | collective-permute-start | bytes 147464 | tf_op jit(solution)/shard_map/ppermute | solution.py:369
  101.2 6.5 %collective-permute-start.26 = (bf16[4,8,768]{2,1,0:T(8,128)(2,1)S(1)}, bf16[4,8,768]{2,1,0:T(8,128)(2,1)S(1)}, u32[]{:S(2)}, u32[]{:S(2)}) collective-permute-start(bf16[4,8,768]{2,1,0:T(8,128)(2,1)S(1)} %get-tuple-element.231), channel_id=1, source_target_pairs={{0,16},{8,24},{16,0},{24,8},{1,17},{9,25},{17,1},{25,9},{2,18},{10... | collective-permute-start | bytes 147464 | tf_op jit(solution)/shard_map/ppermute | solution.py:369
  103.6 13.1 %collective-permute-start.17 = (bf16[4,4,2,48,384]{4,3,2,1,0:T(8,128)(2,1)}, bf16[4,4,2,48,384]{4,3,2,1,0:T(8,128)(2,1)}, u32[]{:S(2)}, u32[]{:S(2)}) collective-permute-start(bf16[4,4,2,48,384]{4,3,2,1,0:T(8,128)(2,1)} %get-tuple-element.63), channel_id=1, source_target_pairs={{0,4},{4,0},{1,5},{5,1},{2,6},{6,2},{3,7},{7,3},{8,12},{12,8},{9,1... | collective-permute-start | bytes 3538952 | tf_op jit(solution)/shard_map/ppermute | solution.py:369
  107.7 7.0 %collective-permute-start.28 = (bf16[4,4,8,768]{3,2,1,0:T(8,128)(2,1)S(1)}, bf16[4,4,8,768]{3,2,1,0:T(8,128)(2,1)S(1)}, u32[]{:S(2)}, u32[]{:S(2)}) collective-permute-start(bf16[4,4,8,768]{3,2,1,0:T(8,128)(2,1)S(1)} %get-tuple-element.229), channel_id=1, source_target_pairs={{0,4},{4,0},{1,5},{5,1},{2,6},{6,2},{3,7},{7,3},{8,12},{12,8},{9,1... | collective-permute-start | bytes 589832 | tf_op jit(solution)/shard_map/ppermute | solution.py:369
  110.9 13.2 %collective-permute-start.21 = (bf16[16,48,384]{2,1,0:T(8,128)(2,1)}, bf16[16,48,384]{2,1,0:T(8,128)(2,1)}, u32[]{:S(2)}, u32[]{:S(2)}) collective-permute-start(bf16[16,48,384]{2,1,0:T(8,128)(2,1)} %get-tuple-element.66), channel_id=1, source_target_pairs={{0,4},{4,0},{1,5},{5,1},{2,6},{6,2},{3,7},{7,3},{8,12},{12,8},{9,1... | collective-permute-start | bytes 1769480 | tf_op jit(solution)/shard_map/ppermute | solution.py:369
  111.8 22.3 %all-to-all-start.2 = ((bf16[32,8,1536]{2,1,0:T(8,128)(2,1)}), bf16[32,8,1536]{2,1,0:T(8,128)(2,1)S(1)}, u32[]{:S(2)}, u32[]{:S(2)}) async-start(bf16[32,8,1536]{2,1,0:T(8,128)(2,1)} %broadcast_in_dim.78), calls=%async_computation.2 | async-start | bytes 1572864 | tf_op jit(solution)/shard_map/all_to_all | solution.py:373
  119.2 20.6 %collective-permute-start.18 = (bf16[4,2,48,384]{3,2,1,0:T(8,128)(2,1)}, bf16[4,2,48,384]{3,2,1,0:T(8,128)(2,1)}, u32[]{:S(2)}, u32[]{:S(2)}) collective-permute-start(bf16[4,2,48,384]{3,2,1,0:T(8,128)(2,1)} %get-tuple-element.216), channel_id=1, source_target_pairs={{0,8},{8,0},{16,24},{24,16},{1,9},{9,1},{17,25},{25,17},{2,10},{10... | collective-permute-start | bytes 884744 | tf_op jit(solution)/shard_map/ppermute | solution.py:369
  120.9 18.9 %collective-permute-start.19 = (bf16[4,2,48,384]{3,2,1,0:T(8,128)(2,1)}, bf16[4,2,48,384]{3,2,1,0:T(8,128)(2,1)}, u32[]{:S(2)}, u32[]{:S(2)}) collective-permute-start(bf16[4,2,48,384]{3,2,1,0:T(8,128)(2,1)} %get-tuple-element.215), channel_id=1, source_target_pairs={{0,16},{8,24},{16,0},{24,8},{1,17},{9,25},{17,1},{25,9},{2,18},{10... | collective-permute-start | bytes 884744 | tf_op jit(solution)/shard_map/ppermute | solution.py:369
  122.4 17.8 %collective-permute-start.20 = (bf16[4,2,48,384]{3,2,1,0:T(8,128)(2,1)}, bf16[4,2,48,384]{3,2,1,0:T(8,128)(2,1)}, u32[]{:S(2)}, u32[]{:S(2)}) collective-permute-start(bf16[4,2,48,384]{3,2,1,0:T(8,128)(2,1)} %get-tuple-element.214), channel_id=1, source_target_pairs={{0,24},{8,16},{16,8},{24,0},{1,25},{9,17},{17,9},{25,1},{2,26},{10... | collective-permute-start | bytes 884744 | tf_op jit(solution)/shard_map/ppermute | solution.py:369
  134.1 32.8 %all-to-all-start.3 = ((bf16[16,48,384]{2,1,0:T(8,128)(2,1)}), bf16[16,48,384]{2,1,0:T(8,128)(2,1)}, u32[]{:S(2)}, u32[]{:S(2)}) async-start(bf16[16,48,384]{2,1,0:T(8,128)(2,1)} %add_convert_fusion), calls=%async_computation.3 | async-start | bytes 1179648 | tf_op jit(solution)/shard_map/all_to_all | solution.py:373
  144.6 12.6 %collective-permute-start.29 = (bf16[256,96]{0,1:T(8,128)(2,1)S(1)}, bf16[256,96]{0,1:T(8,128)(2,1)S(1)}, u32[]{:S(2)}, u32[]{:S(2)}) collective-permute-start(bf16[256,96]{0,1:T(8,128)(2,1)S(1)} %get-tuple-element.233), channel_id=1, source_target_pairs={{0,1},{1,0},{2,3},{3,2},{4,5},{5,4},{6,7},{7,6},{8,9},{9,8},{10,11... | collective-permute-start | bytes 147464 | tf_op jit(solution)/shard_map/ppermute | solution.py:369
  146.5 15.9 %collective-permute-start.30 = (bf16[256,96]{0,1:T(8,128)(2,1)S(1)}, bf16[256,96]{0,1:T(8,128)(2,1)S(1)}, u32[]{:S(2)}, u32[]{:S(2)}) collective-permute-start(bf16[256,96]{0,1:T(8,128)(2,1)S(1)} %get-tuple-element.233), channel_id=1, source_target_pairs={{0,2},{1,3},{2,0},{3,1},{4,6},{5,7},{6,4},{7,5},{8,10},{9,11},{10,... | collective-permute-start | bytes 147464 | tf_op jit(solution)/shard_map/ppermute | solution.py:369
  148.6 13.9 %collective-permute-start.31 = (bf16[256,96]{0,1:T(8,128)(2,1)S(1)}, bf16[256,96]{0,1:T(8,128)(2,1)S(1)}, u32[]{:S(2)}, u32[]{:S(2)}) collective-permute-start(bf16[256,96]{0,1:T(8,128)(2,1)S(1)} %get-tuple-element.233), channel_id=1, source_target_pairs={{0,3},{1,2},{2,1},{3,0},{4,7},{5,6},{6,5},{7,4},{8,11},{9,10},{10,... | collective-permute-start | bytes 147464 | tf_op jit(solution)/shard_map/ppermute | solution.py:369
  150.5 12.3 %collective-permute-start.32 = (bf16[2,48,384]{2,1,0:T(8,128)(2,1)S(1)}, bf16[2,48,384]{2,1,0:T(8,128)(2,1)S(1)}, u32[]{:S(2)}, u32[]{:S(2)}) collective-permute-start(bf16[2,48,384]{2,1,0:T(8,128)(2,1)S(1)} %get-tuple-element.218), channel_id=1, source_target_pairs={{0,1},{1,0},{2,3},{3,2},{4,5},{5,4},{6,7},{7,6},{8,9},{9,8},{10,11... | collective-permute-start | bytes 221192 | tf_op jit(solution)/shard_map/ppermute | solution.py:369
  151.4 14.5 %collective-permute-start.33 = (bf16[2,48,384]{2,1,0:T(8,128)(2,1)S(1)}, bf16[2,48,384]{2,1,0:T(8,128)(2,1)S(1)}, u32[]{:S(2)}, u32[]{:S(2)}) collective-permute-start(bf16[2,48,384]{2,1,0:T(8,128)(2,1)S(1)} %get-tuple-element.220), channel_id=1, source_target_pairs={{0,2},{1,3},{2,0},{3,1},{4,6},{5,7},{6,4},{7,5},{8,10},{9,11},{10,... | collective-permute-start | bytes 221192 | tf_op jit(solution)/shard_map/ppermute | solution.py:369
  157.2 8.6 %collective-permute-start.34 = (bf16[2,48,384]{2,1,0:T(8,128)(2,1)S(1)}, bf16[2,48,384]{2,1,0:T(8,128)(2,1)S(1)}, u32[]{:S(2)}, u32[]{:S(2)}) collective-permute-start(bf16[2,48,384]{2,1,0:T(8,128)(2,1)S(1)} %get-tuple-element.219), channel_id=1, source_target_pairs={{0,3},{1,2},{2,1},{3,0},{4,7},{5,6},{6,5},{7,4},{8,11},{9,10},{10,... | collective-permute-start | bytes 221192 | tf_op jit(solution)/shard_map/ppermute | solution.py:369
  169.1 17.3 %all-to-all-start.4 = ((bf16[8,3,48,384]{3,2,1,0:T(8,128)(2,1)}), bf16[8,3,48,384]{3,2,1,0:T(8,128)(2,1)S(1)}, u32[]{:S(2)}, u32[]{:S(2)}) async-start(bf16[8,3,48,384]{3,2,1,0:T(8,128)(2,1)} %broadcast_in_dim.87), calls=%async_computation.4 | async-start | bytes 1769472 | tf_op jit(solution)/shard_map/all_to_all | solution.py:373
  (48 other events, 304.8 us)

commit v2 on v1

--- a/solution.py
+++ b/solution.py
@@ -238,7 +238,9 @@
                     target[hop, step, 1] = down_t[pl.ds(top, rows), :].astype(half)
 
 
-def attn_backward(info_ref, tok_ref, mod_ref, qkv_ref, prob_ref, attn_ref, dmid_ref, *rest):
+def attn_backward(
+    info_ref, tok_ref, mod_ref, qkv_ref, prob_ref, attn_ref, dmid_ref, two_ref, *rest
+):
     *parts, grad_ref, keep_ref, send_ref, note_ref, vec_ref, d_qkv_ref, acc_ref, weight_ref = rest
     features = tok_ref.shape[2]
     slot = pl.program_id(0)
@@ -310,7 +312,8 @@
 
     @pl.when(slot == pl.num_programs(0) - 1)
     def _():
-        note_ref[...] = vec_ref[...].astype(half)
+        note_ref[:, : 2 * features] = vec_ref[...].astype(half)
+        note_ref[:, 2 * features :] = two_ref[...]
         if keep_ref.ndim == 2:
             keep_ref[...] = acc_ref[...].astype(half)
             send_ref[...] = jnp.zeros_like(send_ref)
@@ -379,6 +382,10 @@
 
 def neighbours(values, axis):
     return [values] + [swap(values, axis, k) for k in range(1, lax.axis_size(axis))]
+
+
+def after(values, first):
+    return lax.optimization_barrier((values, first))[0]
 
 
 def order(pieces, index):
@@ -606,9 +613,7 @@
         for k in range(chips)
     ]
     by_chip = [by_chip[0]] + [swap(by_chip[k], "chip", k) for k in range(1, chips)]
-    all_two = spread(note_two, devices, ("chip", "core", "fsdp"))
-
-    token_grad, first_keep, first_send, note_three = run_kernel(
+    token_grad, first_keep, first_send, note = run_kernel(
         attn_backward,
         capacity,
         3 * work,
@@ -619,12 +624,13 @@
             per_slot(HEADS, length, length),
             slot_tok,
             slot_tok,
+            whole(8, wide),
             *first_specs,
         ],
         [
             (slot_tok, shaped(half, capacity, length, features)),
             *[(whole(*pack), shaped(half, *pack)) for pack in first_packs],
-            (whole(8, 2 * features), shaped(half, 8, 2 * features)),
+            (whole(8, 6 * features), shaped(half, 8, 6 * features)),
         ],
         [
             pltpu.VMEM((8, 2 * features), full),
@@ -633,7 +639,7 @@
             pltpu.VMEM((features, wide), half),
         ],
         info,
-        (tokens, modulation, qkv_rows, probs, attn_out, d_mid, *first_parts),
+        (tokens, modulation, qkv_rows, probs, attn_out, d_mid, note_two, *first_parts),
     )
     if not aligned:
         packed = (
@@ -645,7 +651,7 @@
     first_back = swap(first_send, "core", 1)
     first_sum = (first_keep.astype(full) + first_back.astype(full)).astype(half)
     pieces = exchange(first_sum, ("chip", "fsdp"))
-    by_chip, all_two, first_sum = lax.optimization_barrier((by_chip, all_two, first_sum))
+    by_chip = after(by_chip, first_sum)
 
     by_group = []
     for k in range(groups):
@@ -658,27 +664,15 @@
         second_sum = second_sum + swap(by_group[k], "fsdp", k).astype(full)
     second_sum = second_sum.astype(half)
 
-    note_three = jnp.stack(neighbours(note_three, "fsdp"))
-    note_three = jnp.stack(neighbours(note_three, "chip"))
-    note_three = jnp.stack(neighbours(note_three, "core"))
-    count = devices * 8
-    spot = lax.iota(jnp.int32, count)
-    line, where = spot % 8, spot // 8
-    where_group = (where % groups) ^ group
-    where_core = (where // groups % cores) ^ core
-    where_chip = (where // (groups * cores)) ^ chip
-    where = ((where_core * chips + where_chip) * groups + where_group) * 8 + line
-    moved = (where[:, None] == spot[None, :]).astype(half)
-    d_three = jnp.dot(
-        moved, note_three.reshape(count, 2 * features), preferred_element_type=full
-    ).astype(half)
-    d_two = all_two.reshape(count, wide)
+    note = jnp.stack(neighbours(note, "fsdp"))
+    note = jnp.stack(neighbours(note, "chip"))
 
     first_sum = add_up(pieces).astype(half)
     if aligned:
         third = jnp.concatenate([second_sum, first_sum[None]])
     else:
         third = jnp.concatenate([second_sum, first_sum.reshape(-1)])
+    note = after(jnp.stack(neighbours(note, "core")), third)
     third = spread(third, reps, ("chip", "core")).reshape(chips, cores, *third.shape)
     if aligned:
         up_all, down_all, first_all = third[:, :, 0], third[:, :, 1], third[:, :, 2]
@@ -694,40 +688,40 @@
     qkv_grad = first_grad[:, : 3 * features]
     out_grad = first_grad[:, 3 * features :]
 
-    label_notes = all_two[:, 6, :16].astype(jnp.int32)
+    count = devices * 8
+    line = lax.iota(jnp.int32, count) % 8
+    note = note.reshape(devices, 8, 6 * features)
+    label_notes = note[:, 6, 2 * features : 2 * features + 16].astype(jnp.int32)
     all_labels = (32 * label_notes[:, :8] + label_notes[:, 8:]).reshape(-1)
+    d_mod = note.reshape(count, 6 * features)
     all_cond = cond_table[jnp.maximum(all_labels, 0)]
     all_cond = lax.dynamic_slice_in_dim(all_cond, column, shard, 1).astype(full)
     all_live = (all_labels >= 0)[:, None]
     sigmoid_c = jax.nn.sigmoid(all_cond)
     all_active = jnp.where(all_live, all_cond * sigmoid_c, 0.0).astype(half)
     slope_c = jnp.where(all_live, sigmoid_c * (1.0 + all_cond * (1.0 - sigmoid_c)), 0.0)
-    mod_grad = jnp.concatenate([dot_tn(all_active, d_three), dot_tn(all_active, d_two)], axis=1)
-    d_act = dot_nt(d_three, mod_half[:, : 2 * features]) + dot_nt(
-        d_two, mod_half[:, 2 * features :]
-    )
+    mod_grad = dot_tn(all_active, d_mod)
+    d_act = dot_nt(d_mod, mod_half)
     picks = jnp.stack([line < capacity, line == 4, line == 5]).astype(half)
-    sum_two = dot_nn(picks, d_two)
-    sum_three = dot_nn(picks, d_three)
-    d_cond = order(neighbours((d_act * slope_c).astype(half), "fsdp"), group)
+    sums = dot_nn(picks, d_mod)
+    d_cond = neighbours((d_act * slope_c).astype(half), "fsdp")
     class_share = classes_all // groups
     class_ids = lax.iota(jnp.int32, class_share) + group * class_share
-    chosen = (class_ids[:, None] == all_labels[None, :]).astype(half)
-    table_grad = jnp.concatenate(
-        [
-            jnp.dot(chosen, d_cond[k], preferred_element_type=full)
-            for k in range(groups)
-        ],
-        axis=1,
-    )
+    by_place = all_labels.reshape(reps, groups, 8)
+    tables = []
+    for k in range(groups):
+        seen = jnp.concatenate([by_place[:, g ^ k : (g ^ k) + 1] for g in range(groups)], axis=1)
+        chosen = (class_ids[:, None] == seen.reshape(1, -1)).astype(half)
+        tables.append(dot_nn(chosen, d_cond[k]))
+    table_grad = order(tables, group).transpose(1, 0, 2).reshape(class_share, features)
+    two = 2 * features
     bias_all = jnp.concatenate(
         [
-            sum_three[0],
-            sum_two[0],
-            sum_three[1],
-            sum_two[2, :features],
-            sum_two[1],
-            sum_two[2, features : 2 * features],
+            sums[0],
+            sums[1, :two],
+            sums[2, two : two + features],
+            sums[1, two:],
+            sums[2, two + features : 2 * two],
         ]
     )
     bias_share = biases.shape[0]

time: 196 us -> 194 us (0.990)
  waiting for transfers between devices: 46.4 us -> 55 us
  starting transfers between devices: 73.4 us -> 66 us
  local copies, waits for them, and re-layouts: 20.2 us -> 16.1 us
  matrix products: 3.68 us -> 6.02 us
    ppermute x35, waiting for transfers between devices: 24.7 us -> 46.7 us  [swap(): return lax.ppermute(values, axis, [(i, i ^ step) for i in range(count)])]
    all_to_all x5 -> x4, waiting for transfers between devices: 21.7 us -> 8.26 us  [exchange(): return lax.all_to_all(pieces, axes, 0, 0, tiled=True)]
    all_to_all x5 -> x4, starting transfers between devices: 20.6 us -> 16.2 us  [exchange(): return lax.all_to_all(pieces, axes, 0, 0, tiled=True)]
    dot_general x2 -> x1, matrix products: 0.45 us -> 4.02 us  [dot_tn(): lax.dot_general(left, right, (((0,), (0,)), ((), ())), preferred_element_...]
    ppermute x35, starting transfers between devices: 52.7 us -> 49.8 us  [swap(): return lax.ppermute(values, axis, [(i, i ^ step) for i in range(count)])]
    another operation x3, other arithmetic: 0.79 us -> 3.26 us  [the longest x2 2.46 us: body(): note = after(jnp.stack(neighbours(note, 'core')), third)]
    sub x6 -> x5, other arithmetic: 7.9 us -> 5.91 us  [adamw_update(): weight - learn_rate * (mean_hat / (jnp.sqrt(square_hat) + adam_eps) + wei...]
    unnamed x90 -> x77, local copies, waits for them, and re-layouts: 6.35 us -> 4.67 us
  transfers between devices with their start and end apart: 40 -> 39, of which waited for: 12 -> 13; matrix products, arithmetic and copies ran while one was open for 15% -> 13% of each run, Pallas kernels for 4% -> 9%
where the time goes in v2:
time: 194 us; the launch traced here: 193 us
  starting transfers between devices  66 us (34%)
  waiting for transfers between devices  55 us (28%)
  Pallas kernels  29.4 us (15%)
  other arithmetic  18.5 us (10%)
  local copies, waits for them, and re-layouts  16.1 us (8%)
  matrix products  6.02 us (3%)
  between operations  2 us (1%)
    ppermute x35, starting transfers between devices, swap(): return lax.ppermute(values, axis, [(i, i ^ step) for i in range(count)])  49.8 us
    ppermute x35, waiting for transfers between devices, swap(): return lax.ppermute(values, axis, [(i, i ^ step) for i in range(count)])  46.7 us
    pallas_call x3, Pallas kernels, run_kernel(): pl.pallas_call(kernel, grid_spec=pltpu.PrefetchScalarGridSpec(num_scalar_...  29.4 us
    all_to_all x4, starting transfers between devices, exchange(): return lax.all_to_all(pieces, axes, 0, 0, tiled=True)  16.2 us
    all_to_all x4, waiting for transfers between devices, exchange(): return lax.all_to_all(pieces, axes, 0, 0, tiled=True)  8.26 us
    sub x5, other arithmetic, adamw_update(): weight - learn_rate * (mean_hat / (jnp.sqrt(square_hat) + adam_eps) + wei...  5.91 us
    unnamed x77, local copies, waits for them, and re-layouts  4.67 us
    dot_general x1, matrix products, dot_tn(): lax.dot_general(left, right, (((0,), (0,)), ((), ())), preferred_element_...  4.02 us
  transfers between devices with their start and end apart: 39, of which 13 were waited for; matrix products, arithmetic and copies ran while one was open for 13% of the time, Pallas kernels for 9%

profile of v2, /device:TPU:0, one launch (start us, length us, event | category | flops | bytes accessed | tf_op | source)
XLA Modules:
  0.0 193.1 jit_solution(840034402552939432)
XLA Ops:
  2.7 3.1 %collective-permute-start.6 = (bf16[48,1536]{1,0:T(8,128)(2,1)S(1)}, bf16[48,1536]{1,0:T(8,128)(2,1)S(1)}, u32[]{:S(2)}, u32[]{:S(2)}) collective-permute-start(bf16[48,1536]{1,0:T(8,128)(2,1)S(1)} %pad_maximum_fusion.3.rest_0_), channel_id=1, source_target_pairs={{0,1},{1,0},{2,3},{3,2},{4,5},{5,4},{6,7},{7,6},{8,9},{9,8},{10,11... | collective-permute-start | bytes 442376 | tf_op jit(solution)/shard_map/ppermute | solution.py:372
  5.8 2.6 %collective-permute-start.7 = (bf16[48,1536]{1,0:T(8,128)(2,1)S(1)}, bf16[48,1536]{1,0:T(8,128)(2,1)}, u32[]{:S(2)}, u32[]{:S(2)}) collective-permute-start(bf16[48,1536]{1,0:T(8,128)(2,1)S(1)} %pad_maximum_fusion.3.rest_0_), channel_id=1, source_target_pairs={{0,2},{1,3},{2,0},{3,1},{4,6},{5,7},{6,4},{7,5},{8,10},{9,11},{10,... | collective-permute-start | bytes 442376 | tf_op jit(solution)/shard_map/ppermute | solution.py:372
  11.1 5.1 %all-to-all-start = ((f32[4,1,1348]{2,1,0:T(1,128)}), f32[4,1,1348]{2,1,0:T(1,128)S(1)}, u32[]{:S(2)}, u32[]{:S(2)}) async-start(f32[4,1,1348]{2,1,0:T(1,128)} %broadcast_in_dim.69), calls=%async_computation | async-start | bytes 45056 | tf_op jit(solution)/shard_map/all_to_all | solution.py:376
  18.0 3.9 %collective-permute-start.2 = (bf16[2,48,384]{2,1,0:T(8,128)(2,1)S(1)}, bf16[2,48,384]{2,1,0:T(8,128)(2,1)S(1)}, u32[]{:S(2)}, u32[]{:S(2)}) collective-permute-start(bf16[2,48,384]{2,1,0:T(8,128)(2,1)S(1)} %pad_maximum_fusion.6), channel_id=1, source_target_pairs={{0,3},{1,2},{2,1},{3,0},{4,7},{5,6},{6,5},{7,4},{8,11},{9,10},{10,... | collective-permute-start | bytes 221192 | tf_op jit(solution)/shard_map/ppermute | solution.py:372
  22.5 1.9 all-to-all-done
  26.3 3.3 %all-to-all-start.1 = ((f32[4,4,2304]{2,1,0:T(4,128)}), f32[4,4,2304]{2,1,0:T(4,128)S(1)}, u32[]{:S(2)}, u32[]{:S(2)}) async-start(f32[4,4,2304]{2,1,0:T(4,128)} %reshape.270), calls=%async_computation.1 | async-start | bytes 294912 | tf_op jit(solution)/shard_map/all_to_all | solution.py:376
  29.6 2.9 %collective-permute-start.1 = (bf16[2,48,384]{2,1,0:T(8,128)(2,1)S(1)}, bf16[2,48,384]{2,1,0:T(8,128)(2,1)S(1)}, u32[]{:S(2)}, u32[]{:S(2)}) collective-permute-start(bf16[2,48,384]{2,1,0:T(8,128)(2,1)S(1)} %pad_maximum_fusion.6), channel_id=1, source_target_pairs={{0,2},{1,3},{2,0},{3,1},{4,6},{5,7},{6,4},{7,5},{8,10},{9,11},{10,... | collective-permute-start | bytes 221192 | tf_op jit(solution)/shard_map/ppermute | solution.py:372
  33.1 4.3 %collective-permute-done.1 = bf16[2,48,384]{2,1,0:T(8,128)(2,1)S(1)} collective-permute-done((bf16[2,48,384]{2,1,0:T(8,128)(2,1)S(1)}, bf16[2,48,384]{2,1,0:T(8,128)(2,1)S(1)}, u32[]{:S(2)}, u32[]{:S(2)}) %collective-permute-start.1) | collective-permute-done | bytes 73760 | tf_op jit(solution)/shard_map/ppermute | solution.py:372
  37.5 1.6 collective-permute-start.3
  42.5 7.7 %shard_map.430 = (bf16[4,256,1152]{2,1,0:T(8,128)(2,1)}, bf16[4,6,256,256]{3,2,1,0:T(8,128)(2,1)}, bf16[4,256,384]{2,1,0:T(8,128)(2,1)}, f32[4,256,384]{2,1,0:T(8,128)}) custom-call(s32[12]{0:T(128)} %concatenate.39.info_ref, bf16[4,256,384]{2,1,0:T(8,128)(2,1)} %tok_ref.5, f32[4,1,2304]{2,1,0:T(1,128)} %reshape_add_fusion.mod_ref, ...), custom_call_target="tpu_custom_call" | custom-call | flops 9663676416 | bytes 32212254 | tf_op jit(solution)/shard_map/pallas_call | solution.py:343
  50.2 5.8 %collective-permute-done.4.rest_2_ = bf16[4,2,48,384]{3,2,1,0:T(8,128)(2,1)S(1)} collective-permute-done((bf16[4,2,48,384]{3,2,1,0:T(8,128)(2,1)S(1)}, bf16[4,2,48,384]{3,2,1,0:T(8,128)(2,1)S(1)}, u32[]{:S(2)}, u32[]{:S(2)}) %collective-permute-start.4) | collective-permute-done | bytes 294944 | tf_op jit(solution)/shard_map/ppermute | solution.py:372
  59.5 12.2 %shard_map.431 = (bf16[4,256,384]{2,1,0:T(8,128)(2,1)}, f32[4,256,384]{2,1,0:T(8,128)}, bf16[4,4,2,48,384]{4,3,2,1,0:T(8,128)(2,1)}, bf16[4,4,2,48,384]{4,3,2,1,0:T(8,128)(2,1)}, bf16[8,1536]{1,0:T(8,128)(2,1)}) custom-call(s32[12]{0:T(128)} %concatenate.39.info_ref, bf16[4,256,384]{2,1,0:T(8,128)(2,1)} %tok_ref.5, bf16[4,256,384]{2,1,0:T(8,128)(2,1)} %cot_ref.1, ...), custom_call_target="tpu_custom_call" | custom-call | flops 19327352832 | bytes 64424508 | tf_op jit(solution)/shard_map/pallas_call | solution.py:343
  72.0 9.5 %shard_map.432 = (bf16[4,256,384]{2,1,0:T(8,128)(2,1)}, bf16[16,48,384]{2,1,0:T(8,128)(2,1)}, bf16[16,48,384]{2,1,0:T(8,128)(2,1)}, bf16[8,2304]{1,0:T(8,128)(2,1)}) custom-call(s32[12]{0:T(128)} %concatenate.39.info_ref, bf16[4,256,384]{2,1,0:T(8,128)(2,1)} %tok_ref.5, f32[4,1,2304]{2,1,0:T(1,128)} %reshape_add_fusion.mod_ref, ...), custom_call_target="tpu_custom_call" | custom-call | flops 14495514624 | bytes 48318384 | tf_op jit(solution)/shard_map/pallas_call | solution.py:343
  81.9 8.3 %collective-permute-start.18 = (bf16[8,2304]{1,0:T(8,128)(2,1)}, bf16[8,2304]{1,0:T(8,128)(2,1)S(1)}, u32[]{:S(2)}, u32[]{:S(2)}) collective-permute-start(bf16[8,2304]{1,0:T(8,128)(2,1)} %get-tuple-element.63), channel_id=1, source_target_pairs={{0,2},{1,3},{2,0},{3,1},{4,6},{5,7},{6,4},{7,5},{8,10},{9,11},{10,... | collective-permute-start | bytes 110600 | tf_op jit(solution)/shard_map/ppermute | solution.py:372
  90.2 2.4 %collective-permute-done.18 = bf16[8,2304]{1,0:T(8,128)(2,1)S(1)} collective-permute-done((bf16[8,2304]{1,0:T(8,128)(2,1)}, bf16[8,2304]{1,0:T(8,128)(2,1)S(1)}, u32[]{:S(2)}, u32[]{:S(2)}) %collective-permute-start.18) | collective-permute-done | bytes 36896 | tf_op jit(solution)/shard_map/ppermute | solution.py:372
  92.6 3.6 %collective-permute-done.19 = bf16[8,2304]{1,0:T(8,128)(2,1)S(1)} collective-permute-done((bf16[8,2304]{1,0:T(8,128)(2,1)}, bf16[8,2304]{1,0:T(8,128)(2,1)S(1)}, u32[]{:S(2)}, u32[]{:S(2)}) %collective-permute-start.19) | collective-permute-done | bytes 36896 | tf_op jit(solution)/shard_map/ppermute | solution.py:372
  96.9 9.1 %collective-permute-start.20 = (bf16[4,8,2304]{2,1,0:T(8,128)(2,1)S(1)}, bf16[4,8,2304]{2,1,0:T(8,128)(2,1)S(1)}, u32[]{:S(2)}, u32[]{:S(2)}) collective-permute-start(bf16[4,8,2304]{2,1,0:T(8,128)(2,1)S(1)} %get-tuple-element.172), channel_id=1, source_target_pairs={{0,8},{8,0},{16,24},{24,16},{1,9},{9,1},{17,25},{25,17},{2,10},{10... | collective-permute-start | bytes 442376 | tf_op jit(solution)/shard_map/ppermute | solution.py:372
  106.1 1.5 collective-permute-start.22
  107.6 2.8 %collective-permute-done.20 = bf16[4,8,2304]{2,1,0:T(8,128)(2,1)S(1)} collective-permute-done((bf16[4,8,2304]{2,1,0:T(8,128)(2,1)S(1)}, bf16[4,8,2304]{2,1,0:T(8,128)(2,1)S(1)}, u32[]{:S(2)}, u32[]{:S(2)}) %collective-permute-start.20) | collective-permute-done | bytes 147488 | tf_op jit(solution)/shard_map/ppermute | solution.py:372
  110.4 5.3 %collective-permute-done.21 = bf16[4,8,2304]{2,1,0:T(8,128)(2,1)S(1)} collective-permute-done((bf16[4,8,2304]{2,1,0:T(8,128)(2,1)S(1)}, bf16[4,8,2304]{2,1,0:T(8,128)(2,1)S(1)}, u32[]{:S(2)}, u32[]{:S(2)}) %collective-permute-start.21) | collective-permute-done | bytes 147488 | tf_op jit(solution)/shard_map/ppermute | solution.py:372
  117.8 3.6 %all-to-all-start.2 = ((bf16[16,48,384]{2,1,0:T(8,128)(2,1)}), bf16[16,48,384]{2,1,0:T(8,128)(2,1)S(1)}, u32[]{:S(2)}, u32[]{:S(2)}) async-start(bf16[16,48,384]{2,1,0:T(8,128)(2,1)} %add_convert_fusion), calls=%async_computation.2 | async-start | bytes 1179648 | tf_op jit(solution)/shard_map/all_to_all | solution.py:376
  121.5 2.4 %fusion.12 = (bf16[4,2,48,384]{3,2,1,0:T(8,128)(2,1)}, bf16[4,2,48,384]{3,2,1,0:T(8,128)(2,1)}, bf16[4,2,48,384]{3,2,1,0:T(8,128)(2,1)}, bf16[4,2,48,384]{3,2,1,0:T(8,128)(2,1)}) fusion(bf16[4,4,2,48,384]{4,3,2,1,0:T(8,128)(2,1)} %collective-permute-done.24, bf16[4,4,2,48,384]{4,3,2,1,0:T(8,128)(2,1)S(1)} %copy-done.3), kind=kLoop, calls=%fused_computation.40 | loop fusion | flops 2359296 | bytes 3538944 | tf_op jit(solution)/shard_map/convert_element_type | solution.py:612
  123.9 1.8 collective-permute-start.25
  127.4 9.4 %collective-permute-done.25 = bf16[4,2,48,384]{3,2,1,0:T(8,128)(2,1)S(1)} collective-permute-done((bf16[4,2,48,384]{3,2,1,0:T(8,128)(2,1)}, bf16[4,2,48,384]{3,2,1,0:T(8,128)(2,1)S(1)}, u32[]{:S(2)}, u32[]{:S(2)}) %collective-permute-start.25) | collective-permute-done | bytes 294944 | tf_op jit(solution)/shard_map/ppermute | solution.py:372
  136.8 7.9 %collective-permute-done.27 = bf16[4,2,48,384]{3,2,1,0:T(8,128)(2,1)S(1)} collective-permute-done((bf16[4,2,48,384]{3,2,1,0:T(8,128)(2,1)}, bf16[4,2,48,384]{3,2,1,0:T(8,128)(2,1)S(1)}, u32[]{:S(2)}, u32[]{:S(2)}) %collective-permute-start.27) | collective-permute-done | bytes 294944 | tf_op jit(solution)/shard_map/ppermute | solution.py:372
  145.9 2.2 %collective-permute-start.29 = (bf16[2,48,384]{2,1,0:T(8,128)(2,1)S(1)}, bf16[2,48,384]{2,1,0:T(8,128)(2,1)S(1)}, u32[]{:S(2)}, u32[]{:S(2)}) collective-permute-start(bf16[2,48,384]{2,1,0:T(8,128)(2,1)S(1)} %get-tuple-element.159), channel_id=1, source_target_pairs={{0,1},{1,0},{2,3},{3,2},{4,5},{5,4},{6,7},{7,6},{8,9},{9,8},{10,11... | collective-permute-start | bytes 221192 | tf_op jit(solution)/shard_map/ppermute | solution.py:372
  151.9 4.4 %collective-permute-done.30 = bf16[2,48,384]{2,1,0:T(8,128)(2,1)S(1)} collective-permute-done((bf16[2,48,384]{2,1,0:T(8,128)(2,1)S(1)}, bf16[2,48,384]{2,1,0:T(8,128)(2,1)S(1)}, u32[]{:S(2)}, u32[]{:S(2)}) %collective-permute-start.30) | collective-permute-done | bytes 73760 | tf_op jit(solution)/shard_map/ppermute | solution.py:372
  162.8 1.9 collective-permute-start.34
  165.6 4.2 %all-to-all-start.3 = ((bf16[8,3,48,384]{3,2,1,0:T(8,128)(2,1)}), bf16[8,3,48,384]{3,2,1,0:T(8,128)(2,1)}, u32[]{:S(2)}, u32[]{:S(2)}) async-start(bf16[8,3,48,384]{3,2,1,0:T(8,128)(2,1)} %broadcast_in_dim.81), calls=%async_computation.3 | async-start | bytes 1769472 | tf_op jit(solution)/shard_map/all_to_all | solution.py:376
  170.0 4.0 %multiply_subtract_fusion = (f32[96,2304]{1,0:T(8,128)}, f32[96,2304]{1,0:T(8,128)}, f32[96,2304]{1,0:T(8,128)}, f32[96,2304]{1,0:T(8,128)}) fusion(f32[96,2304]{1,0:T(8,128)S(1)} %copy-done.1, f32[96,2304]{1,0:T(8,128)} %param.34, f32[96,2304]{1,0:T(8,128)} %param.40, bf16[256,2304]{1,0:T(8,128)(2,1)S(1)} %bitcast.113, bf16[256,96]{0,1:T(8,128)(2,1)S(1)} %copy.69, ...), kind=kOutput, calls=%fused_computation.16 | convolution fusion | flops 116736000 | bytes 7422208 | tf_op jit(solution)/shard_map/dot_general | solution.py:37
  177.1 6.4 %all-to-all-done.3 = bf16[8,3,48,384]{3,2,1,0:T(8,128)(2,1)} async-done(((bf16[8,3,48,384]{3,2,1,0:T(8,128)(2,1)}), bf16[8,3,48,384]{3,2,1,0:T(8,128)(2,1)}, u32[]{:S(2)}, u32[]{:S(2)}) %all-to-all-start.3) | async-done | bytes 884768 | tf_op jit(solution)/shard_map/all_to_all | solution.py:376
  191.6 1.6 multiply_subtract_fusion.1
  (208 shorter events, 44.5 us)
Async XLA Ops:
  2.7 36.3 %collective-permute-start.6 = (bf16[48,1536]{1,0:T(8,128)(2,1)S(1)}, bf16[48,1536]{1,0:T(8,128)(2,1)S(1)}, u32[]{:S(2)}, u32[]{:S(2)}) collective-permute-start(bf16[48,1536]{1,0:T(8,128)(2,1)S(1)} %pad_maximum_fusion.3.rest_0_), channel_id=1, source_target_pairs={{0,1},{1,0},{2,3},{3,2},{4,5},{5,4},{6,7},{7,6},{8,9},{9,8},{10,11... | collective-permute-start | bytes 442376 | tf_op jit(solution)/shard_map/ppermute | solution.py:372
  5.8 33.2 %collective-permute-start.7 = (bf16[48,1536]{1,0:T(8,128)(2,1)S(1)}, bf16[48,1536]{1,0:T(8,128)(2,1)}, u32[]{:S(2)}, u32[]{:S(2)}) collective-permute-start(bf16[48,1536]{1,0:T(8,128)(2,1)S(1)} %pad_maximum_fusion.3.rest_0_), channel_id=1, source_target_pairs={{0,2},{1,3},{2,0},{3,1},{4,6},{5,7},{6,4},{7,5},{8,10},{9,11},{10,... | collective-permute-start | bytes 442376 | tf_op jit(solution)/shard_map/ppermute | solution.py:372
  8.4 31.2 %collective-permute-start.8 = (bf16[48,1536]{1,0:T(8,128)(2,1)S(1)}, bf16[48,1536]{1,0:T(8,128)(2,1)}, u32[]{:S(2)}, u32[]{:S(2)}) collective-permute-start(bf16[48,1536]{1,0:T(8,128)(2,1)S(1)} %pad_maximum_fusion.3.rest_0_), channel_id=1, source_target_pairs={{0,3},{1,2},{2,1},{3,0},{4,7},{5,6},{6,5},{7,4},{8,11},{9,10},{10,... | collective-permute-start | bytes 442376 | tf_op jit(solution)/shard_map/ppermute | solution.py:372
  11.1 13.3 %all-to-all-start = ((f32[4,1,1348]{2,1,0:T(1,128)}), f32[4,1,1348]{2,1,0:T(1,128)S(1)}, u32[]{:S(2)}, u32[]{:S(2)}) async-start(f32[4,1,1348]{2,1,0:T(1,128)} %broadcast_in_dim.69), calls=%async_computation | async-start | bytes 45056 | tf_op jit(solution)/shard_map/all_to_all | solution.py:376
  18.0 11.6 %collective-permute-start.2 = (bf16[2,48,384]{2,1,0:T(8,128)(2,1)S(1)}, bf16[2,48,384]{2,1,0:T(8,128)(2,1)S(1)}, u32[]{:S(2)}, u32[]{:S(2)}) collective-permute-start(bf16[2,48,384]{2,1,0:T(8,128)(2,1)S(1)} %pad_maximum_fusion.6), channel_id=1, source_target_pairs={{0,3},{1,2},{2,1},{3,0},{4,7},{5,6},{6,5},{7,4},{8,11},{9,10},{10,... | collective-permute-start | bytes 221192 | tf_op jit(solution)/shard_map/ppermute | solution.py:372
  21.9 11.2 %collective-permute-start = (bf16[2,48,384]{2,1,0:T(8,128)(2,1)S(1)}, bf16[2,48,384]{2,1,0:T(8,128)(2,1)S(1)}, u32[]{:S(2)}, u32[]{:S(2)}) collective-permute-start(bf16[2,48,384]{2,1,0:T(8,128)(2,1)S(1)} %pad_maximum_fusion.6), channel_id=1, source_target_pairs={{0,1},{1,0},{2,3},{3,2},{4,5},{5,4},{6,7},{7,6},{8,9},{9,8},{10,11... | collective-permute-start | bytes 221192 | tf_op jit(solution)/shard_map/ppermute | solution.py:372
  26.3 13.4 %all-to-all-start.1 = ((f32[4,4,2304]{2,1,0:T(4,128)}), f32[4,4,2304]{2,1,0:T(4,128)S(1)}, u32[]{:S(2)}, u32[]{:S(2)}) async-start(f32[4,4,2304]{2,1,0:T(4,128)} %reshape.270), calls=%async_computation.1 | async-start | bytes 294912 | tf_op jit(solution)/shard_map/all_to_all | solution.py:376
  29.6 7.8 %collective-permute-start.1 = (bf16[2,48,384]{2,1,0:T(8,128)(2,1)S(1)}, bf16[2,48,384]{2,1,0:T(8,128)(2,1)S(1)}, u32[]{:S(2)}, u32[]{:S(2)}) collective-permute-start(bf16[2,48,384]{2,1,0:T(8,128)(2,1)S(1)} %pad_maximum_fusion.6), channel_id=1, source_target_pairs={{0,2},{1,3},{2,0},{3,1},{4,6},{5,7},{6,4},{7,5},{8,10},{9,11},{10,... | collective-permute-start | bytes 221192 | tf_op jit(solution)/shard_map/ppermute | solution.py:372
  33.1 7.2 %collective-permute-start.9 = (bf16[48,1536]{1,0:T(8,128)(2,1)S(1)}, bf16[48,1536]{1,0:T(8,128)(2,1)}, u32[]{:S(2)}, u32[]{:S(2)}) collective-permute-start(bf16[48,1536]{1,0:T(8,128)(2,1)S(1)} %pad_maximum_fusion.3.rest_0_), channel_id=1, source_target_pairs={{0,4},{4,0},{1,5},{5,1},{2,6},{6,2},{3,7},{7,3},{8,12},{12,8},{9,1... | collective-permute-start | bytes 442376 | tf_op jit(solution)/shard_map/ppermute | solution.py:372
  37.5 12.7 %collective-permute-start.3 = (bf16[4,2,48,384]{3,2,1,0:T(8,128)(2,1)S(1)}, bf16[4,2,48,384]{3,2,1,0:T(8,128)(2,1)S(1)}, u32[]{:S(2)}, u32[]{:S(2)}) collective-permute-start(bf16[4,2,48,384]{3,2,1,0:T(8,128)(2,1)S(1)} %pad_maximum_fusion.2.rest_0_), channel_id=1, source_target_pairs={{0,8},{8,0},{16,24},{24,16},{1,9},{9,1},{17,25},{25,17},{2,10},{10... | collective-permute-start | bytes 884744 | tf_op jit(solution)/shard_map/ppermute | solution.py:372
  40.3 15.7 %collective-permute-start.4 = (bf16[4,2,48,384]{3,2,1,0:T(8,128)(2,1)S(1)}, bf16[4,2,48,384]{3,2,1,0:T(8,128)(2,1)S(1)}, u32[]{:S(2)}, u32[]{:S(2)}) collective-permute-start(bf16[4,2,48,384]{3,2,1,0:T(8,128)(2,1)S(1)} %pad_maximum_fusion.2.rest_0_), channel_id=1, source_target_pairs={{0,16},{8,24},{16,0},{24,8},{1,17},{9,25},{17,1},{25,9},{2,18},{10... | collective-permute-start | bytes 884744 | tf_op jit(solution)/shard_map/ppermute | solution.py:372
  41.9 14.1 %collective-permute-start.5 = (bf16[4,2,48,384]{3,2,1,0:T(8,128)(2,1)S(1)}, bf16[4,2,48,384]{3,2,1,0:T(8,128)(2,1)S(1)}, u32[]{:S(2)}, u32[]{:S(2)}) collective-permute-start(bf16[4,2,48,384]{3,2,1,0:T(8,128)(2,1)S(1)} %pad_maximum_fusion.2.rest_0_), channel_id=1, source_target_pairs={{0,24},{8,16},{16,8},{24,0},{1,25},{9,17},{17,9},{25,1},{2,26},{10... | collective-permute-start | bytes 884744 | tf_op jit(solution)/shard_map/ppermute | solution.py:372
  71.8 49.7 %collective-permute-start.24 = (bf16[4,4,2,48,384]{4,3,2,1,0:T(8,128)(2,1)}, bf16[4,4,2,48,384]{4,3,2,1,0:T(8,128)(2,1)}, u32[]{:S(2)}, u32[]{:S(2)}) collective-permute-start(bf16[4,4,2,48,384]{4,3,2,1,0:T(8,128)(2,1)} %get-tuple-element.65), channel_id=1, source_target_pairs={{0,4},{4,0},{1,5},{5,1},{2,6},{6,2},{3,7},{7,3},{8,12},{12,8},{9,1... | collective-permute-start | bytes 3538952 | tf_op jit(solution)/shard_map/ppermute | solution.py:372
  81.5 8.7 %collective-permute-start.17 = (bf16[8,2304]{1,0:T(8,128)(2,1)}, bf16[8,2304]{1,0:T(8,128)(2,1)S(1)}, u32[]{:S(2)}, u32[]{:S(2)}) collective-permute-start(bf16[8,2304]{1,0:T(8,128)(2,1)} %get-tuple-element.63), channel_id=1, source_target_pairs={{0,1},{1,0},{2,3},{3,2},{4,5},{5,4},{6,7},{7,6},{8,9},{9,8},{10,11... | collective-permute-start | bytes 110600 | tf_op jit(solution)/shard_map/ppermute | solution.py:372
  81.9 10.7 %collective-permute-start.18 = (bf16[8,2304]{1,0:T(8,128)(2,1)}, bf16[8,2304]{1,0:T(8,128)(2,1)S(1)}, u32[]{:S(2)}, u32[]{:S(2)}) collective-permute-start(bf16[8,2304]{1,0:T(8,128)(2,1)} %get-tuple-element.63), channel_id=1, source_target_pairs={{0,2},{1,3},{2,0},{3,1},{4,6},{5,7},{6,4},{7,5},{8,10},{9,11},{10,... | collective-permute-start | bytes 110600 | tf_op jit(solution)/shard_map/ppermute | solution.py:372
  90.2 6.0 %collective-permute-start.19 = (bf16[8,2304]{1,0:T(8,128)(2,1)}, bf16[8,2304]{1,0:T(8,128)(2,1)S(1)}, u32[]{:S(2)}, u32[]{:S(2)}) collective-permute-start(bf16[8,2304]{1,0:T(8,128)(2,1)} %get-tuple-element.63), channel_id=1, source_target_pairs={{0,3},{1,2},{2,1},{3,0},{4,7},{5,6},{6,5},{7,4},{8,11},{9,10},{10,... | collective-permute-start | bytes 110600 | tf_op jit(solution)/shard_map/ppermute | solution.py:372
  90.2 26.7 %collective-permute-start.28 = (bf16[16,48,384]{2,1,0:T(8,128)(2,1)}, bf16[16,48,384]{2,1,0:T(8,128)(2,1)S(1)}, u32[]{:S(2)}, u32[]{:S(2)}) collective-permute-start(bf16[16,48,384]{2,1,0:T(8,128)(2,1)} %get-tuple-element.67), channel_id=1, source_target_pairs={{0,4},{4,0},{1,5},{5,1},{2,6},{6,2},{3,7},{7,3},{8,12},{12,8},{9,1... | collective-permute-start | bytes 1769480 | tf_op jit(solution)/shard_map/ppermute | solution.py:372
  96.9 13.5 %collective-permute-start.20 = (bf16[4,8,2304]{2,1,0:T(8,128)(2,1)S(1)}, bf16[4,8,2304]{2,1,0:T(8,128)(2,1)S(1)}, u32[]{:S(2)}, u32[]{:S(2)}) collective-permute-start(bf16[4,8,2304]{2,1,0:T(8,128)(2,1)S(1)} %get-tuple-element.172), channel_id=1, source_target_pairs={{0,8},{8,0},{16,24},{24,16},{1,9},{9,1},{17,25},{25,17},{2,10},{10... | collective-permute-start | bytes 442376 | tf_op jit(solution)/shard_map/ppermute | solution.py:372
  106.1 9.7 %collective-permute-start.21 = (bf16[4,8,2304]{2,1,0:T(8,128)(2,1)S(1)}, bf16[4,8,2304]{2,1,0:T(8,128)(2,1)S(1)}, u32[]{:S(2)}, u32[]{:S(2)}) collective-permute-start(bf16[4,8,2304]{2,1,0:T(8,128)(2,1)S(1)} %get-tuple-element.172), channel_id=1, source_target_pairs={{0,16},{8,24},{16,0},{24,8},{1,17},{9,25},{17,1},{25,9},{2,18},{10... | collective-permute-start | bytes 442376 | tf_op jit(solution)/shard_map/ppermute | solution.py:372
  106.1 9.7 %collective-permute-start.22 = (bf16[4,8,2304]{2,1,0:T(8,128)(2,1)S(1)}, bf16[4,8,2304]{2,1,0:T(8,128)(2,1)S(1)}, u32[]{:S(2)}, u32[]{:S(2)}) collective-permute-start(bf16[4,8,2304]{2,1,0:T(8,128)(2,1)S(1)} %get-tuple-element.172), channel_id=1, source_target_pairs={{0,24},{8,16},{16,8},{24,0},{1,25},{9,17},{17,9},{25,1},{2,26},{10... | collective-permute-start | bytes 442376 | tf_op jit(solution)/shard_map/ppermute | solution.py:372
  116.9 33.6 %collective-permute-start.23 = (bf16[4,4,8,2304]{3,2,1,0:T(8,128)(2,1)}, bf16[4,4,8,2304]{3,2,1,0:T(8,128)(2,1)}, u32[]{:S(2)}, u32[]{:S(2)}) collective-permute-start(bf16[4,4,8,2304]{3,2,1,0:T(8,128)(2,1)} %get-tuple-element.166), channel_id=1, source_target_pairs={{0,4},{4,0},{1,5},{5,1},{2,6},{6,2},{3,7},{7,3},{8,12},{12,8},{9,1... | collective-permute-start | bytes 1769480 | tf_op jit(solution)/shard_map/ppermute | solution.py:372
  117.8 39.5 %all-to-all-start.2 = ((bf16[16,48,384]{2,1,0:T(8,128)(2,1)}), bf16[16,48,384]{2,1,0:T(8,128)(2,1)S(1)}, u32[]{:S(2)}, u32[]{:S(2)}) async-start(bf16[16,48,384]{2,1,0:T(8,128)(2,1)} %add_convert_fusion), calls=%async_computation.2 | async-start | bytes 1179648 | tf_op jit(solution)/shard_map/all_to_all | solution.py:376
  123.9 12.9 %collective-permute-start.25 = (bf16[4,2,48,384]{3,2,1,0:T(8,128)(2,1)}, bf16[4,2,48,384]{3,2,1,0:T(8,128)(2,1)S(1)}, u32[]{:S(2)}, u32[]{:S(2)}) collective-permute-start(bf16[4,2,48,384]{3,2,1,0:T(8,128)(2,1)} %get-tuple-element.157), channel_id=1, source_target_pairs={{0,8},{8,0},{16,24},{24,16},{1,9},{9,1},{17,25},{25,17},{2,10},{10... | collective-permute-start | bytes 884744 | tf_op jit(solution)/shard_map/ppermute | solution.py:372
  125.7 11.1 %collective-permute-start.26 = (bf16[4,2,48,384]{3,2,1,0:T(8,128)(2,1)}, bf16[4,2,48,384]{3,2,1,0:T(8,128)(2,1)S(1)}, u32[]{:S(2)}, u32[]{:S(2)}) collective-permute-start(bf16[4,2,48,384]{3,2,1,0:T(8,128)(2,1)} %get-tuple-element.156), channel_id=1, source_target_pairs={{0,16},{8,24},{16,0},{24,8},{1,17},{9,25},{17,1},{25,9},{2,18},{10... | collective-permute-start | bytes 884744 | tf_op jit(solution)/shard_map/ppermute | solution.py:372
  127.2 17.5 %collective-permute-start.27 = (bf16[4,2,48,384]{3,2,1,0:T(8,128)(2,1)}, bf16[4,2,48,384]{3,2,1,0:T(8,128)(2,1)S(1)}, u32[]{:S(2)}, u32[]{:S(2)}) collective-permute-start(bf16[4,2,48,384]{3,2,1,0:T(8,128)(2,1)} %get-tuple-element.155), channel_id=1, source_target_pairs={{0,24},{8,16},{16,8},{24,0},{1,25},{9,17},{17,9},{25,1},{2,26},{10... | collective-permute-start | bytes 884744 | tf_op jit(solution)/shard_map/ppermute | solution.py:372
  145.9 6.0 %collective-permute-start.29 = (bf16[2,48,384]{2,1,0:T(8,128)(2,1)S(1)}, bf16[2,48,384]{2,1,0:T(8,128)(2,1)S(1)}, u32[]{:S(2)}, u32[]{:S(2)}) collective-permute-start(bf16[2,48,384]{2,1,0:T(8,128)(2,1)S(1)} %get-tuple-element.159), channel_id=1, source_target_pairs={{0,1},{1,0},{2,3},{3,2},{4,5},{5,4},{6,7},{7,6},{8,9},{9,8},{10,11... | collective-permute-start | bytes 221192 | tf_op jit(solution)/shard_map/ppermute | solution.py:372
  148.0 8.3 %collective-permute-start.30 = (bf16[2,48,384]{2,1,0:T(8,128)(2,1)S(1)}, bf16[2,48,384]{2,1,0:T(8,128)(2,1)S(1)}, u32[]{:S(2)}, u32[]{:S(2)}) collective-permute-start(bf16[2,48,384]{2,1,0:T(8,128)(2,1)S(1)} %get-tuple-element.161), channel_id=1, source_target_pairs={{0,2},{1,3},{2,0},{3,1},{4,6},{5,7},{6,4},{7,5},{8,10},{9,11},{10,... | collective-permute-start | bytes 221192 | tf_op jit(solution)/shard_map/ppermute | solution.py:372
  149.5 6.8 %collective-permute-start.31 = (bf16[2,48,384]{2,1,0:T(8,128)(2,1)S(1)}, bf16[2,48,384]{2,1,0:T(8,128)(2,1)S(1)}, u32[]{:S(2)}, u32[]{:S(2)}) collective-permute-start(bf16[2,48,384]{2,1,0:T(8,128)(2,1)S(1)} %get-tuple-element.160), channel_id=1, source_target_pairs={{0,3},{1,2},{2,1},{3,0},{4,7},{5,6},{6,5},{7,4},{8,11},{9,10},{10,... | collective-permute-start | bytes 221192 | tf_op jit(solution)/shard_map/ppermute | solution.py:372
  160.2 15.2 %collective-permute-start.32 = (bf16[256,96]{0,1:T(8,128)(2,1)S(1)}, bf16[256,96]{0,1:T(8,128)(2,1)S(1)}, u32[]{:S(2)}, u32[]{:S(2)}) collective-permute-start(bf16[256,96]{0,1:T(8,128)(2,1)S(1)} %fusion.4), channel_id=1, source_target_pairs={{0,1},{1,0},{2,3},{3,2},{4,5},{5,4},{6,7},{7,6},{8,9},{9,8},{10,11... | collective-permute-start | bytes 147464 | tf_op jit(solution)/shard_map/ppermute | solution.py:372
  161.6 14.1 %collective-permute-start.33 = (bf16[256,96]{0,1:T(8,128)(2,1)S(1)}, bf16[256,96]{0,1:T(8,128)(2,1)S(1)}, u32[]{:S(2)}, u32[]{:S(2)}) collective-permute-start(bf16[256,96]{0,1:T(8,128)(2,1)S(1)} %fusion.4), channel_id=1, source_target_pairs={{0,2},{1,3},{2,0},{3,1},{4,6},{5,7},{6,4},{7,5},{8,10},{9,11},{10,... | collective-permute-start | bytes 147464 | tf_op jit(solution)/shard_map/ppermute | solution.py:372
  162.8 13.2 %collective-permute-start.34 = (bf16[256,96]{0,1:T(8,128)(2,1)S(1)}, bf16[256,96]{0,1:T(8,128)(2,1)S(1)}, u32[]{:S(2)}, u32[]{:S(2)}) collective-permute-start(bf16[256,96]{0,1:T(8,128)(2,1)S(1)} %fusion.4), channel_id=1, source_target_pairs={{0,3},{1,2},{2,1},{3,0},{4,7},{5,6},{6,5},{7,4},{8,11},{9,10},{10,... | collective-permute-start | bytes 147464 | tf_op jit(solution)/shard_map/ppermute | solution.py:372
  165.6 17.9 %all-to-all-start.3 = ((bf16[8,3,48,384]{3,2,1,0:T(8,128)(2,1)}), bf16[8,3,48,384]{3,2,1,0:T(8,128)(2,1)}, u32[]{:S(2)}, u32[]{:S(2)}) async-start(bf16[8,3,48,384]{3,2,1,0:T(8,128)(2,1)} %broadcast_in_dim.81), calls=%async_computation.3 | async-start | bytes 1769472 | tf_op jit(solution)/shard_map/all_to_all | solution.py:376
  (41 other events, 254.9 us)

commit v3 on v2

--- a/solution.py
+++ b/solution.py
@@ -265,7 +265,7 @@
         h_one = (normed_one * (1.0 + scale_one) + shift_one).astype(half)
         d_mid = dmid_ref[0]
         d_proj = (d_mid * gate_one).astype(half)
-        acc_ref[:, 3 * features :] += dot_tn(attn_ref[0], d_proj)
+        acc_ref[3] += dot_tn(attn_ref[0], d_proj)
         d_attn = dot_nt(d_proj, weight_ref[:, 3 * features :]).astype(half)
         masks = head_masks()
         width = 2 * HD
@@ -301,7 +301,8 @@
             vec_ref[4:5, features + low : features + low + width] += jnp.sum(
                 sums[2], axis=0, keepdims=True
             )
-        acc_ref[:, : 3 * features] += dot_tn(h_one, d_qkv_ref[...])
+        for part in range(3):
+            acc_ref[part] += dot_tn(h_one, d_qkv_ref[:, part * features : (part + 1) * features])
         d_h_one = dot_nt(d_qkv_ref[...], weight_ref[:, : 3 * features])
         d_scale_one = jnp.sum(d_h_one * normed_one, axis=0, keepdims=True)
         d_shift_one = jnp.sum(d_h_one, axis=0, keepdims=True)
@@ -315,20 +316,19 @@
         note_ref[:, : 2 * features] = vec_ref[...].astype(half)
         note_ref[:, 2 * features :] = two_ref[...]
         if keep_ref.ndim == 2:
-            keep_ref[...] = acc_ref[...].astype(half)
+            for part in range(4):
+                keep_ref[:, part * features : (part + 1) * features] = acc_ref[part].astype(half)
             send_ref[...] = jnp.zeros_like(send_ref)
             return
-        pieces, rows, cols = keep_ref.shape
-        chips = acc_ref.shape[1] // cols
-        groups = pieces // chips
+        chips, groups, rows, _ = keep_ref.shape
         for flip, target in enumerate((keep_ref, send_ref)):
             core = info_ref[1] ^ flip
-            for chip in range(chips):
-                for group in range(groups):
+            for hop in range(chips):
+                for step in range(groups):
+                    chip = info_ref[2] ^ hop
+                    group = info_ref[3] ^ step
                     top = pl.multiple_of((group * 2 + core) * rows, rows)
-                    target[chip * groups + group] = acc_ref[
-                        pl.ds(top, rows), chip * cols : (chip + 1) * cols
-                    ].astype(half)
+                    target[hop, step] = acc_ref[chip, pl.ds(top, rows), :].astype(half)
 
 
 def per_slot(*extent):
@@ -393,6 +393,25 @@
     for step, piece in enumerate(pieces):
         buffer = lax.dynamic_update_index_in_dim(buffer, piece, index ^ step, 0)
     return buffer
+
+
+def pair_sum(keep, back):
+    return [
+        (keep[k].astype(full) + back[k].astype(full)).astype(half) for k in range(keep.shape[0])
+    ]
+
+
+def group_sum(by_chip, groups):
+    pieces = []
+    for k in range(groups):
+        total = by_chip[0][k].astype(full)
+        for part in by_chip[1:]:
+            total = total + part[k].astype(full)
+        pieces.append(total.astype(half))
+    total = pieces[0].astype(full)
+    for k in range(1, groups):
+        total = total + swap(pieces[k], "fsdp", k).astype(full)
+    return total.astype(half)
 
 
 def choose(values, index):
@@ -445,6 +464,10 @@
     down_rows = wide // (devices)
     aligned = rows % 16 == 0 and cols % 128 == 0 and (rows, cols) == (down_rows, features)
 
+    def relative(packed):
+        packed = packed[:, lax.iota(jnp.int32, chips) ^ chip]
+        return packed[:, :, lax.iota(jnp.int32, groups) ^ group]
+
     live = lax.iota(jnp.int32, capacity) < counts[0]
     own_labels = jnp.where(live, labels, -1)
     head = jnp.concatenate([own_labels.astype(full), lax.reduce_precision(biases, 8, 7)])
@@ -556,7 +579,7 @@
     second_specs = [whole(*part.shape) for part in second_parts]
 
     if aligned:
-        first_packs = [(chips * groups, rows, cols)] * 2
+        first_packs = [(chips, groups, rows, cols)] * 2
         second_packs = [(chips, groups, 2, rows, cols)] * 2
     else:
         first_packs = [(features, wide), (8, 128)]
@@ -604,14 +627,10 @@
             .reshape(cores, chips, groups, -1)
         )
         packed = jnp.concatenate([up_part, down_part], axis=-1)
-        packed = packed[:, lax.iota(jnp.int32, chips) ^ chip]
-        packed = packed[:, :, lax.iota(jnp.int32, groups) ^ group]
+        packed = relative(packed)
         second_keep, second_send = choose(packed, core), choose(packed, 1 - core)
     second_back = swap(second_send, "core", 1)
-    by_chip = [
-        (second_keep[k].astype(full) + second_back[k].astype(full)).astype(half)
-        for k in range(chips)
-    ]
+    by_chip = pair_sum(second_keep, second_back)
     by_chip = [by_chip[0]] + [swap(by_chip[k], "chip", k) for k in range(1, chips)]
     token_grad, first_keep, first_send, note = run_kernel(
         attn_backward,
@@ -635,44 +654,33 @@
         [
             pltpu.VMEM((8, 2 * features), full),
             pltpu.VMEM((length, 3 * features), half),
-            pltpu.VMEM((features, wide), full),
+            pltpu.VMEM((4, features, features), full),
             pltpu.VMEM((features, wide), half),
         ],
         info,
         (tokens, modulation, qkv_rows, probs, attn_out, d_mid, note_two, *first_parts),
     )
     if not aligned:
-        packed = (
-            first_keep.reshape(groups, cores, rows, chips, cols)
-            .transpose(1, 3, 0, 2, 4)
-            .reshape(cores, chips * groups, rows, cols)
+        packed = relative(
+            first_keep.reshape(groups, cores, rows, chips, cols).transpose(1, 3, 0, 2, 4)
         )
         first_keep, first_send = choose(packed, core), choose(packed, 1 - core)
     first_back = swap(first_send, "core", 1)
-    first_sum = (first_keep.astype(full) + first_back.astype(full)).astype(half)
-    pieces = exchange(first_sum, ("chip", "fsdp"))
-    by_chip = after(by_chip, first_sum)
-
-    by_group = []
-    for k in range(groups):
-        total = by_chip[0][k].astype(full)
-        for part in by_chip[1:]:
-            total = total + part[k].astype(full)
-        by_group.append(total.astype(half))
-    second_sum = by_group[0].astype(full)
-    for k in range(1, groups):
-        second_sum = second_sum + swap(by_group[k], "fsdp", k).astype(full)
-    second_sum = second_sum.astype(half)
-
-    note = jnp.stack(neighbours(note, "fsdp"))
-    note = jnp.stack(neighbours(note, "chip"))
-
-    first_sum = add_up(pieces).astype(half)
+    first_chip = pair_sum(first_keep, first_back)
+    by_chip = after(by_chip, first_chip)
+    first_chip = [first_chip[0]] + [swap(first_chip[k], "chip", k) for k in range(1, chips)]
+    second_sum = group_sum(by_chip, groups)
+    first_sum = group_sum(first_chip, groups)
+
+    note = jnp.stack(after(neighbours(note, "fsdp"), first_chip[0]))
+    note = neighbours(note, "chip")
+
     if aligned:
         third = jnp.concatenate([second_sum, first_sum[None]])
     else:
         third = jnp.concatenate([second_sum, first_sum.reshape(-1)])
-    note = after(jnp.stack(neighbours(note, "core")), third)
+    note = jnp.stack(after(note, third))
+    note = jnp.stack(neighbours(note, "core"))
     third = spread(third, reps, ("chip", "core")).reshape(chips, cores, *third.shape)
     if aligned:
         up_all, down_all, first_all = third[:, :, 0], third[:, :, 1], third[:, :, 2]

time: 194 us -> 171 us (0.88)
  waiting for transfers between devices: 55 us -> 33.6 us
  starting transfers between devices: 66 us -> 70.8 us
  other arithmetic: 18.5 us -> 14 us
    ppermute x35 -> x41, waiting for transfers between devices: 46.7 us -> 31.7 us  [swap(): return lax.ppermute(values, axis, [(i, i ^ step) for i in range(count)])]
    ppermute x35 -> x41, starting transfers between devices: 49.8 us -> 58.1 us  [swap(): return lax.ppermute(values, axis, [(i, i ^ step) for i in range(count)])]
    all_to_all x4 -> x3, waiting for transfers between devices: 8.26 us -> 1.88 us  [exchange(): return lax.all_to_all(pieces, axes, 0, 0, tiled=True)]
    all_to_all x4 -> x3, starting transfers between devices: 16.2 us -> 12.7 us  [exchange(): return lax.all_to_all(pieces, axes, 0, 0, tiled=True)]
    another operation x3, other arithmetic: 3.26 us -> 1.29 us  [the longest x2 1.27 us: body(): note = jnp.stack(neighbours(note, 'core'))]
    unnamed x77 -> x73, local copies, waits for them, and re-layouts: 4.67 us -> 4.51 us
  transfers between devices with their start and end apart: 39 -> 44, of which waited for: 13 -> 13; matrix products, arithmetic and copies ran while one was open for 13% -> 13% of each run, Pallas kernels for 9% -> 10%
where the time goes in v3:
time: 171 us; the launch traced here: 170 us
  starting transfers between devices  70.8 us (41%)
  waiting for transfers between devices  33.6 us (20%)
  Pallas kernels  29.5 us (17%)
  local copies, waits for them, and re-layouts  15.9 us (9%)
  other arithmetic  14 us (8%)
  matrix products  4.6 us (3%)
  between operations  2.04 us (1%)
    ppermute x41, starting transfers between devices, swap(): return lax.ppermute(values, axis, [(i, i ^ step) for i in range(count)])  58.1 us
    ppermute x41, waiting for transfers between devices, swap(): return lax.ppermute(values, axis, [(i, i ^ step) for i in range(count)])  31.7 us
    pallas_call x3, Pallas kernels, run_kernel(): pl.pallas_call(kernel, grid_spec=pltpu.PrefetchScalarGridSpec(num_scalar_...  29.5 us
    all_to_all x3, starting transfers between devices, exchange(): return lax.all_to_all(pieces, axes, 0, 0, tiled=True)  12.7 us
    sub x5, other arithmetic, adamw_update(): weight - learn_rate * (mean_hat / (jnp.sqrt(square_hat) + adam_eps) + wei...  5.91 us
    unnamed x73, local copies, waits for them, and re-layouts  4.51 us
  transfers between devices with their start and end apart: 44, of which 13 were waited for; matrix products, arithmetic and copies ran while one was open for 13% of the time, Pallas kernels for 10%

profile of v3, /device:TPU:0, one launch (start us, length us, event | category | flops | bytes accessed | tf_op | source)
XLA Modules:
  0.0 170.4 jit_solution(8330570880325988505)
XLA Ops:
  2.7 3.1 %collective-permute-start.6 = (bf16[48,1536]{1,0:T(8,128)(2,1)S(1)}, bf16[48,1536]{1,0:T(8,128)(2,1)S(1)}, u32[]{:S(2)}, u32[]{:S(2)}) collective-permute-start(bf16[48,1536]{1,0:T(8,128)(2,1)S(1)} %pad_maximum_fusion.3.rest_0_), channel_id=1, source_target_pairs={{0,1},{1,0},{2,3},{3,2},{4,5},{5,4},{6,7},{7,6},{8,9},{9,8},{10,11... | collective-permute-start | bytes 442376 | tf_op jit(solution)/shard_map/ppermute | solution.py:372
  5.8 2.6 %collective-permute-start.7 = (bf16[48,1536]{1,0:T(8,128)(2,1)S(1)}, bf16[48,1536]{1,0:T(8,128)(2,1)}, u32[]{:S(2)}, u32[]{:S(2)}) collective-permute-start(bf16[48,1536]{1,0:T(8,128)(2,1)S(1)} %pad_maximum_fusion.3.rest_0_), channel_id=1, source_target_pairs={{0,2},{1,3},{2,0},{3,1},{4,6},{5,7},{6,4},{7,5},{8,10},{9,11},{10,... | collective-permute-start | bytes 442376 | tf_op jit(solution)/shard_map/ppermute | solution.py:372
  11.1 5.1 %all-to-all-start = ((f32[4,1,1348]{2,1,0:T(1,128)}), f32[4,1,1348]{2,1,0:T(1,128)S(1)}, u32[]{:S(2)}, u32[]{:S(2)}) async-start(f32[4,1,1348]{2,1,0:T(1,128)} %broadcast_in_dim.69), calls=%async_computation | async-start | bytes 45056 | tf_op jit(solution)/shard_map/all_to_all | solution.py:376
  18.0 3.9 %collective-permute-start.2 = (bf16[2,48,384]{2,1,0:T(8,128)(2,1)S(1)}, bf16[2,48,384]{2,1,0:T(8,128)(2,1)S(1)}, u32[]{:S(2)}, u32[]{:S(2)}) collective-permute-start(bf16[2,48,384]{2,1,0:T(8,128)(2,1)S(1)} %pad_maximum_fusion.6), channel_id=1, source_target_pairs={{0,3},{1,2},{2,1},{3,0},{4,7},{5,6},{6,5},{7,4},{8,11},{9,10},{10,... | collective-permute-start | bytes 221192 | tf_op jit(solution)/shard_map/ppermute | solution.py:372
  22.5 1.9 %all-to-all-done = f32[4,1,1348]{2,1,0:T(1,128)S(1)} async-done(((f32[4,1,1348]{2,1,0:T(1,128)}), f32[4,1,1348]{2,1,0:T(1,128)S(1)}, u32[]{:S(2)}, u32[]{:S(2)}) %all-to-all-start) | async-done | bytes 21600 | tf_op jit(solution)/shard_map/all_to_all | solution.py:376
  26.3 3.3 %all-to-all-start.1 = ((f32[4,4,2304]{2,1,0:T(4,128)}), f32[4,4,2304]{2,1,0:T(4,128)S(1)}, u32[]{:S(2)}, u32[]{:S(2)}) async-start(f32[4,4,2304]{2,1,0:T(4,128)} %reshape.330), calls=%async_computation.1 | async-start | bytes 294912 | tf_op jit(solution)/shard_map/all_to_all | solution.py:376
  29.6 2.9 %collective-permute-start.1 = (bf16[2,48,384]{2,1,0:T(8,128)(2,1)S(1)}, bf16[2,48,384]{2,1,0:T(8,128)(2,1)S(1)}, u32[]{:S(2)}, u32[]{:S(2)}) collective-permute-start(bf16[2,48,384]{2,1,0:T(8,128)(2,1)S(1)} %pad_maximum_fusion.6), channel_id=1, source_target_pairs={{0,2},{1,3},{2,0},{3,1},{4,6},{5,7},{6,4},{7,5},{8,10},{9,11},{10,... | collective-permute-start | bytes 221192 | tf_op jit(solution)/shard_map/ppermute | solution.py:372
  33.1 4.3 %collective-permute-done.1 = bf16[2,48,384]{2,1,0:T(8,128)(2,1)S(1)} collective-permute-done((bf16[2,48,384]{2,1,0:T(8,128)(2,1)S(1)}, bf16[2,48,384]{2,1,0:T(8,128)(2,1)S(1)}, u32[]{:S(2)}, u32[]{:S(2)}) %collective-permute-start.1) | collective-permute-done | bytes 73760 | tf_op jit(solution)/shard_map/ppermute | solution.py:372
  37.5 1.6 collective-permute-start.3
  40.3 1.5 collective-permute-start.4
  42.5 7.7 %shard_map.430 = (bf16[4,256,1152]{2,1,0:T(8,128)(2,1)}, bf16[4,6,256,256]{3,2,1,0:T(8,128)(2,1)}, bf16[4,256,384]{2,1,0:T(8,128)(2,1)}, f32[4,256,384]{2,1,0:T(8,128)}) custom-call(s32[12]{0:T(128)} %concatenate.39.info_ref, bf16[4,256,384]{2,1,0:T(8,128)(2,1)} %tok_ref.5, f32[4,1,2304]{2,1,0:T(1,128)} %reshape_add_fusion.mod_ref, ...), custom_call_target="tpu_custom_call" | custom-call | flops 9663676416 | bytes 32212254 | tf_op jit(solution)/shard_map/pallas_call | solution.py:343
  50.2 5.8 %collective-permute-done.4.rest_2_ = bf16[4,2,48,384]{3,2,1,0:T(8,128)(2,1)S(1)} collective-permute-done((bf16[4,2,48,384]{3,2,1,0:T(8,128)(2,1)S(1)}, bf16[4,2,48,384]{3,2,1,0:T(8,128)(2,1)S(1)}, u32[]{:S(2)}, u32[]{:S(2)}) %collective-permute-start.4) | collective-permute-done | bytes 294944 | tf_op jit(solution)/shard_map/ppermute | solution.py:372
  59.5 12.2 %shard_map.431 = (bf16[4,256,384]{2,1,0:T(8,128)(2,1)}, f32[4,256,384]{2,1,0:T(8,128)}, bf16[4,4,2,48,384]{4,3,2,1,0:T(8,128)(2,1)}, bf16[4,4,2,48,384]{4,3,2,1,0:T(8,128)(2,1)}, bf16[8,1536]{1,0:T(8,128)(2,1)}) custom-call(s32[12]{0:T(128)} %concatenate.39.info_ref, bf16[4,256,384]{2,1,0:T(8,128)(2,1)} %tok_ref.5, bf16[4,256,384]{2,1,0:T(8,128)(2,1)} %cot_ref.1, ...), custom_call_target="tpu_custom_call" | custom-call | flops 19327352832 | bytes 64424508 | tf_op jit(solution)/shard_map/pallas_call | solution.py:343
  71.9 9.6 %shard_map.432 = (bf16[4,256,384]{2,1,0:T(8,128)(2,1)}, bf16[4,4,48,384]{3,2,1,0:T(8,128)(2,1)}, bf16[4,4,48,384]{3,2,1,0:T(8,128)(2,1)}, bf16[8,2304]{1,0:T(8,128)(2,1)}) custom-call(s32[12]{0:T(128)} %concatenate.39.info_ref, bf16[4,256,384]{2,1,0:T(8,128)(2,1)} %tok_ref.5, f32[4,1,2304]{2,1,0:T(1,128)} %reshape_add_fusion.mod_ref, ...), custom_call_target="tpu_custom_call" | custom-call | flops 14495514624 | bytes 48318384 | tf_op jit(solution)/shard_map/pallas_call | solution.py:343
  82.3 8.1 %collective-permute-start.18 = (bf16[8,2304]{1,0:T(8,128)(2,1)}, bf16[8,2304]{1,0:T(8,128)(2,1)S(1)}, u32[]{:S(2)}, u32[]{:S(2)}) collective-permute-start(bf16[8,2304]{1,0:T(8,128)(2,1)} %get-tuple-element.73), channel_id=1, source_target_pairs={{0,2},{1,3},{2,0},{3,1},{4,6},{5,7},{6,4},{7,5},{8,10},{9,11},{10,... | collective-permute-start | bytes 110600 | tf_op jit(solution)/shard_map/ppermute | solution.py:372
  91.7 12.0 %collective-permute-start.31 = (bf16[4,48,384]{2,1,0:T(8,128)(2,1)S(1)}, bf16[4,48,384]{2,1,0:T(8,128)(2,1)S(1)}, u32[]{:S(2)}, u32[]{:S(2)}) collective-permute-start(bf16[4,48,384]{2,1,0:T(8,128)(2,1)S(1)} %get-tuple-element.176), channel_id=1, source_target_pairs={{0,8},{8,0},{16,24},{24,16},{1,9},{9,1},{17,25},{25,17},{2,10},{10... | collective-permute-start | bytes 442376 | tf_op jit(solution)/shard_map/ppermute | solution.py:372
  103.6 1.5 collective-permute-start.33
  105.2 1.5 fusion.12
  106.7 3.1 %collective-permute-start.25 = (bf16[4,2,48,384]{3,2,1,0:T(8,128)(2,1)S(1)}, bf16[4,2,48,384]{3,2,1,0:T(8,128)(2,1)S(1)}, u32[]{:S(2)}, u32[]{:S(2)}) collective-permute-start(bf16[4,2,48,384]{3,2,1,0:T(8,128)(2,1)S(1)} %get-tuple-element.171), channel_id=1, source_target_pairs={{0,8},{8,0},{16,24},{24,16},{1,9},{9,1},{17,25},{25,17},{2,10},{10... | collective-permute-start | bytes 884744 | tf_op jit(solution)/shard_map/ppermute | solution.py:372
  109.9 1.5 collective-permute-start.27
  113.5 4.4 %collective-permute-done.25 = bf16[4,2,48,384]{3,2,1,0:T(8,128)(2,1)S(1)} collective-permute-done((bf16[4,2,48,384]{3,2,1,0:T(8,128)(2,1)S(1)}, bf16[4,2,48,384]{3,2,1,0:T(8,128)(2,1)S(1)}, u32[]{:S(2)}, u32[]{:S(2)}) %collective-permute-start.25) | collective-permute-done | bytes 294944 | tf_op jit(solution)/shard_map/ppermute | solution.py:372
  118.7 7.3 %collective-permute-done.26 = bf16[4,2,48,384]{3,2,1,0:T(8,128)(2,1)S(1)} collective-permute-done((bf16[4,2,48,384]{3,2,1,0:T(8,128)(2,1)S(1)}, bf16[4,2,48,384]{3,2,1,0:T(8,128)(2,1)S(1)}, u32[]{:S(2)}, u32[]{:S(2)}) %collective-permute-start.26) | collective-permute-done | bytes 294944 | tf_op jit(solution)/shard_map/ppermute | solution.py:372
  127.0 2.0 %collective-permute-start.36 = (bf16[48,384]{1,0:T(8,128)(2,1)S(1)}, bf16[48,384]{1,0:T(8,128)(2,1)S(1)}, u32[]{:S(2)}, u32[]{:S(2)}) collective-permute-start(bf16[48,384]{1,0:T(8,128)(2,1)S(1)} %get-tuple-element.186), channel_id=1, source_target_pairs={{0,3},{1,2},{2,1},{3,0},{4,7},{5,6},{6,5},{7,4},{8,11},{9,10},{10,... | collective-permute-start | bytes 110600 | tf_op jit(solution)/shard_map/ppermute | solution.py:372
  129.8 2.4 %collective-permute-done.35 = bf16[48,384]{1,0:T(8,128)(2,1)S(1)} collective-permute-done((bf16[48,384]{1,0:T(8,128)(2,1)S(1)}, bf16[48,384]{1,0:T(8,128)(2,1)S(1)}, u32[]{:S(2)}, u32[]{:S(2)}) %collective-permute-start.35) | collective-permute-done | bytes 36896 | tf_op jit(solution)/shard_map/ppermute | solution.py:372
  133.2 1.7 collective-permute-start.30
  135.0 1.8 %collective-permute-start.23 = (bf16[4,8,2304]{2,1,0:T(8,128)(2,1)S(1)}, bf16[4,8,2304]{2,1,0:T(8,128)(2,1)S(1)}, u32[]{:S(2)}, u32[]{:S(2)}) collective-permute-start(bf16[4,8,2304]{2,1,0:T(8,128)(2,1)S(1)} %pad_maximum_fusion.4), channel_id=1, source_target_pairs={{0,24},{8,16},{16,8},{24,0},{1,25},{9,17},{17,9},{25,1},{2,26},{10... | collective-permute-start | bytes 442376 | tf_op jit(solution)/shard_map/ppermute | solution.py:372
  137.4 2.1 %collective-permute-done.30 = bf16[2,48,384]{2,1,0:T(8,128)(2,1)S(1)} collective-permute-done((bf16[2,48,384]{2,1,0:T(8,128)(2,1)S(1)}, bf16[2,48,384]{2,1,0:T(8,128)(2,1)S(1)}, u32[]{:S(2)}, u32[]{:S(2)}) %collective-permute-start.30) | collective-permute-done | bytes 73760 | tf_op jit(solution)/shard_map/ppermute | solution.py:372
  142.3 4.2 %all-to-all-start.2 = ((bf16[8,3,48,384]{3,2,1,0:T(8,128)(2,1)}), bf16[8,3,48,384]{3,2,1,0:T(8,128)(2,1)}, u32[]{:S(2)}, u32[]{:S(2)}) async-start(bf16[8,3,48,384]{3,2,1,0:T(8,128)(2,1)} %broadcast_in_dim.81), calls=%async_computation.2 | async-start | bytes 1769472 | tf_op jit(solution)/shard_map/all_to_all | solution.py:376
  151.2 2.0 %collective-permute-start.39 = (bf16[256,96]{0,1:T(8,128)(2,1)S(1)}, bf16[256,96]{0,1:T(8,128)(2,1)S(1)}, u32[]{:S(2)}, u32[]{:S(2)}) collective-permute-start(bf16[256,96]{0,1:T(8,128)(2,1)S(1)} %fusion.4), channel_id=1, source_target_pairs={{0,2},{1,3},{2,0},{3,1},{4,6},{5,7},{6,4},{7,5},{8,10},{9,11},{10,... | collective-permute-start | bytes 147464 | tf_op jit(solution)/shard_map/ppermute | solution.py:372
  153.2 1.7 collective-permute-start.40
  155.0 2.6 %multiply_subtract_fusion = (f32[96,2304]{1,0:T(8,128)}, f32[96,2304]{1,0:T(8,128)}, f32[96,2304]{1,0:T(8,128)}, f32[96,2304]{1,0:T(8,128)}) fusion(f32[96,2304]{1,0:T(8,128)S(1)} %copy-done.1, f32[96,2304]{1,0:T(8,128)S(1)} %copy-done.4, f32[96,2304]{1,0:T(8,128)S(1)} %copy-done.5, bf16[256,2304]{1,0:T(8,128)(2,1)S(1)} %bitcast.153, ...), kind=kOutput, calls=%fused_computation.15 | convolution fusion | flops 116736000 | bytes 7422208 | tf_op jit(solution)/shard_map/dot_general | solution.py:37
  168.8 1.6 multiply_subtract_fusion.1
  (215 shorter events, 41.5 us)
Async XLA Ops:
  2.7 36.3 %collective-permute-start.6 = (bf16[48,1536]{1,0:T(8,128)(2,1)S(1)}, bf16[48,1536]{1,0:T(8,128)(2,1)S(1)}, u32[]{:S(2)}, u32[]{:S(2)}) collective-permute-start(bf16[48,1536]{1,0:T(8,128)(2,1)S(1)} %pad_maximum_fusion.3.rest_0_), channel_id=1, source_target_pairs={{0,1},{1,0},{2,3},{3,2},{4,5},{5,4},{6,7},{7,6},{8,9},{9,8},{10,11... | collective-permute-start | bytes 442376 | tf_op jit(solution)/shard_map/ppermute | solution.py:372
  5.8 33.2 %collective-permute-start.7 = (bf16[48,1536]{1,0:T(8,128)(2,1)S(1)}, bf16[48,1536]{1,0:T(8,128)(2,1)}, u32[]{:S(2)}, u32[]{:S(2)}) collective-permute-start(bf16[48,1536]{1,0:T(8,128)(2,1)S(1)} %pad_maximum_fusion.3.rest_0_), channel_id=1, source_target_pairs={{0,2},{1,3},{2,0},{3,1},{4,6},{5,7},{6,4},{7,5},{8,10},{9,11},{10,... | collective-permute-start | bytes 442376 | tf_op jit(solution)/shard_map/ppermute | solution.py:372
  8.4 31.2 %collective-permute-start.8 = (bf16[48,1536]{1,0:T(8,128)(2,1)S(1)}, bf16[48,1536]{1,0:T(8,128)(2,1)}, u32[]{:S(2)}, u32[]{:S(2)}) collective-permute-start(bf16[48,1536]{1,0:T(8,128)(2,1)S(1)} %pad_maximum_fusion.3.rest_0_), channel_id=1, source_target_pairs={{0,3},{1,2},{2,1},{3,0},{4,7},{5,6},{6,5},{7,4},{8,11},{9,10},{10,... | collective-permute-start | bytes 442376 | tf_op jit(solution)/shard_map/ppermute | solution.py:372
  11.1 13.3 %all-to-all-start = ((f32[4,1,1348]{2,1,0:T(1,128)}), f32[4,1,1348]{2,1,0:T(1,128)S(1)}, u32[]{:S(2)}, u32[]{:S(2)}) async-start(f32[4,1,1348]{2,1,0:T(1,128)} %broadcast_in_dim.69), calls=%async_computation | async-start | bytes 45056 | tf_op jit(solution)/shard_map/all_to_all | solution.py:376
  18.0 11.6 %collective-permute-start.2 = (bf16[2,48,384]{2,1,0:T(8,128)(2,1)S(1)}, bf16[2,48,384]{2,1,0:T(8,128)(2,1)S(1)}, u32[]{:S(2)}, u32[]{:S(2)}) collective-permute-start(bf16[2,48,384]{2,1,0:T(8,128)(2,1)S(1)} %pad_maximum_fusion.6), channel_id=1, source_target_pairs={{0,3},{1,2},{2,1},{3,0},{4,7},{5,6},{6,5},{7,4},{8,11},{9,10},{10,... | collective-permute-start | bytes 221192 | tf_op jit(solution)/shard_map/ppermute | solution.py:372
  21.9 11.2 %collective-permute-start = (bf16[2,48,384]{2,1,0:T(8,128)(2,1)S(1)}, bf16[2,48,384]{2,1,0:T(8,128)(2,1)S(1)}, u32[]{:S(2)}, u32[]{:S(2)}) collective-permute-start(bf16[2,48,384]{2,1,0:T(8,128)(2,1)S(1)} %pad_maximum_fusion.6), channel_id=1, source_target_pairs={{0,1},{1,0},{2,3},{3,2},{4,5},{5,4},{6,7},{7,6},{8,9},{9,8},{10,11... | collective-permute-start | bytes 221192 | tf_op jit(solution)/shard_map/ppermute | solution.py:372
  26.3 13.4 %all-to-all-start.1 = ((f32[4,4,2304]{2,1,0:T(4,128)}), f32[4,4,2304]{2,1,0:T(4,128)S(1)}, u32[]{:S(2)}, u32[]{:S(2)}) async-start(f32[4,4,2304]{2,1,0:T(4,128)} %reshape.330), calls=%async_computation.1 | async-start | bytes 294912 | tf_op jit(solution)/shard_map/all_to_all | solution.py:376
  29.6 7.8 %collective-permute-start.1 = (bf16[2,48,384]{2,1,0:T(8,128)(2,1)S(1)}, bf16[2,48,384]{2,1,0:T(8,128)(2,1)S(1)}, u32[]{:S(2)}, u32[]{:S(2)}) collective-permute-start(bf16[2,48,384]{2,1,0:T(8,128)(2,1)S(1)} %pad_maximum_fusion.6), channel_id=1, source_target_pairs={{0,2},{1,3},{2,0},{3,1},{4,6},{5,7},{6,4},{7,5},{8,10},{9,11},{10,... | collective-permute-start | bytes 221192 | tf_op jit(solution)/shard_map/ppermute | solution.py:372
  33.1 7.2 %collective-permute-start.9 = (bf16[48,1536]{1,0:T(8,128)(2,1)S(1)}, bf16[48,1536]{1,0:T(8,128)(2,1)S(1)}, u32[]{:S(2)}, u32[]{:S(2)}) collective-permute-start(bf16[48,1536]{1,0:T(8,128)(2,1)S(1)} %pad_maximum_fusion.3.rest_0_), channel_id=1, source_target_pairs={{0,4},{4,0},{1,5},{5,1},{2,6},{6,2},{3,7},{7,3},{8,12},{12,8},{9,1... | collective-permute-start | bytes 442376 | tf_op jit(solution)/shard_map/ppermute | solution.py:372
  37.5 12.7 %collective-permute-start.3 = (bf16[4,2,48,384]{3,2,1,0:T(8,128)(2,1)S(1)}, bf16[4,2,48,384]{3,2,1,0:T(8,128)(2,1)S(1)}, u32[]{:S(2)}, u32[]{:S(2)}) collective-permute-start(bf16[4,2,48,384]{3,2,1,0:T(8,128)(2,1)S(1)} %pad_maximum_fusion.2.rest_0_), channel_id=1, source_target_pairs={{0,8},{8,0},{16,24},{24,16},{1,9},{9,1},{17,25},{25,17},{2,10},{10... | collective-permute-start | bytes 884744 | tf_op jit(solution)/shard_map/ppermute | solution.py:372
  40.3 15.7 %collective-permute-start.4 = (bf16[4,2,48,384]{3,2,1,0:T(8,128)(2,1)S(1)}, bf16[4,2,48,384]{3,2,1,0:T(8,128)(2,1)S(1)}, u32[]{:S(2)}, u32[]{:S(2)}) collective-permute-start(bf16[4,2,48,384]{3,2,1,0:T(8,128)(2,1)S(1)} %pad_maximum_fusion.2.rest_0_), channel_id=1, source_target_pairs={{0,16},{8,24},{16,0},{24,8},{1,17},{9,25},{17,1},{25,9},{2,18},{10... | collective-permute-start | bytes 884744 | tf_op jit(solution)/shard_map/ppermute | solution.py:372
  41.9 14.1 %collective-permute-start.5 = (bf16[4,2,48,384]{3,2,1,0:T(8,128)(2,1)S(1)}, bf16[4,2,48,384]{3,2,1,0:T(8,128)(2,1)S(1)}, u32[]{:S(2)}, u32[]{:S(2)}) collective-permute-start(bf16[4,2,48,384]{3,2,1,0:T(8,128)(2,1)S(1)} %pad_maximum_fusion.2.rest_0_), channel_id=1, source_target_pairs={{0,24},{8,16},{16,8},{24,0},{1,25},{9,17},{17,9},{25,1},{2,26},{10... | collective-permute-start | bytes 884744 | tf_op jit(solution)/shard_map/ppermute | solution.py:372
  71.7 33.4 %collective-permute-start.24 = (bf16[4,4,2,48,384]{4,3,2,1,0:T(8,128)(2,1)}, bf16[4,4,2,48,384]{4,3,2,1,0:T(8,128)(2,1)}, u32[]{:S(2)}, u32[]{:S(2)}) collective-permute-start(bf16[4,4,2,48,384]{4,3,2,1,0:T(8,128)(2,1)} %get-tuple-element.78), channel_id=1, source_target_pairs={{0,4},{4,0},{1,5},{5,1},{2,6},{6,2},{3,7},{7,3},{8,12},{12,8},{9,1... | collective-permute-start | bytes 3538952 | tf_op jit(solution)/shard_map/ppermute | solution.py:372
  81.6 8.8 %collective-permute-start.20 = (bf16[4,4,48,384]{3,2,1,0:T(8,128)(2,1)}, bf16[4,4,48,384]{3,2,1,0:T(8,128)(2,1)S(1)}, u32[]{:S(2)}, u32[]{:S(2)}) collective-permute-start(bf16[4,4,48,384]{3,2,1,0:T(8,128)(2,1)} %get-tuple-element.72), channel_id=1, source_target_pairs={{0,4},{4,0},{1,5},{5,1},{2,6},{6,2},{3,7},{7,3},{8,12},{12,8},{9,1... | collective-permute-start | bytes 1769480 | tf_op jit(solution)/shard_map/ppermute | solution.py:372
  82.0 21.6 %collective-permute-start.17 = (bf16[8,2304]{1,0:T(8,128)(2,1)}, bf16[8,2304]{1,0:T(8,128)(2,1)S(1)}, u32[]{:S(2)}, u32[]{:S(2)}) collective-permute-start(bf16[8,2304]{1,0:T(8,128)(2,1)} %get-tuple-element.73), channel_id=1, source_target_pairs={{0,1},{1,0},{2,3},{3,2},{4,5},{5,4},{6,7},{7,6},{8,9},{9,8},{10,11... | collective-permute-start | bytes 110600 | tf_op jit(solution)/shard_map/ppermute | solution.py:372
  82.3 21.3 %collective-permute-start.18 = (bf16[8,2304]{1,0:T(8,128)(2,1)}, bf16[8,2304]{1,0:T(8,128)(2,1)S(1)}, u32[]{:S(2)}, u32[]{:S(2)}) collective-permute-start(bf16[8,2304]{1,0:T(8,128)(2,1)} %get-tuple-element.73), channel_id=1, source_target_pairs={{0,2},{1,3},{2,0},{3,1},{4,6},{5,7},{6,4},{7,5},{8,10},{9,11},{10,... | collective-permute-start | bytes 110600 | tf_op jit(solution)/shard_map/ppermute | solution.py:372
  90.4 14.8 %collective-permute-start.19 = (bf16[8,2304]{1,0:T(8,128)(2,1)}, bf16[8,2304]{1,0:T(8,128)(2,1)S(1)}, u32[]{:S(2)}, u32[]{:S(2)}) collective-permute-start(bf16[8,2304]{1,0:T(8,128)(2,1)} %get-tuple-element.73), channel_id=1, source_target_pairs={{0,3},{1,2},{2,1},{3,0},{4,7},{5,6},{6,5},{7,4},{8,11},{9,10},{10,... | collective-permute-start | bytes 110600 | tf_op jit(solution)/shard_map/ppermute | solution.py:372
  91.7 18.2 %collective-permute-start.31 = (bf16[4,48,384]{2,1,0:T(8,128)(2,1)S(1)}, bf16[4,48,384]{2,1,0:T(8,128)(2,1)S(1)}, u32[]{:S(2)}, u32[]{:S(2)}) collective-permute-start(bf16[4,48,384]{2,1,0:T(8,128)(2,1)S(1)} %get-tuple-element.176), channel_id=1, source_target_pairs={{0,8},{8,0},{16,24},{24,16},{1,9},{9,1},{17,25},{25,17},{2,10},{10... | collective-permute-start | bytes 442376 | tf_op jit(solution)/shard_map/ppermute | solution.py:372
  103.6 9.2 %collective-permute-start.32 = (bf16[4,48,384]{2,1,0:T(8,128)(2,1)S(1)}, bf16[4,48,384]{2,1,0:T(8,128)(2,1)S(1)}, u32[]{:S(2)}, u32[]{:S(2)}) collective-permute-start(bf16[4,48,384]{2,1,0:T(8,128)(2,1)S(1)} %get-tuple-element.178), channel_id=1, source_target_pairs={{0,16},{8,24},{16,0},{24,8},{1,17},{9,25},{17,1},{25,9},{2,18},{10... | collective-permute-start | bytes 442376 | tf_op jit(solution)/shard_map/ppermute | solution.py:372
  103.6 9.8 %collective-permute-start.33 = (bf16[4,48,384]{2,1,0:T(8,128)(2,1)S(1)}, bf16[4,48,384]{2,1,0:T(8,128)(2,1)S(1)}, u32[]{:S(2)}, u32[]{:S(2)}) collective-permute-start(bf16[4,48,384]{2,1,0:T(8,128)(2,1)S(1)} %get-tuple-element.177), channel_id=1, source_target_pairs={{0,24},{8,16},{16,8},{24,0},{1,25},{9,17},{17,9},{25,1},{2,26},{10... | collective-permute-start | bytes 442376 | tf_op jit(solution)/shard_map/ppermute | solution.py:372
  106.7 11.2 %collective-permute-start.25 = (bf16[4,2,48,384]{3,2,1,0:T(8,128)(2,1)S(1)}, bf16[4,2,48,384]{3,2,1,0:T(8,128)(2,1)S(1)}, u32[]{:S(2)}, u32[]{:S(2)}) collective-permute-start(bf16[4,2,48,384]{3,2,1,0:T(8,128)(2,1)S(1)} %get-tuple-element.171), channel_id=1, source_target_pairs={{0,8},{8,0},{16,24},{24,16},{1,9},{9,1},{17,25},{25,17},{2,10},{10... | collective-permute-start | bytes 884744 | tf_op jit(solution)/shard_map/ppermute | solution.py:372
  109.8 16.1 %collective-permute-start.26 = (bf16[4,2,48,384]{3,2,1,0:T(8,128)(2,1)S(1)}, bf16[4,2,48,384]{3,2,1,0:T(8,128)(2,1)S(1)}, u32[]{:S(2)}, u32[]{:S(2)}) collective-permute-start(bf16[4,2,48,384]{3,2,1,0:T(8,128)(2,1)S(1)} %get-tuple-element.170), channel_id=1, source_target_pairs={{0,16},{8,24},{16,0},{24,8},{1,17},{9,25},{17,1},{25,9},{2,18},{10... | collective-permute-start | bytes 884744 | tf_op jit(solution)/shard_map/ppermute | solution.py:372
  109.9 17.2 %collective-permute-start.27 = (bf16[4,2,48,384]{3,2,1,0:T(8,128)(2,1)S(1)}, bf16[4,2,48,384]{3,2,1,0:T(8,128)(2,1)S(1)}, u32[]{:S(2)}, u32[]{:S(2)}) collective-permute-start(bf16[4,2,48,384]{3,2,1,0:T(8,128)(2,1)S(1)} %get-tuple-element.169), channel_id=1, source_target_pairs={{0,24},{8,16},{16,8},{24,0},{1,25},{9,17},{17,9},{25,1},{2,26},{10... | collective-permute-start | bytes 884744 | tf_op jit(solution)/shard_map/ppermute | solution.py:372
  112.8 26.8 %collective-permute-start.21 = (bf16[4,8,2304]{2,1,0:T(8,128)(2,1)S(1)}, bf16[4,8,2304]{2,1,0:T(8,128)(2,1)S(1)}, u32[]{:S(2)}, u32[]{:S(2)}) collective-permute-start(bf16[4,8,2304]{2,1,0:T(8,128)(2,1)S(1)} %pad_maximum_fusion.4), channel_id=1, source_target_pairs={{0,8},{8,0},{16,24},{24,16},{1,9},{9,1},{17,25},{25,17},{2,10},{10... | collective-permute-start | bytes 442376 | tf_op jit(solution)/shard_map/ppermute | solution.py:372
  113.5 26.1 %collective-permute-start.22 = (bf16[4,8,2304]{2,1,0:T(8,128)(2,1)S(1)}, bf16[4,8,2304]{2,1,0:T(8,128)(2,1)S(1)}, u32[]{:S(2)}, u32[]{:S(2)}) collective-permute-start(bf16[4,8,2304]{2,1,0:T(8,128)(2,1)S(1)} %pad_maximum_fusion.4), channel_id=1, source_target_pairs={{0,16},{8,24},{16,0},{24,8},{1,17},{9,25},{17,1},{25,9},{2,18},{10... | collective-permute-start | bytes 442376 | tf_op jit(solution)/shard_map/ppermute | solution.py:372
  118.0 11.2 %collective-permute-start.34 = (bf16[48,384]{1,0:T(8,128)(2,1)S(1)}, bf16[48,384]{1,0:T(8,128)(2,1)S(1)}, u32[]{:S(2)}, u32[]{:S(2)}) collective-permute-start(bf16[48,384]{1,0:T(8,128)(2,1)S(1)} %get-tuple-element.185), channel_id=1, source_target_pairs={{0,1},{1,0},{2,3},{3,2},{4,5},{5,4},{6,7},{7,6},{8,9},{9,8},{10,11... | collective-permute-start | bytes 110600 | tf_op jit(solution)/shard_map/ppermute | solution.py:372
  127.0 6.2 %collective-permute-start.36 = (bf16[48,384]{1,0:T(8,128)(2,1)S(1)}, bf16[48,384]{1,0:T(8,128)(2,1)S(1)}, u32[]{:S(2)}, u32[]{:S(2)}) collective-permute-start(bf16[48,384]{1,0:T(8,128)(2,1)S(1)} %get-tuple-element.186), channel_id=1, source_target_pairs={{0,3},{1,2},{2,1},{3,0},{4,7},{5,6},{6,5},{7,4},{8,11},{9,10},{10,... | collective-permute-start | bytes 110600 | tf_op jit(solution)/shard_map/ppermute | solution.py:372
  133.2 6.3 %collective-permute-start.30 = (bf16[2,48,384]{2,1,0:T(8,128)(2,1)S(1)}, bf16[2,48,384]{2,1,0:T(8,128)(2,1)S(1)}, u32[]{:S(2)}, u32[]{:S(2)}) collective-permute-start(bf16[2,48,384]{2,1,0:T(8,128)(2,1)S(1)} %get-tuple-element.174), channel_id=1, source_target_pairs={{0,3},{1,2},{2,1},{3,0},{4,7},{5,6},{6,5},{7,4},{8,11},{9,10},{10,... | collective-permute-start | bytes 221192 | tf_op jit(solution)/shard_map/ppermute | solution.py:372
  142.3 18.4 %all-to-all-start.2 = ((bf16[8,3,48,384]{3,2,1,0:T(8,128)(2,1)}), bf16[8,3,48,384]{3,2,1,0:T(8,128)(2,1)}, u32[]{:S(2)}, u32[]{:S(2)}) async-start(bf16[8,3,48,384]{3,2,1,0:T(8,128)(2,1)} %broadcast_in_dim.81), calls=%async_computation.2 | async-start | bytes 1769472 | tf_op jit(solution)/shard_map/all_to_all | solution.py:376
  150.4 8.5 %collective-permute-start.38 = (bf16[256,96]{0,1:T(8,128)(2,1)S(1)}, bf16[256,96]{0,1:T(8,128)(2,1)S(1)}, u32[]{:S(2)}, u32[]{:S(2)}) collective-permute-start(bf16[256,96]{0,1:T(8,128)(2,1)S(1)} %fusion.4), channel_id=1, source_target_pairs={{0,1},{1,0},{2,3},{3,2},{4,5},{5,4},{6,7},{7,6},{8,9},{9,8},{10,11... | collective-permute-start | bytes 147464 | tf_op jit(solution)/shard_map/ppermute | solution.py:372
  151.2 8.0 %collective-permute-start.39 = (bf16[256,96]{0,1:T(8,128)(2,1)S(1)}, bf16[256,96]{0,1:T(8,128)(2,1)S(1)}, u32[]{:S(2)}, u32[]{:S(2)}) collective-permute-start(bf16[256,96]{0,1:T(8,128)(2,1)S(1)} %fusion.4), channel_id=1, source_target_pairs={{0,2},{1,3},{2,0},{3,1},{4,6},{5,7},{6,4},{7,5},{8,10},{9,11},{10,... | collective-permute-start | bytes 147464 | tf_op jit(solution)/shard_map/ppermute | solution.py:372
  153.2 6.3 %collective-permute-start.40 = (bf16[256,96]{0,1:T(8,128)(2,1)S(1)}, bf16[256,96]{0,1:T(8,128)(2,1)S(1)}, u32[]{:S(2)}, u32[]{:S(2)}) collective-permute-start(bf16[256,96]{0,1:T(8,128)(2,1)S(1)} %fusion.4), channel_id=1, source_target_pairs={{0,3},{1,2},{2,1},{3,0},{4,7},{5,6},{6,5},{7,4},{8,11},{9,10},{10,... | collective-permute-start | bytes 147464 | tf_op jit(solution)/shard_map/ppermute | solution.py:372
  (44 other events, 237.7 us)
